TPU v7x, 128 devices: a whole 4x4x4 slice. The times are simulated.
128 devices in a mesh: lat: 4 (over y_hi, core), grp: 32 (over z, x, y_lo).
Axes of the slice: x: 4, y: 4 (y_hi: 2, y_lo: 2; y = y_hi * 2 + y_lo), z: 4, core: 2. Of those that a mesh axis runs over, the one named last changes fastest.
Arguments:
- inputs: bfloat16 [256, 1024, 1024], P(None, ('lat', 'grp')), may hold values from -6 to 6
- w_in: bfloat16 [256, 512], replicated, may hold values from -0.375 to 0.375
- bias_in: float32 [512], replicated, may hold values from -3 to 3
- w_out: bfloat16 [512, 256], replicated, may hold values from -0.25 to 0.25
- advected: bfloat16 [256, 1024, 1024], P('grp', 'lat'), may hold values from -6 to 6
- cotangent: bfloat16 [256, 1024, 1024], P('grp', 'lat'), may hold values from -6 to 6
- offsets: int32 [2, 64, 4], P(None, 'lat'), may hold values from 0 to 3
- stencil_row: int32 [64, 4], P('lat'), may hold values from 0 to 4
- stencil_col: int32 [64, 4], P('lat'), may hold values from 0 to 124
- fracs: float32 [2, 64, 4], P(None, 'lat'), may hold values from 0 to 1
Outputs:
- grad_inputs: bfloat16 [256, 1024, 1024], P(None, ('lat', 'grp'))
- grad_w_in: float32 [256, 512], P(None, ('lat', 'grp'))
- grad_bias: float32 [512], P(('lat', 'grp'))
- grad_w_out: float32 [512, 256], P(('lat', 'grp'))
- grad_frac: float32 [2, 64, 4], P(None, 'lat')
All inputs are finite; a program needn't handle non-finite values.
Results may differ from a plain program's by a relative error of at most 0.0068.
Values may be sent and summed in bfloat16 or wider, within the bound.
No kernel may reach another device: no remote copies, remote signals or barrier semaphores. Data moves between devices by JAX's collectives and lax.ppermute only.
A program may use at most 128 MiB of HBM per device.

v0:
```python
import math

import jax
import jax.numpy as jnp
from jax import lax
from jax.sharding import PartitionSpec as P

C = 256
BH = 16
BW = 256


def extended_2(cells, sides, width):
    for axis, dim in sides:
        count = lax.axis_size(axis)
        ends = count - 1
        head = lax.slice_in_dim(cells, 0, width, axis=dim)
        tail = lax.slice_in_dim(cells, cells.shape[dim] - width, cells.shape[dim], axis=dim)
        cells = jnp.concatenate(
            [
                lax.ppermute(tail, axis, [(i, (i + 1) % count) for i in range(ends)]),
                cells,
                lax.ppermute(head, axis, [((i + 1) % count, i) for i in range(ends)]),
            ],
            axis=dim,
        )
    return cells


def from_behind(block, axis, distance):
    devices = range(lax.axis_size(axis))
    route = [(i - distance, i) for i in devices if i - distance in devices]
    return lax.ppermute(block, axis, route)


def catmull(frac):
    square = frac * frac
    cube = square * frac
    weights = (
        0.5 * (-cube + 2.0 * square - frac),
        0.5 * (3.0 * cube - 5.0 * square + 2.0),
        0.5 * (-3.0 * cube + 4.0 * square + frac),
        0.5 * (cube - square),
    )
    slopes = (
        0.5 * (-3.0 * square + 4.0 * frac - 1.0),
        0.5 * (9.0 * square - 10.0 * frac),
        0.5 * (-9.0 * square + 8.0 * frac + 1.0),
        0.5 * (3.0 * square - 2.0 * frac),
    )
    return (weights, slopes)


def band_matrix(position, frac, inner):
    offset_grid = (
        jnp.arange(3 * inner, dtype=jnp.int32)[None, None, :]
        - jnp.arange(inner, dtype=jnp.int32)[None, :, None]
        - position[:, None, None]
    )
    weights, slopes = catmull(frac)
    value = jnp.zeros(offset_grid.shape, jnp.float32)
    slope = jnp.zeros(offset_grid.shape, jnp.float32)
    for tap in range(4):
        value = value + jnp.where(offset_grid == tap, weights[tap][:, None, None], 0.0)
        slope = slope + jnp.where(offset_grid == tap, slopes[tap][:, None, None], 0.0)
    return (value.astype(jnp.bfloat16), slope.astype(jnp.bfloat16))


def contract_points(left, right):
    return lax.dot_general(
        left, right, (((1,), (1,)), ((), ())), preferred_element_type=jnp.float32
    )


def shards(
    inputs, w_in, bias_in, w_out, advected, cotangent, offsets, stencil_row, stencil_col, fracs
):
    channels_dev, band_rows, columns = advected.shape
    row_blocks = band_rows // BH
    blocks = columns // BW
    point_rows = inputs.shape[1]
    x_flat = inputs.reshape(C, point_rows * columns)
    pre_act = (
        lax.dot_general(w_in, x_flat, (((0,), (0,)), ((), ())), preferred_element_type=jnp.float32)
        + bias_in[:, None]
    )
    sigma = jax.nn.sigmoid(pre_act)
    act = (pre_act * sigma).astype(jnp.bfloat16)
    padded = extended_2(advected, (("lat", 1),), BH)
    row_pos = BH // 2 * offsets[0] + stencil_row
    col_pos = BW // 2 * offsets[1] + stencil_col

    def per_row(index, state):
        extended, frac_acc = state
        drow = lax.dynamic_slice_in_dim(cotangent, index * BH, BH, 1)
        window = lax.dynamic_slice_in_dim(padded, index * BH, 3 * BH, 1)
        ry_value, ry_slope = band_matrix(row_pos[index], fracs[0][index], BH)
        rx_value, rx_slope = band_matrix(col_pos[index], fracs[1][index], BW)
        column_sums = [
            jnp.zeros((channels_dev, 3 * BH, BW), jnp.float32) for unused in range(blocks)
        ]
        grad_rows = []
        grad_cols = []
        for block in range(blocks):
            left = (block - 1) % blocks
            right = (block + 1) % blocks
            rx_both = jnp.concatenate([rx_value[block], rx_slope[block]], axis=1)
            block_cot = drow[:, :, block * BW : (block + 1) * BW].reshape(channels_dev * BH, BW)
            product = jnp.dot(block_cot, rx_both, preferred_element_type=jnp.float32)
            product = product.reshape(channels_dev, BH, 6 * BW)
            z_value = product[:, :, : 3 * BW]
            z_slope = product[:, :, 3 * BW :]
            ry_value_all = jnp.broadcast_to(ry_value[block], (channels_dev, BH, 3 * BH))
            ry_slope_all = jnp.broadcast_to(ry_slope[block], (channels_dev, BH, 3 * BH))
            spread = jnp.einsum(
                "cho,chv->cov",
                ry_value_all,
                z_value.astype(jnp.bfloat16),
                preferred_element_type=jnp.float32,
            )
            source = jnp.concatenate(
                [
                    window[:, :, left * BW : (left + 1) * BW],
                    window[:, :, block * BW : (block + 1) * BW],
                    window[:, :, right * BW : (right + 1) * BW],
                ],
                axis=2,
            )
            ry_both = jnp.concatenate([ry_value_all, ry_slope_all], axis=1)
            lifted = jnp.einsum("cjo,cov->cjv", ry_both, source, preferred_element_type=jnp.float32)
            grad_rows.append(jnp.sum(lifted[:, BH:] * z_value))
            grad_cols.append(jnp.sum(lifted[:, :BH] * z_slope))
            for part, target in ((0, left), (1, block), (2, right)):
                column_sums[target] = (
                    column_sums[target] + spread[:, :, part * BW : (part + 1) * BW]
                )
        row_sum = jnp.concatenate(column_sums, axis=2)
        current = lax.dynamic_slice_in_dim(extended, index * BH, 3 * BH, 1)
        extended = lax.dynamic_update_slice_in_dim(extended, current + row_sum, index * BH, 1)
        frac_acc = frac_acc.at[:, index].set(
            jnp.stack([jnp.stack(grad_rows), jnp.stack(grad_cols)])
        )
        return (extended, frac_acc)

    start_field = jnp.zeros((channels_dev, band_rows + 2 * BH, columns), jnp.float32)
    start_frac = jnp.zeros((2, row_blocks, blocks), jnp.float32)
    extended, frac_local = lax.fori_loop(0, row_blocks, per_row, (start_field, start_frac))
    from_below = from_behind(extended[:, :BH], "lat", -1)
    from_above = from_behind(extended[:, band_rows + BH :], "lat", 1)
    inner_rows = jnp.concatenate(
        [
            extended[:, BH : 2 * BH] + from_above,
            extended[:, 2 * BH : band_rows],
            extended[:, band_rows : band_rows + BH] + from_below,
        ],
        axis=1,
    )
    dy_band = inner_rows.astype(jnp.bfloat16)
    dy_points = lax.all_to_all(dy_band, "grp", split_axis=1, concat_axis=0, tiled=True)
    dy_flat = dy_points.reshape(C, point_rows * columns)
    dact = jnp.dot(w_out, dy_flat, preferred_element_type=jnp.float32)
    frac_total = lax.psum(frac_local, "grp")
    grad_frac = frac_total / math.sqrt(C * BH * BW)
    dpre = (dact * sigma * (1.0 + pre_act * (1.0 - sigma))).astype(jnp.bfloat16)
    dx_flat = dy_flat.astype(jnp.float32) + jnp.dot(w_in, dpre, preferred_element_type=jnp.float32)
    grad_inputs = dx_flat.astype(jnp.bfloat16).reshape(C, point_rows, columns)
    grad_first = contract_points(x_flat, dpre)
    grad_shift = jnp.sum(dpre.astype(jnp.float32), axis=1)
    grad_second = contract_points(act, dy_flat)
    total_points = point_rows * columns * lax.axis_size("lat") * lax.axis_size("grp")
    scale = 1.0 / math.sqrt(total_points)
    summed = (
        lax.psum_scatter(grad_first, ("lat", "grp"), scatter_dimension=1, tiled=True),
        lax.psum_scatter(grad_shift, ("lat", "grp"), scatter_dimension=0, tiled=True),
        lax.psum_scatter(grad_second, ("lat", "grp"), scatter_dimension=0, tiled=True),
    )
    return (grad_inputs, summed[0] * scale, summed[1] * scale, summed[2] * scale, grad_frac)


def solution(mesh):
    placed = (
        P(None, ("lat", "grp"), None),
        P(),
        P(),
        P(),
        P("grp", "lat", None),
        P("grp", "lat", None),
        P(None, "lat", None),
        P("lat", None),
        P("lat", None),
        P(None, "lat", None),
    )
    return jax.shard_map(
        shards,
        mesh=mesh,
        in_specs=placed,
        out_specs=(
            P(None, ("lat", "grp"), None),
            P(None, ("lat", "grp")),
            P(("lat", "grp")),
            P(("lat", "grp"), None),
            P(None, "lat", None),
        ),
        check_vma=False,
    )
```

profile of v0, /device:TPU:1, one launch (start us, length us, event | category | flops | bytes accessed | tf_op | source)
XLA Modules:
  0.0 892.8 jit_solution(14742110184681917502)
XLA Ops:
  8.3 6.2 collective-permute-start
  18.1 5.6 collective-permute-done.1
  23.7 4.1 pad_maximum_fusion
  27.8 4.8 broadcast_in_dim.522.clone
  32.6 511.4 %while.19 = (s32[]{:T(128)}, f32[8,288,1024]{2,0,1:T(8,128)}, f32[2,16,4]{2,0,1:T(2,128)S(1)}, s32[16,4]{1,0:T(8,128)S(1)}, f32[2,16,4]{2,1,0:T(8,128)S(1)}, /*i...) while((s32[]{:T(128)}, f32[8,288,1024]{2,0,1:T(8,128)}, ...), condition=%wide.region_10.11_spmd, body=%wide.region_0.10_spmd.sunk | while | flops 545456192 | bytes 57158856 | solution.py:147
  83.7 2.6 maximum_bitcast_fusion.22
  179.6 2.6 maximum_bitcast_fusion.22
  549.7 3.7 slice.820
  553.4 5.9 collective-permute-done.3
  562.9 8.1 all-to-all-start
  571.2 8.5 copy.49
  579.8 10.3 %fusion.118 = f32[512,8192]{0,1:T(8,128)} fusion(bf16[256,512]{1,0:T(8,128)(2,1)S(1)} %copy-done, bf16[256,8192]{1,0:T(8,128)(2,1)} %bitcast.155), kind=kOutput, calls=%fused_computation.217 | convolution fusion | flops 2147483648 | bytes 21233664 | tf_op jit(solution)/shard_map/dot_general | solution.py:84
  590.1 86.8 %psum.7 = f32[2,16,4]{1,2,0:T(4,128)S(1)} all-reduce(f32[2,16,4]{1,2,0:T(4,128)S(1)} %copy.41), channel_id=1, replica_groups=mesh['lat'=4,'grp'=32] {'grp'}, use_global_device_ids=true, to_apply=%region_15.16 | all-reduce | flops 128 | bytes 1024 | tf_op jit(solution)/shard_map/psum | solution.py:162
  677.6 6.5 copy.53
  684.1 6.3 copy.48
  690.4 6.6 copy.39
  697.0 10.2 %fusion.111 = f32[512,256]{1,0:T(8,128)} fusion(bf16[256,8192]{1,0:T(8,128)(2,1)} %bitcast.152, f32[512,8192]{0,1:T(8,128)} %fusion.118, f32[512]{0:T(512)S(1)} %copy-done.8), kind=kOutput, calls=%fused_computation.199 | convolution fusion | flops 2172649472 | bytes 21497856 | tf_op jit(solution)/shard_map/dot_general | solution.py:70
  707.2 11.6 %convert_reduce_fusion = (f32[512]{0:T(512)S(1)}, bf16[512,8192]{0,1:T(8,128)(2,1)S(1)}) fusion(f32[512,8192]{0,1:T(8,128)} %fusion.118, f32[512]{0:T(512)S(1)} %copy-done.8, bf16[256,8192]{1,0:T(8,128)(2,1)S(1)} %bitcast.153, bf16[512,256]{1,0:T(8,128)(2,1)S(1)} %copy-done.7), kind=kOutput, calls=%fused_computation.194 | convolution fusion | flops 2197814784 | bytes 29626368 | tf_op jit(solution)/shard_map/dot_general | solution.py:161
  718.8 3.2 copy-done.5
  722.1 3.2 convolution_bitcast_fusion.1
  725.3 8.9 fusion.110
  734.2 6.7 copy.42
  740.9 75.2 %all-reduce.1 = f32[512]{0:T(512)S(1)} all-reduce(f32[512]{0:T(512)S(1)} %get-tuple-element.375), channel_id=3, replica_groups=mesh['lat'=4,'grp'=32] {'lat','grp'}, use_global_device_ids=true, to_apply=%region_13.14.clone | all-reduce | flops 512 | bytes 4096
  816.7 66.3 %all-reduce.6.cloned.1.call-done = (f32[256,512]{0,1:T(8,128)}, f32[512,256]{1,0:T(8,128)}) async-done(((f32[256,512]{0,1:T(8,128)}, f32[512,256]{1,0:T(8,128)}), (f32[256,512]{0,1:T(8,128)}, f32[512,256]{1,0:T(8,128)})) %all-reduce.6.cloned.1.call-update) | async-done | bytes 1048592
  (849 shorter events, 520.1 us)
Async XLA Ops:
  7.2 572.6 %copy-start = (bf16[256,512]{1,0:T(8,128)(2,1)S(1)}, bf16[256,512]{1,0:T(8,128)(2,1)}, u32[]{:S(2)}) copy-start(bf16[256,512]{1,0:T(8,128)(2,1)} %param.15) | copy-start | bytes 786436
  8.3 9.8 %collective-permute-start = (bf16[8,16,1024]{2,1,0:T(8,128)(2,1)S(1)}, bf16[8,16,1024]{2,1,0:T(8,128)(2,1)S(1)}, u32[]{:S(2)}, u32[]{:S(2)}) collective-permute-start(bf16[8,16,1024]{2,1,0:T(8,128)(2,1)S(1)} %get-tuple-element.371), channel_id=1, source_target_pairs={{0,32},{32,64},{64,96},{1,33},{33,65},{65,97},{2,34},{34,66},{66,9... | collective-permute-start | bytes 786440 | tf_op jit(solution)/shard_map/ppermute | solution.py:21
  14.5 9.2 %collective-permute-start.1 = (bf16[8,16,1024]{2,1,0:T(8,128)(2,1)S(1)}, bf16[8,16,1024]{2,1,0:T(8,128)(2,1)S(1)}, u32[]{:S(2)}, u32[]{:S(2)}) collective-permute-start(bf16[8,16,1024]{2,1,0:T(8,128)(2,1)S(1)} %get-tuple-element.372), channel_id=1, source_target_pairs={{32,0},{64,32},{96,64},{33,1},{65,33},{97,65},{34,2},{66,34},{98,6... | collective-permute-start | bytes 786440 | tf_op jit(solution)/shard_map/ppermute | solution.py:23
  45.5 5.2 copy-start.1
  45.6 5.2 copy-start.2
  77.5 5.2 copy-start.1
  77.5 5.2 copy-start.2
  173.4 5.2 copy-start.1
  173.4 5.2 copy-start.2
  237.2 5.2 copy-start.1
  237.2 5.2 copy-start.2
  269.2 5.2 copy-start.1
  269.2 5.2 copy-start.2
  365.0 5.2 copy-start.1
  365.0 5.2 copy-start.2
  524.9 5.2 copy-start.1
  545.3 8.0 collective-permute-start.2
  547.2 12.0 %collective-permute-start.3 = (f32[8,16,1024]{2,0,1:T(8,128)S(1)}, f32[8,16,1024]{2,0,1:T(8,128)S(1)}, u32[]{:S(2)}, u32[]{:S(2)}) collective-permute-start(f32[8,16,1024]{2,0,1:T(8,128)S(1)} %get-tuple-element.370), channel_id=1, source_target_pairs={{32,0},{64,32},{96,64},{33,1},{65,33},{97,65},{34,2},{66,34},{98,6... | collective-permute-start | bytes 1572872 | tf_op jit(solution)/shard_map/ppermute | solution.py:33
  562.9 114.7 %all-to-all-start = ((bf16[8,256,1024]{2,0,1:T(8,128)(2,1)}), bf16[8,256,1024]{2,0,1:T(8,128)(2,1)}, u32[]{:S(2)}, u32[]{:S(2)}) async-start(bf16[8,256,1024]{2,0,1:T(8,128)(2,1)} %pad_maximum_fusion.1), calls=%async_computation | async-start | bytes 8388608 | tf_op jit(solution)/shard_map/all_to_all | solution.py:159
  571.0 311.9 %all-reduce.6.cloned.1.call-start = ((), (), s32[]{:S(2)}) async-start(), calls=%async_computation.1 | async-start | bytes 2097152
  690.4 6.6 copy-start.8
  697.0 10.2 %copy-start.3 = (bf16[32,8,8,1024]{3,1,2,0:T(8,128)(2,1)S(1)}, bf16[32,8,8,1024]{3,1,2,0:T(8,128)(2,1)}, u32[]{:S(2)}) copy-start(bf16[32,8,8,1024]{3,1,2,0:T(8,128)(2,1)} %copy.48) | copy-start | bytes 12582916
  697.0 10.2 %copy-start.7 = (bf16[512,256]{1,0:T(8,128)(2,1)S(1)}, bf16[512,256]{1,0:T(8,128)(2,1)}, u32[]{:S(2)}) copy-start(bf16[512,256]{1,0:T(8,128)(2,1)} %param.17) | copy-start | bytes 786436
  707.2 14.9 %copy-start.4 = (bf16[32,8,8,1024]{3,1,2,0:T(8,128)(2,1)S(1)}, bf16[32,8,8,1024]{3,1,2,0:T(8,128)(2,1)}, u32[]{:S(2)}) copy-start(bf16[32,8,8,1024]{3,1,2,0:T(8,128)(2,1)} %copy.49) | copy-start | bytes 12582916
  (21 other events, 106.1 us)
Sparse Core Ops, SparseCore 0:
  725.4 157.4 all-reduce.5
where the time goes:
time: 907 us; the launch traced here: 893 us
  other arithmetic  225 us (25%)
  local copies, waits for them, and re-layouts  195 us (21%)
  matrix products  193 us (21%)
  blocking collectives  162 us (18%)
  waiting for transfers between devices  77.8 us (9%)
  starting transfers between devices  20.8 us (2%)
  between operations  14.6 us (2%)
    psum x1, blocking collectives, shards(): frac_total = lax.psum(frac_local, 'grp')  86.8 us
    another operation x32, other arithmetic, per_row(): jnp.stack([jnp.stack(grad_rows), jnp.stack(grad_cols)])  82.1 us
    dot_general x64, matrix products, per_row(): product = jnp.dot(block_cot, rx_both, preferred_element_type=jnp.float32)  76.3 us
    unnamed x1, blocking collectives  75.2 us
    unnamed x2, waiting for transfers between devices  66.3 us
    dot_general x64, matrix products, per_row(): jnp.einsum('cjo,cov->cjv', ry_both, source, preferred_element_type=jnp.fl...  49.8 us
    reduce_sum x64, other arithmetic, per_row(): grad_rows.append(jnp.sum(lifted[:, BH:] * z_value))  49 us
    convert_element_type x32, other arithmetic, band_matrix(): return (value.astype(jnp.bfloat16), slope.astype(jnp.bfloat16))  37.5 us
  transfers between devices with their start and end apart: 6, of which 3 were waited for; matrix products, arithmetic and copies ran while one was open for 5% of the time, Pallas kernels for 0%

commit v1 on v0

v1 whole, which is shorter than its diff:
```python
import math

import jax
import jax.numpy as jnp
from jax import lax
from jax.experimental import pallas as pl
from jax.experimental.pallas import tpu as pltpu
from jax.sharding import PartitionSpec as P

C = 256
BH = 16
BW = 256
LANES = 128
HID = 512
F32 = jnp.float32
BF16 = jnp.bfloat16


def catmull(frac):
    square = frac * frac
    cube = square * frac
    weights = (
        0.5 * (-cube + 2.0 * square - frac),
        0.5 * (3.0 * cube - 5.0 * square + 2.0),
        0.5 * (-3.0 * cube + 4.0 * square + frac),
        0.5 * (cube - square),
    )
    slopes = (
        0.5 * (-3.0 * square + 4.0 * frac - 1.0),
        0.5 * (9.0 * square - 10.0 * frac),
        0.5 * (-9.0 * square + 8.0 * frac + 1.0),
        0.5 * (3.0 * square - 2.0 * frac),
    )
    return (jnp.stack(weights, axis=-1), jnp.stack(slopes, axis=-1))


def rounded(values):
    return lax.reduce_precision(values, 8, 7)


def halo(band, dim, width):
    count = lax.axis_size("lat")
    size = band.shape[dim]
    head = lax.slice_in_dim(band, 0, width, axis=dim)
    tail = lax.slice_in_dim(band, size - width, size, axis=dim)
    above = lax.ppermute(tail, "lat", [(i, i + 1) for i in range(count - 1)])
    below = lax.ppermute(head, "lat", [(i + 1, i) for i in range(count - 1)])
    return above, below


def diagonal():
    row = lax.broadcasted_iota(jnp.int32, (LANES, 2 * LANES), 0)
    col = lax.broadcasted_iota(jnp.int32, (LANES, 2 * LANES), 1)
    return col - row


def channel_minor():
    out = lax.broadcasted_iota(jnp.int32, (LANES, LANES), 0)
    src = lax.broadcasted_iota(jnp.int32, (LANES, LANES), 1)
    return ((out % 8) * 16 + out // 8 == src).astype(F32).astype(BF16)


def taps(masks, weights):
    value = jnp.zeros((LANES, 2 * LANES), F32)
    for tap in range(4):
        value = jnp.where(masks[tap], weights[tap], value)
    return value.astype(BF16)


def spread_body(pos_ref, wgt_ref, top_ref, mid_ref, bot_ref, out_ref, row_scr, cot_scr, z_scr, acc):
    step = pl.program_id(0)
    last = pl.num_programs(0) - 1

    @pl.when(step == 0)
    def _():
        acc[0 : 2 * BH] = jnp.zeros((2 * BH,) + acc.shape[1:], F32)
        row_scr[...] = top_ref[...]

    @pl.when(step == last)
    def _():
        row_scr[...] = bot_ref[...]

    @pl.when(jnp.logical_and(step > 0, step < last))
    def _():
        row_scr[...] = mid_ref[...]

    acc[pl.ds((step + 2) * BH, BH)] = jnp.zeros((BH,) + acc.shape[1:], F32)
    rows = row_scr[...].reshape(LANES, row_scr.shape[2])
    cot_scr[...] = jnp.dot(channel_minor(), rows, preferred_element_type=F32).astype(BF16)
    diag = diagonal()
    for block in range(4):
        base = step * 4 + block
        py = pos_ref[base * 3]
        tile = pos_ref[base * 3 + 1]
        shift = diag - pos_ref[base * 3 + 2]
        masks = [shift == tap for tap in range(4)]
        cols = taps(masks, [wgt_ref[base * 16 + tap] for tap in range(4)])
        wy = [wgt_ref[base * 16 + 4 + tap] for tap in range(4)]
        halves = jnp.concatenate(
            [
                cot_scr[:, block * BW : block * BW + LANES],
                cot_scr[:, block * BW + LANES : (block + 1) * BW],
            ],
            axis=0,
        )
        z_scr[block] = jnp.dot(halves, cols, preferred_element_type=F32)
        for part in range(3):
            if part == 0:
                z = z_scr[block, 0:LANES, 0:LANES]
            elif part == 1:
                z = z_scr[block, 0:LANES, LANES:] + z_scr[block, LANES:, 0:LANES]
            else:
                z = z_scr[block, LANES:, LANES:]
            z = z.astype(BF16).astype(F32).reshape(BH, 8, LANES)
            target = (2 * block + 6 + part + tile) & 7
            for j in range(BH + 3):
                value = None
                for tap in range(4):
                    if 0 <= j - tap < BH:
                        term = wy[tap] * z[j - tap]
                        value = term if value is None else value + term
                at = step * BH + py + j
                acc[at, target] = acc[at, target] + value

    for tile_index in range(8):
        done = acc[pl.ds(step * BH, BH), tile_index].reshape(BH * 8, LANES)
        out_ref[0, :, tile_index * LANES : (tile_index + 1) * LANES] = done.astype(BF16)


def spread(pos, wgt, top, cot, bottom):
    channels, band_rows, columns = cot.shape
    blocks = band_rows // BH
    spec = lambda shape, index: pl.BlockSpec(shape, index)
    return pl.pallas_call(
        spread_body,
        name="spread",
        out_shape=jax.ShapeDtypeStruct((blocks, BH * channels, columns), BF16),
        grid_spec=pltpu.PrefetchScalarGridSpec(
            num_scalar_prefetch=2,
            grid=(blocks + 2,),
            in_specs=[
                spec((channels, BH, columns), lambda g, a, b: (0, 0, 0)),
                spec(
                    (channels, BH, columns),
                    lambda g, a, b: (0, jnp.clip(g - 1, 0, blocks - 1), 0),
                ),
                spec((channels, BH, columns), lambda g, a, b: (0, 0, 0)),
            ],
            out_specs=spec(
                (1, BH * channels, columns), lambda g, a, b: (jnp.maximum(g - 2, 0), 0, 0)
            ),
            scratch_shapes=[
                pltpu.VMEM((channels, BH, columns), BF16),
                pltpu.VMEM((BH * channels, columns), BF16),
                pltpu.VMEM((4, 2 * LANES, 2 * LANES), F32),
                pltpu.VMEM(((blocks + 4) * BH, columns // LANES, channels, LANES), F32),
            ],
        ),
        compiler_params=pltpu.CompilerParams(dimension_semantics=("arbitrary",)),
    )(pos, wgt, top, cot, bottom)


def frac_body(
    pos_ref, wgt_ref, top_ref, mid_ref, next_ref, bot_ref, cot_ref, out_ref, cot_scr, z_scr, field
):
    step = pl.program_id(0)
    last = pl.num_programs(0) - 1
    width = cot_scr.shape[1]
    order = channel_minor()

    def put(row_block, source):
        rows = source[...].reshape(LANES, width)
        moved = jnp.dot(order, rows, preferred_element_type=F32)
        for tile_index in range(8):
            field[pl.ds(row_block * BH, BH), tile_index] = moved[
                :, tile_index * LANES : (tile_index + 1) * LANES
            ].reshape(BH, 8, LANES)

    @pl.when(step == 0)
    def _():
        put(0, top_ref)
        put(1, mid_ref)

    @pl.when(step == last)
    def _():
        put(step + 2, bot_ref)

    @pl.when(step < last)
    def _():
        put(step + 2, next_ref)

    rows = cot_ref[...].reshape(LANES, width)
    cot_scr[...] = jnp.dot(order, rows, preferred_element_type=F32).astype(BF16)
    diag = diagonal()
    for block in range(4):
        base = (step + 1) * 4 + block
        py = pos_ref[base * 3]
        tile = pos_ref[base * 3 + 1]
        shift = diag - pos_ref[base * 3 + 2]
        masks = [shift == tap for tap in range(4)]
        both = jnp.concatenate(
            [
                taps(masks, [wgt_ref[base * 16 + tap] for tap in range(4)]),
                taps(masks, [wgt_ref[base * 16 + 8 + tap] for tap in range(4)]),
            ],
            axis=1,
        )
        halves = jnp.concatenate(
            [
                cot_scr[:, block * BW : block * BW + LANES],
                cot_scr[:, block * BW + LANES : (block + 1) * BW],
            ],
            axis=0,
        )
        z_scr[block] = jnp.dot(halves, both, preferred_element_type=F32)
        by_value = [jnp.zeros((8, LANES), F32) for tap in range(4)]
        by_slope = [jnp.zeros((8, LANES), F32) for tap in range(4)]
        for part in range(3):
            pair = []
            for lane in (0, 2 * LANES):
                if part == 0:
                    z = z_scr[block, 0:LANES, lane : lane + LANES]
                elif part == 1:
                    z = (
                        z_scr[block, 0:LANES, lane + LANES : lane + 2 * LANES]
                        + z_scr[block, LANES:, lane : lane + LANES]
                    )
                else:
                    z = z_scr[block, LANES:, lane + LANES : lane + 2 * LANES]
                pair.append(z.reshape(BH, 8, LANES))
            source = (2 * block + 6 + part + tile) & 7
            for j in range(BH + 3):
                value = field[step * BH + py + j, source]
                for tap in range(4):
                    if 0 <= j - tap < BH:
                        by_value[tap] = by_value[tap] + value * pair[0][j - tap]
                        by_slope[tap] = by_slope[tap] + value * pair[1][j - tap]
        first = jnp.zeros((8, LANES), F32)
        second = jnp.zeros((8, LANES), F32)
        for tap in range(4):
            first = first + wgt_ref[base * 16 + 12 + tap] * by_value[tap]
            second = second + wgt_ref[base * 16 + 4 + tap] * by_slope[tap]
        out_ref[0, block] = first
        out_ref[1, block] = second


def frac_sums(pos, wgt, top, field, bottom, cot):
    channels, band_rows, columns = cot.shape
    blocks = band_rows // BH
    shape = (channels, BH, columns)
    return pl.pallas_call(
        frac_body,
        name="frac_sums",
        out_shape=jax.ShapeDtypeStruct((2, blocks * 4, 8, LANES), F32),
        grid_spec=pltpu.PrefetchScalarGridSpec(
            num_scalar_prefetch=2,
            grid=(blocks,),
            in_specs=[
                pl.BlockSpec(shape, lambda g, a, b: (0, 0, 0)),
                pl.BlockSpec(shape, lambda g, a, b: (0, 0, 0)),
                pl.BlockSpec(shape, lambda g, a, b: (0, jnp.minimum(g + 1, blocks - 1), 0)),
                pl.BlockSpec(shape, lambda g, a, b: (0, 0, 0)),
                pl.BlockSpec(shape, lambda g, a, b: (0, g, 0)),
            ],
            out_specs=pl.BlockSpec((2, 4, 8, LANES), lambda g, a, b: (0, g, 0, 0)),
            scratch_shapes=[
                pltpu.VMEM((BH * channels, columns), BF16),
                pltpu.VMEM((4, 2 * LANES, 4 * LANES), F32),
                pltpu.VMEM(((blocks + 2) * BH, columns // LANES, channels, LANES), F32),
            ],
        ),
        compiler_params=pltpu.CompilerParams(dimension_semantics=("arbitrary",)),
    )(pos, wgt, top, field, field, bottom, cot)


def mlp_body(x_ref, dy_ref, w_in_t, w_in, w_out, bias, dx_ref, g_in, g_out, g_bias, dy_scr):
    @pl.when(jnp.logical_and(pl.program_id(0) == 0, pl.program_id(1) == 0))
    def _():
        g_in[...] = jnp.zeros_like(g_in)
        g_out[...] = jnp.zeros_like(g_out)
        g_bias[...] = jnp.zeros_like(g_bias)

    width = x_ref.shape[2]
    dy_scr[...] = dy_ref[...].reshape(C, width)
    x = x_ref[0]
    dy = dy_scr[...]
    pre = jnp.dot(w_in_t[...], x, preferred_element_type=F32) + bias[...]
    sigma = 0.5 + 0.5 * jnp.tanh(0.5 * pre)
    act = (pre * sigma).astype(BF16)
    dact = jnp.dot(w_out[...], dy, preferred_element_type=F32)
    dpre = (dact * sigma * (1.0 + pre * (1.0 - sigma))).astype(BF16)
    dx = dy.astype(F32) + jnp.dot(w_in[...], dpre, preferred_element_type=F32)
    dx_ref[0] = dx.astype(BF16)
    points = (((1,), (1,)), ((), ()))
    g_in[...] += lax.dot_general(dpre, x, points, preferred_element_type=F32)
    g_out[...] += lax.dot_general(act, dy, points, preferred_element_type=F32)
    total = g_bias[...]
    for lane in range(0, width, LANES):
        total = total + dpre[:, lane : lane + LANES].astype(F32)
    g_bias[...] = total


def mlp(x, dy, w_in, bias, w_out):
    rows, channels, columns = x.shape
    sources = dy.shape[0]
    width = 512
    whole = lambda shape: pl.BlockSpec(shape, lambda r, c: (0, 0))
    return pl.pallas_call(
        mlp_body,
        name="mlp",
        out_shape=(
            jax.ShapeDtypeStruct((rows, channels, columns), BF16),
            jax.ShapeDtypeStruct((HID, channels), F32),
            jax.ShapeDtypeStruct((HID, channels), F32),
            jax.ShapeDtypeStruct((HID, LANES), F32),
        ),
        grid=(rows, columns // width),
        in_specs=[
            pl.BlockSpec((1, channels, width), lambda r, c: (r, 0, c)),
            pl.BlockSpec((sources, None, 8, width), lambda r, c: (0, r, 0, c)),
            whole((HID, channels)),
            whole((channels, HID)),
            whole((HID, channels)),
            whole((HID, 1)),
        ],
        out_specs=[
            pl.BlockSpec((1, channels, width), lambda r, c: (r, 0, c)),
            whole((HID, channels)),
            whole((HID, channels)),
            whole((HID, LANES)),
        ],
        scratch_shapes=[pltpu.VMEM((channels, width), BF16)],
        compiler_params=pltpu.CompilerParams(dimension_semantics=("arbitrary", "arbitrary")),
    )(x, dy, w_in.T, w_in, w_out, bias[:, None])


def shards(
    inputs, w_in, bias_in, w_out, advected, cotangent, offsets, stencil_row, stencil_col, fracs
):
    channels_dev, band_rows, columns = advected.shape
    row_blocks = band_rows // BH
    point_rows = inputs.shape[1]
    lat = lax.axis_size("lat")
    grp = lax.axis_size("grp")

    cot_top, cot_bottom = halo(cotangent, 1, BH)
    meta = jnp.concatenate(
        [
            offsets.astype(F32),
            stencil_row.astype(F32)[None],
            stencil_col.astype(F32)[None],
            fracs,
        ],
        axis=0,
    )
    meta_top, meta_bottom = halo(meta, 1, 1)
    adv_top, adv_bottom = halo(advected, 1, BH)
    meta = jnp.concatenate([meta_top, meta, meta_bottom], axis=1)
    row_pos = BH // 2 * meta[0] + meta[2]
    pos = jnp.stack([row_pos, meta[1], meta[3]], axis=-1).astype(jnp.int32).reshape(-1)
    row_w, row_s = catmull(meta[4])
    col_w, col_s = catmull(meta[5])
    wgt = rounded(jnp.concatenate([col_w, row_w, col_s, row_s], axis=-1)).reshape(-1)

    dy_band = spread(pos, wgt, cot_top, cotangent, cot_bottom)
    dy_send = dy_band.reshape(grp, point_rows, channels_dev, columns)
    dy_points = lax.all_to_all(dy_send, "grp", split_axis=0, concat_axis=0, tiled=True)
    frac_parts = frac_sums(pos, wgt, adv_top, advected, adv_bottom, cotangent)
    frac_local = jnp.sum(frac_parts, axis=(2, 3)).reshape(-1)

    x_rows = inputs.transpose(1, 0, 2)
    dx_rows, g_in, g_out, g_bias = mlp(x_rows, dy_points, w_in, bias_in, w_out)
    grad_inputs = dx_rows.transpose(1, 0, 2)

    parts = lat * grp
    each = HID // parts
    mine = lax.axis_index("lat")
    slots = jnp.where(jnp.arange(lat) == mine, 1.0, 0.0)[:, None] * frac_local[None]
    slots = jnp.broadcast_to(slots[:, None], (lat, grp, frac_local.shape[0]))
    send = jnp.concatenate(
        [
            g_in.reshape(parts, each * C),
            g_out.reshape(parts, each * C),
            jnp.sum(g_bias, axis=1).reshape(parts, each),
            slots.reshape(parts, -1),
        ],
        axis=1,
    )
    got = lax.all_to_all(send, ("lat", "grp"), split_axis=0, concat_axis=0, tiled=True)
    total = jnp.sum(got, axis=0)
    scale = 1.0 / math.sqrt(point_rows * columns * parts)
    cut = each * C
    grad_first = total[:cut].reshape(each, C).T * scale
    grad_second = total[cut : 2 * cut].reshape(each, C) * scale
    grad_shift = total[2 * cut : 2 * cut + each] * scale
    grad_frac = total[2 * cut + each :].reshape(2, row_blocks, columns // BW)
    grad_frac = grad_frac / math.sqrt(C * BH * BW)
    return (grad_inputs, grad_first, grad_shift, grad_second, grad_frac)


def solution(mesh):
    placed = (
        P(None, ("lat", "grp"), None),
        P(),
        P(),
        P(),
        P("grp", "lat", None),
        P("grp", "lat", None),
        P(None, "lat", None),
        P("lat", None),
        P("lat", None),
        P(None, "lat", None),
    )
    return jax.shard_map(
        shards,
        mesh=mesh,
        in_specs=placed,
        out_specs=(
            P(None, ("lat", "grp"), None),
            P(None, ("lat", "grp")),
            P(("lat", "grp")),
            P(("lat", "grp"), None),
            P(None, "lat", None),
        ),
        check_vma=False,
    )
```

time: 907 us -> 195 us (0.21); the launches traced: 893 us -> 194 us
  other arithmetic: 225 us -> 6.03 us
  matrix products: 193 us -> 0 us
  local copies, waits for them, and re-layouts: 195 us -> 28.2 us
  blocking collectives: 162 us -> 0 us
  Pallas kernels: 0 us -> 62.4 us
  waiting for transfers between devices: 77.8 us -> 37.8 us
  starting transfers between devices: 20.8 us -> 58.3 us
  between operations: 14.6 us -> 0.87 us
    dot_general x197 -> x0, matrix products: 193 us -> none  [the longest x64 76.3 us: per_row(): product = jnp.dot(block_cot, rx_both, preferred_element_type=jnp.float32)]
    another operation x49 -> x0, other arithmetic: 94.8 us -> none  [the longest x32 82.1 us: per_row(): jnp.stack([jnp.stack(grad_rows), jnp.stack(grad_cols)])]
    psum x1 -> x0, blocking collectives: 86.8 us -> none  [shards(): frac_total = lax.psum(frac_local, 'grp')]
    unnamed x1 -> x0, blocking collectives: 75.2 us -> none
    unnamed x2 -> x0, waiting for transfers between devices: 66.3 us -> none
    slice x51 -> x3, local copies, waits for them, and re-layouts: 65 us -> 2.22 us  [the longest x2 2.14 us: halo(): head = lax.slice_in_dim(band, 0, width, axis=dim)]
    pallas_call x0 -> x3, Pallas kernels: none -> 62.4 us  [the longest x1 21.8 us: mlp(): pl.pallas_call(mlp_body, name='mlp', out_shape=(jax.ShapeDtypeStruct((row...]
    reduce_sum x64 -> x3, other arithmetic: 49 us -> 2.44 us  [the longest x1 1.6 us: shards(): frac_local = jnp.sum(frac_parts, axis=(2, 3)).reshape(-1)]
  transfers between devices with their start and end apart: 6 -> 8, of which waited for: 3 -> 4; matrix products, arithmetic and copies ran while one was open for 5% -> 11% of each run, Pallas kernels for 0% -> 11%
where the time goes in v1:
time: 195 us; the launch traced here: 194 us
  Pallas kernels  62.4 us (32%)
  starting transfers between devices  58.3 us (30%)
  waiting for transfers between devices  37.8 us (19%)
  local copies, waits for them, and re-layouts  28.2 us (14%)
  other arithmetic  6.03 us (3%)
    all_to_all x1, starting transfers between devices, shards(): lax.all_to_all(send, ('lat', 'grp'), split_axis=0, concat_axis=0, tiled=T...  30.4 us
    pallas_call x1, Pallas kernels, mlp(): pl.pallas_call(mlp_body, name='mlp', out_shape=(jax.ShapeDtypeStruct((row...  21.8 us
    pallas_call x1, Pallas kernels, frac_sums(): pl.pallas_call(frac_body, name='frac_sums', out_shape=jax.ShapeDtypeStruc...  21.6 us
    pallas_call x1, Pallas kernels, spread(): pl.pallas_call(spread_body, name='spread', out_shape=jax.ShapeDtypeStruct...  19 us
    ppermute x3, waiting for transfers between devices, halo(): below = lax.ppermute(head, 'lat', [(i + 1, i) for i in range(count - 1)])  16.3 us
    unnamed x18, local copies, waits for them, and re-layouts  16 us
    all_to_all x1, waiting for transfers between devices, shards(): lax.all_to_all(send, ('lat', 'grp'), split_axis=0, concat_axis=0, tiled=T...  14.3 us
    ppermute x3, starting transfers between devices, halo(): above = lax.ppermute(tail, 'lat', [(i, i + 1) for i in range(count - 1)])  14 us
  transfers between devices with their start and end apart: 8, of which 4 were waited for; matrix products, arithmetic and copies ran while one was open for 11% of the time, Pallas kernels for 11%

profile of v1, /device:TPU:1, one launch (start us, length us, event | category | flops | bytes accessed | tf_op | source)
XLA Modules:
  0.0 193.6 jit_solution(14755595235181125474)
XLA Ops:
  2.8 6.2 %collective-permute-start = (f32[6,1,4]{1,2,0:T(4,128)S(1)}, f32[6,1,4]{1,2,0:T(4,128)S(1)}, u32[]{:S(2)}, u32[]{:S(2)}) collective-permute-start(f32[6,1,4]{1,2,0:T(4,128)S(1)} %get-tuple-element.54), channel_id=1, source_target_pairs={{0,32},{32,64},{64,96},{1,33},{33,65},{65,97},{2,34},{34,66},{66,9... | collective-permute-start | bytes 296 | tf_op jit(solution)/shard_map/ppermute | solution.py:46
  9.0 1.9 collective-permute-start.1
  10.9 1.1 fusion.2
  12.0 5.1 %collective-permute-start.2 = (bf16[8,16,1024]{2,1,0:T(8,128)(2,1)S(1)}, bf16[8,16,1024]{2,1,0:T(8,128)(2,1)S(1)}, u32[]{:S(2)}, u32[]{:S(2)}) collective-permute-start(bf16[8,16,1024]{2,1,0:T(8,128)(2,1)S(1)} %get-tuple-element.46), channel_id=1, source_target_pairs={{0,32},{32,64},{64,96},{1,33},{33,65},{65,97},{2,34},{34,66},{66,9... | collective-permute-start | bytes 786440 | tf_op jit(solution)/shard_map/ppermute | solution.py:46
  17.2 1.9 collective-permute-start.3
  21.7 4.7 %collective-permute-done.3.bot_ref = bf16[8,16,1024]{2,1,0:T(8,128)(2,1)S(1)} collective-permute-done((bf16[8,16,1024]{2,1,0:T(8,128)(2,1)S(1)}, bf16[8,16,1024]{2,1,0:T(8,128)(2,1)S(1)}, u32[]{:S(2)}, u32[]{:S(2)}) %collective-permute-start.3) | collective-permute-done | bytes 262176 | tf_op jit(solution)/shard_map/ppermute | solution.py:47
  27.0 19.0 %spread.1 = bf16[16,128,1024]{2,1,0:T(8,128)(2,1)} custom-call(s32[216]{0:T(256)} %convert_element_type.20.pos_ref, f32[1152]{0:T(1024)} %reduce_precision.8.wgt_ref, bf16[8,16,1024]{2,1,0:T(8,128)(2,1)} %copy-done.1, bf16[8,256,1024]{2,1,0:T(8,128)(2,1)} %cot_ref.1, bf16[8,16,1024]{2,1,0:T(8,128)(2,1)} %copy-done.2), custom_call_target="tpu_custom_call" | custom-call | tf_op jit(solution)/shard_map/spread/pallas_call | solution.py:134
  46.0 8.1 %all-to-all-start = ((bf16[32,8,8,1024]{3,2,1,0:T(8,128)(2,1)}), bf16[32,8,8,1024]{3,2,1,0:T(8,128)(2,1)}, u32[]{:S(2)}, u32[]{:S(2)}) async-start(bf16[32,8,8,1024]{3,2,1,0:T(8,128)(2,1)} %bitcast.26), calls=%async_computation | async-start | bytes 8388608 | tf_op jit(solution)/shard_map/all_to_all | solution.py:367
  54.2 1.1 fusion.1
  55.3 2.6 %collective-permute-start.4 = (bf16[8,16,1024]{2,1,0:T(8,128)(2,1)S(1)}, bf16[8,16,1024]{2,1,0:T(8,128)(2,1)S(1)}, u32[]{:S(2)}, u32[]{:S(2)}) collective-permute-start(bf16[8,16,1024]{2,1,0:T(8,128)(2,1)S(1)} %get-tuple-element.44), channel_id=1, source_target_pairs={{0,32},{32,64},{64,96},{1,33},{33,65},{65,97},{2,34},{34,66},{66,9... | collective-permute-start | bytes 786440 | tf_op jit(solution)/shard_map/ppermute | solution.py:46
  57.9 1.9 collective-permute-start.5
  59.9 6.6 %copy.87 = bf16[256,8,1024]{2,0,1:T(8,128)(2,1)} copy(bf16[256,8,1024]{2,1,0:T(8,128)(2,1)} %param.10) | data formatting | bytes 8388608 | tf_op args[0]
  67.3 0.9 copy.78.bias
  68.2 7.2 %collective-permute-done.4.top_ref = bf16[8,16,1024]{2,1,0:T(8,128)(2,1)S(1)} collective-permute-done((bf16[8,16,1024]{2,1,0:T(8,128)(2,1)S(1)}, bf16[8,16,1024]{2,1,0:T(8,128)(2,1)S(1)}, u32[]{:S(2)}, u32[]{:S(2)}) %collective-permute-start.4) | collective-permute-done | bytes 262176 | tf_op jit(solution)/shard_map/ppermute | solution.py:46
  75.4 11.6 %collective-permute-done.5.bot_ref = bf16[8,16,1024]{2,1,0:T(8,128)(2,1)S(1)} collective-permute-done((bf16[8,16,1024]{2,1,0:T(8,128)(2,1)S(1)}, bf16[8,16,1024]{2,1,0:T(8,128)(2,1)S(1)}, u32[]{:S(2)}, u32[]{:S(2)}) %collective-permute-start.5) | collective-permute-done | bytes 262176 | tf_op jit(solution)/shard_map/ppermute | solution.py:47
  87.7 21.6 %frac_sums.1 = f32[2,64,8,128]{3,2,1,0:T(8,128)} custom-call(s32[216]{0:T(256)} %convert_element_type.20.pos_ref, f32[1152]{0:T(1024)} %reduce_precision.8.wgt_ref, bf16[8,16,1024]{2,1,0:T(8,128)(2,1)} %copy-done.3, bf16[8,256,1024]{2,1,0:T(8,128)(2,1)} %next_ref.1, bf16[8,256,1024]{2,1,0:T(8,128)(2,1)} %next_ref.1, bf16[8,16,1024]{2,1,0:T(8,128)(2,1)} %copy-done.4, ...), custom_call_target="tpu_custom_call" | custom-call | tf_op jit(solution)/shard_map/frac_sums/pallas_call | solution.py:251
  109.3 1.6 reduce_sum.28
  111.2 21.8 %mlp.1 = (bf16[8,256,1024]{2,1,0:T(8,128)(2,1)}, f32[512,256]{1,0:T(8,128)}, f32[512,256]{1,0:T(8,128)}, f32[512,128]{1,0:T(8,128)}) custom-call(bf16[8,256,1024]{2,1,0:T(8,128)(2,1)} %bitcast.27, bf16[32,8,8,1024]{3,2,1,0:T(8,128)(2,1)} %all-to-all-done.dy_ref, bf16[512,256]{1,0:T(8,128)(2,1)} %bitcast.30, bf16[256,512]{1,0:T(8,128)(2,1)} %w_in.1, ...), custom_call_target="tpu_custom_call" | custom-call | tf_op jit(solution)/shard_map/mlp/pallas_call | solution.py:308
  133.0 1.2 reshape.491
  134.4 1.2 reshape.492
  136.7 2.3 %copy.83 = f32[128,1,2180]{2,1,0:T(1,128)} copy(f32[128,1,2180]{0,2,1:T(8,128)S(1)} %bitcast.28) | data formatting | bytes 2232320 | tf_op jit(solution)/shard_map/all_to_all | solution.py:389
  139.0 30.4 %all-to-all-start.1 = ((f32[128,1,2180]{2,1,0:T(1,128)}), f32[128,1,2180]{2,1,0:T(1,128)S(1)}, u32[]{:S(2)}, u32[]{:S(2)}) async-start(f32[128,1,2180]{2,1,0:T(1,128)} %copy.83), calls=%async_computation.1 | async-start | bytes 2359296 | tf_op jit(solution)/shard_map/all_to_all | solution.py:389
  169.5 6.5 %copy.84 = bf16[256,8,1024]{2,1,0:T(8,128)(2,1)} copy(bf16[256,8,1024]{2,0,1:T(8,128)(2,1)} %bitcast.29) | data formatting | bytes 8388608
  176.0 14.3 %all-to-all-done.1 = f32[128,1,2180]{2,1,0:T(1,128)S(1)} async-done(((f32[128,1,2180]{2,1,0:T(1,128)}), f32[128,1,2180]{2,1,0:T(1,128)S(1)}, u32[]{:S(2)}, u32[]{:S(2)}) %all-to-all-start.1) | async-done | bytes 1116192 | tf_op jit(solution)/shard_map/all_to_all | solution.py:389
  (53 shorter events, 11.7 us)
Async XLA Ops:
  2.8 16.3 %collective-permute-start = (f32[6,1,4]{1,2,0:T(4,128)S(1)}, f32[6,1,4]{1,2,0:T(4,128)S(1)}, u32[]{:S(2)}, u32[]{:S(2)}) collective-permute-start(f32[6,1,4]{1,2,0:T(4,128)S(1)} %get-tuple-element.54), channel_id=1, source_target_pairs={{0,32},{32,64},{64,96},{1,33},{33,65},{65,97},{2,34},{34,66},{66,9... | collective-permute-start | bytes 296 | tf_op jit(solution)/shard_map/ppermute | solution.py:46
  9.0 10.1 %collective-permute-start.1 = (f32[6,1,4]{1,2,0:T(4,128)S(1)}, f32[6,1,4]{1,2,0:T(4,128)S(1)}, u32[]{:S(2)}, u32[]{:S(2)}) collective-permute-start(f32[6,1,4]{1,2,0:T(4,128)S(1)} %get-tuple-element.55), channel_id=1, source_target_pairs={{32,0},{64,32},{96,64},{33,1},{65,33},{97,65},{34,2},{66,34},{98,6... | collective-permute-start | bytes 296 | tf_op jit(solution)/shard_map/ppermute | solution.py:47
  12.0 9.7 %collective-permute-start.2 = (bf16[8,16,1024]{2,1,0:T(8,128)(2,1)S(1)}, bf16[8,16,1024]{2,1,0:T(8,128)(2,1)S(1)}, u32[]{:S(2)}, u32[]{:S(2)}) collective-permute-start(bf16[8,16,1024]{2,1,0:T(8,128)(2,1)S(1)} %get-tuple-element.46), channel_id=1, source_target_pairs={{0,32},{32,64},{64,96},{1,33},{33,65},{65,97},{2,34},{34,66},{66,9... | collective-permute-start | bytes 786440 | tf_op jit(solution)/shard_map/ppermute | solution.py:46
  17.2 9.2 %collective-permute-start.3 = (bf16[8,16,1024]{2,1,0:T(8,128)(2,1)S(1)}, bf16[8,16,1024]{2,1,0:T(8,128)(2,1)S(1)}, u32[]{:S(2)}, u32[]{:S(2)}) collective-permute-start(bf16[8,16,1024]{2,1,0:T(8,128)(2,1)S(1)} %get-tuple-element.45), channel_id=1, source_target_pairs={{32,0},{64,32},{96,64},{33,1},{65,33},{97,65},{34,2},{66,34},{98,6... | collective-permute-start | bytes 786440 | tf_op jit(solution)/shard_map/ppermute | solution.py:47
  21.7 4.7 %copy-start.1 = (bf16[8,16,1024]{2,1,0:T(8,128)(2,1)}, bf16[8,16,1024]{2,1,0:T(8,128)(2,1)S(1)}, u32[]{:S(2)}) copy-start(bf16[8,16,1024]{2,1,0:T(8,128)(2,1)S(1)} %collective-permute-done.2.top_ref) | copy-start | bytes 786436
  26.4 0.7 copy-start.2
  46.0 65.1 %all-to-all-start = ((bf16[32,8,8,1024]{3,2,1,0:T(8,128)(2,1)}), bf16[32,8,8,1024]{3,2,1,0:T(8,128)(2,1)}, u32[]{:S(2)}, u32[]{:S(2)}) async-start(bf16[32,8,8,1024]{3,2,1,0:T(8,128)(2,1)} %bitcast.26), calls=%async_computation | async-start | bytes 8388608 | tf_op jit(solution)/shard_map/all_to_all | solution.py:367
  55.3 20.1 %collective-permute-start.4 = (bf16[8,16,1024]{2,1,0:T(8,128)(2,1)S(1)}, bf16[8,16,1024]{2,1,0:T(8,128)(2,1)S(1)}, u32[]{:S(2)}, u32[]{:S(2)}) collective-permute-start(bf16[8,16,1024]{2,1,0:T(8,128)(2,1)S(1)} %get-tuple-element.44), channel_id=1, source_target_pairs={{0,32},{32,64},{64,96},{1,33},{33,65},{65,97},{2,34},{34,66},{66,9... | collective-permute-start | bytes 786440 | tf_op jit(solution)/shard_map/ppermute | solution.py:46
  57.9 29.1 %collective-permute-start.5 = (bf16[8,16,1024]{2,1,0:T(8,128)(2,1)S(1)}, bf16[8,16,1024]{2,1,0:T(8,128)(2,1)S(1)}, u32[]{:S(2)}, u32[]{:S(2)}) collective-permute-start(bf16[8,16,1024]{2,1,0:T(8,128)(2,1)S(1)} %get-tuple-element.43), channel_id=1, source_target_pairs={{32,0},{64,32},{96,64},{33,1},{65,33},{97,65},{34,2},{66,34},{98,6... | collective-permute-start | bytes 786440 | tf_op jit(solution)/shard_map/ppermute | solution.py:47
  59.8 6.6 %copy-start = (bf16[256,512]{1,0:T(8,128)(2,1)S(1)}, bf16[256,512]{1,0:T(8,128)(2,1)}, u32[]{:S(2)}) copy-start(bf16[256,512]{1,0:T(8,128)(2,1)} %w_in.1) | copy-start | bytes 786436
  59.9 7.4 %copy-start.6 = (f32[512]{0:T(512)S(1)}, f32[512]{0:T(512)}, u32[]{:S(2)}) copy-start(f32[512]{0:T(512)} %param.12) | copy-start | bytes 6148
  75.4 11.6 %copy-start.3 = (bf16[8,16,1024]{2,1,0:T(8,128)(2,1)}, bf16[8,16,1024]{2,1,0:T(8,128)(2,1)S(1)}, u32[]{:S(2)}) copy-start(bf16[8,16,1024]{2,1,0:T(8,128)(2,1)S(1)} %collective-permute-done.4.top_ref) | copy-start | bytes 786436
  87.0 0.7 copy-start.4
  133.0 2.8 %copy-start.5 = (f32[512,128]{1,0:T(8,128)S(1)}, f32[512,128]{1,0:T(8,128)}, u32[]{:S(2)}) copy-start(f32[512,128]{1,0:T(8,128)} %get-tuple-element.12) | copy-start | bytes 786436
  139.0 51.3 %all-to-all-start.1 = ((f32[128,1,2180]{2,1,0:T(1,128)}), f32[128,1,2180]{2,1,0:T(1,128)S(1)}, u32[]{:S(2)}, u32[]{:S(2)}) async-start(f32[128,1,2180]{2,1,0:T(1,128)} %copy.83), calls=%async_computation.1 | async-start | bytes 2359296 | tf_op jit(solution)/shard_map/all_to_all | solution.py:389

commit v2 on v1

v2 whole, which is shorter than its diff:
```python
import math

import jax
import jax.numpy as jnp
import numpy as np
from jax import lax
from jax.experimental import pallas as pl
from jax.experimental.pallas import tpu as pltpu
from jax.sharding import PartitionSpec as P

C = 256
BH = 16
BW = 256
LANES = 128
HID = 512
F32 = jnp.float32
BF16 = jnp.bfloat16


CUBIC = (
    (-1.0, 2.0, -1.0, 0.0),
    (3.0, -5.0, 0.0, 2.0),
    (-3.0, 4.0, 1.0, 0.0),
    (1.0, -1.0, 0.0, 0.0),
    (0.0, -3.0, 4.0, -1.0),
    (0.0, 9.0, -10.0, 0.0),
    (0.0, -9.0, 8.0, 1.0),
    (0.0, 3.0, -2.0, 0.0),
)
COL_W, ROW_W, COL_S, ROW_S = 0, 4, 8, 12
EDGE = 11


def catmull(row_frac, col_frac):
    order = (0, 1, 2, 3, 0, 1, 2, 3, 4, 5, 6, 7, 4, 5, 6, 7)
    table = np.asarray([CUBIC[k] for k in order], np.float32)[:, :, None, None]
    on_col = np.asarray([1, 1, 1, 1, 0, 0, 0, 0] * 2, np.bool_)[:, None, None]
    frac = jnp.where(on_col, col_frac[None], row_frac[None])
    square = frac * frac
    cube = square * frac
    value = table[:, 0] * cube + table[:, 1] * square + table[:, 2] * frac + table[:, 3]
    return lax.reduce_precision(0.5 * value, 8, 7)


def exchange(head, tail):
    count = lax.axis_size("lat")
    above = lax.ppermute(tail, "lat", [(i, i + 1) for i in range(count - 1)])
    below = lax.ppermute(head, "lat", [(i + 1, i) for i in range(count - 1)])
    return above, below


def channel_minor():
    out = lax.broadcasted_iota(jnp.int32, (LANES, LANES), 0)
    src = lax.broadcasted_iota(jnp.int32, (LANES, LANES), 1)
    return ((out % 8) * 16 + out // 8 == src).astype(F32).astype(BF16)


def lanes():
    lane = lax.broadcasted_iota(jnp.int32, (8, LANES), 1)
    return lane, lax.broadcasted_iota(jnp.int32, (8, LANES), 0)


def col_taps(weights, shift):
    lane, row = lanes()
    base = jnp.zeros((8, LANES), F32)
    for tap in range(4):
        base = jnp.where(lane - row == tap, weights[tap], base)
    left, right = [], []
    for group in range(0, LANES, 8):
        moved = pltpu.roll(base, (shift + group) & (LANES - 1), 1)
        inside = lane - row >= shift + group
        left.append(jnp.where(inside, moved, 0.0))
        right.append(jnp.where(inside, 0.0, moved))
    both = [jnp.concatenate(left, axis=0), jnp.concatenate(right, axis=0)]
    return jnp.concatenate(both, axis=1).astype(BF16)


REACH = BH + 4


def row_taps(weights):
    lane, row = lanes()
    base = jnp.zeros((8, LANES), F32)
    for tap in range(4):
        base = jnp.where((lane - BH * row + tap) & (LANES - 1) == 0, weights[tap], base)
    own = lane // BH == row
    moved = [base] + [pltpu.roll(base, step, 1) for step in range(1, REACH)]
    return jnp.concatenate([jnp.where(own, part, 0.0) for part in moved], axis=0).astype(BF16)


def pack_body(offs, srow, scol, wgt, *refs):
    sources, (head_ref, tail_ref) = refs[:4], refs[4:]
    channels = sources[0].shape[0]
    last = offs.shape[2] - 1
    lane = lax.broadcasted_iota(jnp.int32, (BH, LANES), 1)
    for side, (out_ref, row) in enumerate(((head_ref, 0), (tail_ref, last))):
        out_ref[0:channels] = sources[2 * side][...]
        out_ref[channels : 2 * channels] = sources[2 * side + 1][...]
        value = jnp.zeros((BH, LANES), F32)
        for block in range(4):
            own = [
                (BH // 2 * offs[0, block, row] + srow[block, row]).astype(F32),
                offs[1, block, row].astype(F32),
                scol[block, row].astype(F32),
            ]
            own = own + [wgt[tap, block, row] for tap in range(8)]
            for slot, entry in enumerate(own):
                value = jnp.where(lane == block * EDGE + slot, entry, value)
        out_ref[2 * channels] = jnp.zeros(out_ref.shape[1:], BF16)
        out_ref[2 * channels, :, 0:LANES] = value.astype(BF16)


def pack(places, cot, adv):
    channels, band_rows, columns = cot.shape
    shape = (2 * channels + 1, BH, columns)
    first = pl.BlockSpec((channels, BH, columns), lambda g, *a: (0, 0, 0))
    last = pl.BlockSpec((channels, BH, columns), lambda g, *a: (0, band_rows // BH - 1, 0))
    return pl.pallas_call(
        pack_body,
        name="pack",
        out_shape=(jax.ShapeDtypeStruct(shape, BF16),) * 2,
        grid_spec=pltpu.PrefetchScalarGridSpec(
            num_scalar_prefetch=4,
            grid=(1,),
            in_specs=[first, first, last, last],
            out_specs=[pl.BlockSpec(shape, lambda g, *a: (0, 0, 0))] * 2,
        ),
        compiler_params=pltpu.CompilerParams(dimension_semantics=("arbitrary",)),
    )(*places, cot, adv, cot, adv)


def spread_blocks(jobs, tap_scr, row_scr, z_scr, acc):
    for job, (rows, block, first, py, tile, shift, wx, wy) in enumerate(jobs):
        tap_scr[job] = col_taps(wx, shift)
        row_scr[job] = row_taps(wy)
    for job, (rows, block, first, py, tile, shift, wx, wy) in enumerate(jobs):
        z = jnp.dot(halves_of(rows, block), tap_scr[job], preferred_element_type=F32)
        z_scr[job, :, 0:LANES] = z[0:LANES, 0:LANES].astype(BF16)
        middle = z[0:LANES, LANES:] + z[LANES:, 0:LANES]
        z_scr[job, :, LANES : 2 * LANES] = middle.astype(BF16)
        z_scr[job, :, 2 * LANES :] = z[LANES:, LANES:].astype(BF16)
    moved = [
        jnp.dot(row_scr[job], z_scr[job], preferred_element_type=F32) for job in range(len(jobs))
    ]
    for job, (rows, block, first, py, tile, shift, wx, wy) in enumerate(jobs):
        for part in range(3):
            target = (2 * block + 6 + part + tile) & 7
            value = moved[job][:, part * LANES : (part + 1) * LANES].reshape(REACH, 8, LANES)
            at = pl.ds(first + py, REACH)
            acc[at, target] = acc[at, target] + value


def spread_scratch():
    return [
        pltpu.VMEM((8, LANES, 2 * LANES), BF16),
        pltpu.VMEM((8, REACH * 8, LANES), BF16),
        pltpu.VMEM((8, LANES, 3 * LANES), BF16),
    ]


def halves_of(rows, block):
    return jnp.concatenate(
        [
            rows[:, block * BW : block * BW + LANES],
            rows[:, block * BW + LANES : (block + 1) * BW],
        ],
        axis=0,
    )


def emit(acc, first, out_ref):
    for tile_index in range(8):
        done = acc[pl.ds(first, BH), tile_index].reshape(BH * 8, LANES)
        out_ref[:, tile_index * LANES : (tile_index + 1) * LANES] = done.astype(BF16)


def spread_body(offs, srow, scol, wgt, cot_ref, out_ref, edge_ref, tap_scr, row_scr, z_scr, acc):
    step = pl.program_id(0)
    last = pl.num_programs(0) - 1

    @pl.when(step == 0)
    def _():
        acc[0 : 2 * BH] = jnp.zeros((2 * BH,) + acc.shape[1:], F32)

    @pl.when(step < last)
    def _():
        acc[pl.ds((2 * step + 2) * BH, 2 * BH)] = jnp.zeros((2 * BH,) + acc.shape[1:], F32)
        jobs = []
        for half in range(2):
            row = 2 * step + half
            rows = cot_ref[:, half * BH : (half + 1) * BH].reshape(LANES, cot_ref.shape[2])
            for block in range(4):
                jobs.append(
                    (
                        rows,
                        block,
                        row * BH,
                        BH // 2 * offs[0, block, row] + srow[block, row],
                        offs[1, block, row],
                        scol[block, row],
                        [wgt[COL_W + tap, block, row] for tap in range(4)],
                        [wgt[ROW_W + tap, block, row] for tap in range(4)],
                    )
                )
        spread_blocks(jobs, tap_scr, row_scr, z_scr, acc)

    emit(acc, jnp.maximum(2 * step - 1, 0) * BH, out_ref.at[0])
    emit(acc, 2 * step * BH, out_ref.at[1])

    @pl.when(step == 0)
    def _():
        edge_ref[0] = acc[BH : 2 * BH]

    @pl.when(step == last)
    def _():
        edge_ref[0] = acc[pl.ds(2 * last * BH, BH)]


def spread(places, cot):
    channels, band_rows, columns = cot.shape
    blocks = band_rows // BH
    pairs = blocks // 2
    tiles = columns // LANES
    return pl.pallas_call(
        spread_body,
        name="spread",
        out_shape=(
            jax.ShapeDtypeStruct((blocks, BH * channels, columns), BF16),
            jax.ShapeDtypeStruct((2, BH, tiles, channels, LANES), F32),
        ),
        grid_spec=pltpu.PrefetchScalarGridSpec(
            num_scalar_prefetch=4,
            grid=(pairs + 1,),
            in_specs=[
                pl.BlockSpec(
                    (channels, 2 * BH, columns), lambda g, *a: (0, jnp.minimum(g, pairs - 1), 0)
                )
            ],
            out_specs=[
                pl.BlockSpec(
                    (2, BH * channels, columns), lambda g, *a: (jnp.maximum(g - 1, 0), 0, 0)
                ),
                pl.BlockSpec(
                    (1, BH, tiles, channels, LANES),
                    lambda g, *a: (jnp.where(g == pairs, 1, 0), 0, 0, 0, 0),
                ),
            ],
            scratch_shapes=spread_scratch()
            + [pltpu.VMEM(((blocks + 2) * BH, tiles, channels, LANES), F32)],
        ),
        compiler_params=pltpu.CompilerParams(dimension_semantics=("arbitrary",)),
    )(*places, cot)


def edge_body(meta, top_ref, bot_ref, edge_ref, whole, out_ref, tap_scr, row_scr, z_scr, acc):
    step = pl.program_id(0)
    upper, lower = 2 * BH, 3 * BH

    @pl.when(step == 0)
    def _():
        acc[0:upper] = jnp.zeros((upper,) + acc.shape[1:], F32)
        acc[upper : upper + BH] = edge_ref[0]
        acc[lower : lower + BH] = edge_ref[1]
        acc[lower + BH :] = jnp.zeros((2 * BH,) + acc.shape[1:], F32)
        jobs = []
        for side, ref in enumerate((top_ref, bot_ref)):
            rows = ref[...].reshape(LANES, ref.shape[2])
            for block in range(4):
                own = [meta[side, block * EDGE + slot] for slot in range(EDGE)]
                place = [entry.astype(jnp.int32) for entry in own[:3]]
                jobs.append((rows, block, side * lower, *place, own[3:7], own[7:11]))
        spread_blocks(jobs, tap_scr, row_scr, z_scr, acc)

    emit(acc, upper + step * BH, out_ref.at[0])


def spread_edges(meta, top, bottom, edges, dy):
    blocks, rows, columns = dy.shape
    channels = edges.shape[3]
    return pl.pallas_call(
        edge_body,
        name="spread_edges",
        out_shape=jax.ShapeDtypeStruct(dy.shape, dy.dtype),
        grid_spec=pltpu.PrefetchScalarGridSpec(
            num_scalar_prefetch=1,
            grid=(2,),
            in_specs=[
                pl.BlockSpec((channels, BH, columns), lambda g, a: (0, 0, 0)),
                pl.BlockSpec((channels, BH, columns), lambda g, a: (0, 0, 0)),
                pl.BlockSpec(edges.shape, lambda g, a: (0, 0, 0, 0, 0)),
                pl.BlockSpec(memory_space=pl.ANY),
            ],
            out_specs=pl.BlockSpec((1, rows, columns), lambda g, a: (g * (blocks - 1), 0, 0)),
            scratch_shapes=spread_scratch() + [pltpu.VMEM((6 * BH,) + edges.shape[2:], F32)],
        ),
        input_output_aliases={4: 0},
        compiler_params=pltpu.CompilerParams(dimension_semantics=("arbitrary",)),
    )(meta, top, bottom, edges, dy)


def frac_body(
    offs, srow, scol, wgt, top_ref, mid_ref, next_ref, bot_ref, cot_ref, out_ref, cot_scr, z_scr, field
):
    step = pl.program_id(0)
    last = pl.num_programs(0) - 1
    width = cot_scr.shape[1]
    order = channel_minor()

    def put(row_block, source):
        rows = source[...].reshape(LANES, width)
        moved = jnp.dot(order, rows, preferred_element_type=F32)
        for tile_index in range(8):
            field[pl.ds(row_block * BH, BH), tile_index] = moved[
                :, tile_index * LANES : (tile_index + 1) * LANES
            ].reshape(BH, 8, LANES)

    @pl.when(step == 0)
    def _():
        put(0, top_ref)
        put(1, mid_ref)

    @pl.when(step == last)
    def _():
        put(step + 2, bot_ref)

    @pl.when(step < last)
    def _():
        put(step + 2, next_ref)

    rows = cot_ref[...].reshape(LANES, width)
    cot_scr[...] = jnp.dot(order, rows, preferred_element_type=F32).astype(BF16)
    for block in range(4):
        py = BH // 2 * offs[0, block, step] + srow[block, step]
        tile = offs[1, block, step]
        shift = scol[block, step]
        both = jnp.concatenate(
            [
                col_taps([wgt[COL_W + tap, block, step] for tap in range(4)], shift),
                col_taps([wgt[COL_S + tap, block, step] for tap in range(4)], shift),
            ],
            axis=1,
        )
        halves = jnp.concatenate(
            [
                cot_scr[:, block * BW : block * BW + LANES],
                cot_scr[:, block * BW + LANES : (block + 1) * BW],
            ],
            axis=0,
        )
        z_scr[block] = jnp.dot(halves, both, preferred_element_type=F32)
        by_value = [jnp.zeros((8, LANES), F32) for tap in range(4)]
        by_slope = [jnp.zeros((8, LANES), F32) for tap in range(4)]
        for part in range(3):
            pair = []
            for lane in (0, 2 * LANES):
                if part == 0:
                    z = z_scr[block, 0:LANES, lane : lane + LANES]
                elif part == 1:
                    z = (
                        z_scr[block, 0:LANES, lane + LANES : lane + 2 * LANES]
                        + z_scr[block, LANES:, lane : lane + LANES]
                    )
                else:
                    z = z_scr[block, LANES:, lane + LANES : lane + 2 * LANES]
                pair.append(z.reshape(BH, 8, LANES))
            source = (2 * block + 6 + part + tile) & 7
            for j in range(BH + 3):
                value = field[step * BH + py + j, source]
                for tap in range(4):
                    if 0 <= j - tap < BH:
                        by_value[tap] = by_value[tap] + value * pair[0][j - tap]
                        by_slope[tap] = by_slope[tap] + value * pair[1][j - tap]
        first = jnp.zeros((8, LANES), F32)
        second = jnp.zeros((8, LANES), F32)
        for tap in range(4):
            first = first + wgt[ROW_S + tap, block, step] * by_value[tap]
            second = second + wgt[ROW_W + tap, block, step] * by_slope[tap]
        out_ref[0, block] = first
        out_ref[1, block] = second


def frac_sums(places, top, field, bottom, cot):
    channels, band_rows, columns = cot.shape
    blocks = band_rows // BH
    shape = (channels, BH, columns)
    return pl.pallas_call(
        frac_body,
        name="frac_sums",
        out_shape=jax.ShapeDtypeStruct((2, blocks * 4, 8, LANES), F32),
        grid_spec=pltpu.PrefetchScalarGridSpec(
            num_scalar_prefetch=4,
            grid=(blocks,),
            in_specs=[
                pl.BlockSpec(shape, lambda g, *a: (1, 0, 0)),
                pl.BlockSpec(shape, lambda g, *a: (0, 0, 0)),
                pl.BlockSpec(shape, lambda g, *a: (0, jnp.minimum(g + 1, blocks - 1), 0)),
                pl.BlockSpec(shape, lambda g, *a: (1, 0, 0)),
                pl.BlockSpec(shape, lambda g, *a: (0, g, 0)),
            ],
            out_specs=pl.BlockSpec((2, 4, 8, LANES), lambda g, *a: (0, g, 0, 0)),
            scratch_shapes=[
                pltpu.VMEM((BH * channels, columns), BF16),
                pltpu.VMEM((4, 2 * LANES, 4 * LANES), F32),
                pltpu.VMEM(((blocks + 2) * BH, columns // LANES, channels, LANES), F32),
            ],
        ),
        compiler_params=pltpu.CompilerParams(dimension_semantics=("arbitrary",)),
    )(*places, top, field, field, bottom, cot)


def mlp_body(
    x_ref, dy_ref, w_in_t, w_in, w_out, half_bias, tail_ref, dx_ref, send_ref, g_in, g_out, g_bias,
    act_scr, dpre_scr
):
    row = pl.program_id(0)

    @pl.when(row == 0)
    def _():
        g_in[...] = jnp.zeros_like(g_in)
        g_out[...] = jnp.zeros_like(g_out)
        g_bias[...] = jnp.zeros_like(g_bias)

    part = 256
    points = (((1,), (1,)), ((), ()))

    def gates(at):
        x = x_ref[0, :, at : at + part]
        dy = dy_ref[:, :, at : at + part].reshape(C, part)
        half = jnp.dot(w_in_t[...], x, preferred_element_type=F32) + half_bias[...]
        twice = 1.0 + jnp.tanh(half)
        act = half * twice
        dact = jnp.dot(w_out[...], dy, preferred_element_type=F32)
        dpre = (dact * (twice + act * (2.0 - twice))).astype(BF16)
        act_scr[:, at : at + part] = act.astype(BF16)
        dpre_scr[:, at : at + part] = dpre
        total = g_bias[...]
        for lane in range(0, part, LANES):
            total = total + dpre[:, lane : lane + LANES].astype(F32)
        g_bias[...] = total

    def products(at):
        x = x_ref[0, :, at : at + part]
        dy = dy_ref[:, :, at : at + part].reshape(C, part)
        dpre = dpre_scr[:, at : at + part]
        dx = dy.astype(F32) + jnp.dot(w_in[...], dpre, preferred_element_type=F32)
        dx_ref[0, :, at : at + part] = dx.astype(BF16)
        g_in[...] += lax.dot_general(dpre, x, points, preferred_element_type=F32)
        g_out[...] += lax.dot_general(
            act_scr[:, at : at + part], dy, points, preferred_element_type=F32
        )

    width = x_ref.shape[2]
    gates(0)
    for at in range(part, width, part):
        gates(at)
        products(at - part)
    products(width - part)

    @pl.when(row == pl.num_programs(0) - 1)
    def _():
        parts, each, lanes = send_ref.shape
        shift = jnp.sum(g_bias[...], axis=1, keepdims=True)
        high = shift.astype(BF16).astype(F32)
        lane = lax.broadcasted_iota(jnp.int32, (HID, LANES), 1)
        tail = jnp.where(lane == 0, high, jnp.where(lane == 1, shift - high, tail_ref[...]))
        send = jnp.concatenate([g_in[...], g_out[...], tail], axis=1)
        send_ref[...] = send.reshape(parts, each, lanes).astype(BF16)


def mlp(x, dy, w_in, bias, w_out, tail, parts):
    rows, channels, columns = x.shape
    sources = dy.shape[0]
    whole = lambda shape: pl.BlockSpec(shape, lambda r: (0,) * len(shape))
    tile = pl.BlockSpec((1, channels, columns), lambda r: (r, 0, 0))
    send = (parts, HID // parts, 2 * channels + LANES)
    half = jnp.asarray(0.5, BF16)
    return pl.pallas_call(
        mlp_body,
        name="mlp",
        out_shape=(
            jax.ShapeDtypeStruct((rows, channels, columns), BF16),
            jax.ShapeDtypeStruct(send, BF16),
        ),
        grid=(rows,),
        in_specs=[
            tile,
            pl.BlockSpec((sources, None, 8, columns), lambda r: (0, r, 0, 0)),
            whole((HID, channels)),
            whole((channels, HID)),
            whole((HID, channels)),
            whole((HID, 1)),
            whole((HID, LANES)),
        ],
        out_specs=[tile, whole(send)],
        scratch_shapes=[
            pltpu.VMEM((HID, channels), F32),
            pltpu.VMEM((HID, channels), F32),
            pltpu.VMEM((HID, LANES), F32),
            pltpu.VMEM((HID, columns), BF16),
            pltpu.VMEM((HID, columns), BF16),
        ],
        compiler_params=pltpu.CompilerParams(dimension_semantics=("arbitrary",)),
    )(x, dy, w_in.T * half, w_in, w_out * half, 0.5 * bias[:, None], tail)


def shards(
    inputs, w_in, bias_in, w_out, advected, cotangent, offsets, stencil_row, stencil_col, fracs
):
    channels_dev, band_rows, columns = advected.shape
    row_blocks = band_rows // BH
    point_rows = inputs.shape[1]
    lat = lax.axis_size("lat")
    grp = lax.axis_size("grp")

    fracs = fracs.transpose(0, 2, 1)
    places = (
        offsets.transpose(0, 2, 1),
        stencil_row.T,
        stencil_col.T,
        catmull(fracs[0], fracs[1]),
    )
    head, tail = pack(places, cotangent, advected)
    top, bottom = exchange(head, tail)
    dy_band, edges = spread(places, cotangent)
    meta = jnp.stack([top[2 * channels_dev, 0, :LANES], bottom[2 * channels_dev, 0, :LANES]])
    dy_band = spread_edges(meta.astype(F32), top, bottom, edges, dy_band)
    dy_send = dy_band.reshape(grp, point_rows, channels_dev, columns)
    dy_points = lax.all_to_all(dy_send, "grp", split_axis=0, concat_axis=0, tiled=True)

    frac_parts = frac_sums(places, top, advected, bottom, cotangent)
    frac_local = jnp.sum(frac_parts, axis=(2, 3)).reshape(-1)
    parts = lat * grp
    each = HID // parts
    held = frac_local.shape[0] // each
    high = lax.reduce_precision(frac_local, 8, 7)
    both = jnp.stack([high.reshape(each, held), (frac_local - high).reshape(each, held)], axis=1)
    mine = jnp.where(jnp.arange(lat) == lax.axis_index("lat"), 1.0, 0.0)
    slots = mine[:, None, None, None] * both.reshape(1, 1, each, 2 * held)
    slots = jnp.broadcast_to(slots, (lat, grp, each, 2 * held)).reshape(HID, 2 * held)
    extra = jnp.pad(slots, ((0, 0), (held, LANES - 3 * held)))

    x_rows = inputs.transpose(1, 0, 2)
    dx_rows, send = mlp(x_rows, dy_points, w_in, bias_in, w_out, extra, parts)
    grad_inputs = dx_rows.transpose(1, 0, 2)

    got = lax.all_to_all(send, ("lat", "grp"), split_axis=0, concat_axis=0, tiled=True)
    total = jnp.sum(got.astype(F32), axis=0)
    scale = 1.0 / math.sqrt(point_rows * columns * parts)
    grad_first = total[:, :C].T * scale
    grad_second = total[:, C : 2 * C] * scale
    grad_shift = (total[:, 2 * C] + total[:, 2 * C + 1]) * scale
    total = total[:, 2 * C + held : 2 * C + 2 * held] + total[:, 2 * C + 2 * held : 2 * C + 3 * held]
    grad_frac = total.reshape(2, row_blocks, columns // BW) / math.sqrt(C * BH * BW)
    return (grad_inputs, grad_first, grad_shift, grad_second, grad_frac)


def solution(mesh):
    placed = (
        P(None, ("lat", "grp"), None),
        P(),
        P(),
        P(),
        P("grp", "lat", None),
        P("grp", "lat", None),
        P(None, "lat", None),
        P("lat", None),
        P("lat", None),
        P(None, "lat", None),
    )
    return jax.shard_map(
        shards,
        mesh=mesh,
        in_specs=placed,
        out_specs=(
            P(None, ("lat", "grp"), None),
            P(None, ("lat", "grp")),
            P(("lat", "grp")),
            P(("lat", "grp"), None),
            P(None, "lat", None),
        ),
        check_vma=False,
    )
```

time: 195 us -> 139 us (0.71)
  starting transfers between devices: 58.3 us -> 24.3 us
  local copies, waits for them, and re-layouts: 28.2 us -> 17.1 us
  waiting for transfers between devices: 37.8 us -> 28.3 us
    ppermute x6 -> x2, waiting for transfers between devices: 23.5 us -> 0.01 us  [the longest x1 0.01 us: exchange(): above = lax.ppermute(tail, 'lat', [(i, i + 1) for i in range(count - 1)])]
    all_to_all x1, starting transfers between devices: 30.4 us -> 7.39 us  [shards(): lax.all_to_all(send, ('lat', 'grp'), split_axis=0, concat_axis=0, tiled=T...]
    all_to_all x1, waiting for transfers between devices: 0.01 us -> 19.6 us  [shards(): lax.all_to_all(dy_send, 'grp', split_axis=0, concat_axis=0, tiled=True)]
    ppermute x6 -> x2, starting transfers between devices: 19.7 us -> 8.11 us  [the longest x1 4.83 us: exchange(): above = lax.ppermute(tail, 'lat', [(i, i + 1) for i in range(count - 1)])]
    all_to_all x1, waiting for transfers between devices: 14.3 us -> 8.71 us  [shards(): lax.all_to_all(send, ('lat', 'grp'), split_axis=0, concat_axis=0, tiled=T...]
    pallas_call x1, Pallas kernels: 21.8 us -> 17.9 us  [mlp(): pl.pallas_call(mlp_body, name='mlp', out_shape=(jax.ShapeDtypeStruct((row...]
    reshape x7 -> x1, local copies, waits for them, and re-layouts: 3.06 us -> 0.08 us  [shards(): frac_local = jnp.sum(frac_parts, axis=(2, 3)).reshape(-1)]
    pallas_call x1 -> x3, Pallas kernels: 19 us -> 21.7 us  [the longest x1 13.9 us: spread(): pl.pallas_call(spread_body, name='spread', out_shape=(jax.ShapeDtypeStruc...]
  transfers between devices with their start and end apart: 8 -> 4, of which waited for: 4 -> 2; matrix products, arithmetic and copies ran while one was open for 11% -> 13% of each run, Pallas kernels for 11% -> 26%
where the time goes in v2:
time: 139 us
  Pallas kernels  61.1 us (44%)
  waiting for transfers between devices  28.3 us (20%)
  starting transfers between devices  24.3 us (17%)
  local copies, waits for them, and re-layouts  17.1 us (12%)
  other arithmetic  6.98 us (5%)
    pallas_call x1, Pallas kernels, frac_sums(): pl.pallas_call(frac_body, name='frac_sums', out_shape=jax.ShapeDtypeStruc...  21.5 us
    all_to_all x1, waiting for transfers between devices, shards(): lax.all_to_all(dy_send, 'grp', split_axis=0, concat_axis=0, tiled=True)  19.6 us
    pallas_call x1, Pallas kernels, mlp(): pl.pallas_call(mlp_body, name='mlp', out_shape=(jax.ShapeDtypeStruct((row...  17.9 us
    unnamed x14, local copies, waits for them, and re-layouts  14.3 us
    pallas_call x1, Pallas kernels, spread(): pl.pallas_call(spread_body, name='spread', out_shape=(jax.ShapeDtypeStruc...  13.9 us
    all_to_all x1, starting transfers between devices, shards(): lax.all_to_all(dy_send, 'grp', split_axis=0, concat_axis=0, tiled=True)  8.78 us
    all_to_all x1, waiting for transfers between devices, shards(): lax.all_to_all(send, ('lat', 'grp'), split_axis=0, concat_axis=0, tiled=T...  8.71 us
    all_to_all x1, starting transfers between devices, shards(): lax.all_to_all(send, ('lat', 'grp'), split_axis=0, concat_axis=0, tiled=T...  7.39 us
  transfers between devices with their start and end apart: 4, of which 2 were waited for; matrix products, arithmetic and copies ran while one was open for 13% of the time, Pallas kernels for 26%

profile of v2, /device:TPU:1, one launch (start us, length us, event | category | flops | bytes accessed | tf_op | source)
XLA Modules:
  0.0 138.5 jit_solution(16546325323739454793)
XLA Ops:
  0.6 0.7 slice_bitcast_fusion.1
  1.3 1.5 %fusion.5.wgt = f32[16,4,16]{2,1,0:T(4,128)} fusion(f32[16]{0:T(128)} %constant.47, f32[16]{0:T(128)} %constant.46, f32[16]{0:T(128)} %constant.45, f32[4,16]{1,0:T(4,128)S(1)} %get-tuple-element.30, f32[4,16]{1,0:T(4,128)S(1)} %get-tuple-element.29, f32[16]{0:T(128)} %constant.43, pred[16]{0:T(512)(128)(4,1)} %constant.44), kind=kLoop, calls=%fused_computation.12 | loop fusion | flops 11264 | bytes 4880 | tf_op jit(solution)/shard_map/reduce_precision | solution.py:42
  2.8 3.6 %pack.1 = (bf16[17,16,1024]{2,1,0:T(8,128)(2,1)}, bf16[17,16,1024]{2,1,0:T(8,128)(2,1)}) custom-call(s32[2,4,16]{2,1,0:T(4,128)} %bitcast.27, s32[4,16]{1,0:T(4,128)} %bitcast.30, s32[4,16]{1,0:T(4,128)} %bitcast.33, f32[16,4,16]{2,1,0:T(4,128)} %fusion.5.wgt, bf16[8,256,1024]{2,1,0:T(8,128)(2,1)} %cot_ref.3, bf16[8,256,1024]{2,1,0:T(8,128)(2,1)} %next_ref.1, ...), custom_call_target="tpu_custom_call" | custom-call | tf_op jit(solution)/shard_map/pack/pallas_call | solution.py:118
  6.4 3.3 %collective-permute-start.1 = (bf16[17,16,1024]{2,1,0:T(8,128)(2,1)}, bf16[17,16,1024]{2,1,0:T(8,128)(2,1)S(1)}, u32[]{:S(2)}, u32[]{:S(2)}) collective-permute-start(bf16[17,16,1024]{2,1,0:T(8,128)(2,1)} %get-tuple-element.12), channel_id=1, source_target_pairs={{32,0},{64,32},{96,64},{33,1},{65,33},{97,65},{34,2},{66,34},{98,6... | collective-permute-start | bytes 1671176 | tf_op jit(solution)/shard_map/ppermute | solution.py:48
  9.7 4.8 %collective-permute-start = (bf16[17,16,1024]{2,1,0:T(8,128)(2,1)}, bf16[17,16,1024]{2,1,0:T(8,128)(2,1)S(1)}, u32[]{:S(2)}, u32[]{:S(2)}) collective-permute-start(bf16[17,16,1024]{2,1,0:T(8,128)(2,1)} %get-tuple-element.11), channel_id=1, source_target_pairs={{0,32},{32,64},{64,96},{1,33},{33,65},{65,97},{2,34},{34,66},{66,9... | collective-permute-start | bytes 1671176 | tf_op jit(solution)/shard_map/ppermute | solution.py:47
  14.5 13.9 %spread.1 = (bf16[16,128,1024]{2,1,0:T(8,128)(2,1)}, f32[2,16,8,8,128]{4,3,2,1,0:T(8,128)}) custom-call(s32[2,4,16]{2,1,0:T(4,128)} %bitcast.28, s32[4,16]{1,0:T(4,128)} %bitcast.31, s32[4,16]{1,0:T(4,128)} %bitcast.34, f32[16,4,16]{2,1,0:T(4,128)} %fusion.5.wgt, bf16[8,256,1024]{2,1,0:T(8,128)(2,1)} %cot_ref.3), custom_call_target="tpu_custom_call" | custom-call | tf_op jit(solution)/shard_map/spread/pallas_call | solution.py:224
  28.4 0.6 maximum_convert_fusion.meta
  29.5 4.2 %spread_edges.1 = bf16[16,128,1024]{2,1,0:T(8,128)(2,1)} custom-call(f32[2,128]{1,0:T(2,128)} %maximum_convert_fusion.meta, bf16[17,16,1024]{2,1,0:T(8,128)(2,1)} %copy-done.1, bf16[17,16,1024]{2,1,0:T(8,128)(2,1)} %copy-done, f32[2,16,8,8,128]{4,3,2,1,0:T(8,128)} %get-tuple-element.13.edge_ref, ...), custom_call_target="tpu_custom_call", output_to_operand_aliasing={{}: (4, {})} | custom-call | tf_op jit(solution)/shard_map/spread_edges/pallas_call | solution.py:280
  33.7 8.8 %all-to-all-start = ((bf16[32,8,8,1024]{3,2,1,0:T(8,128)(2,1)}), bf16[32,8,8,1024]{3,2,1,0:T(8,128)(2,1)}, u32[]{:S(2)}, u32[]{:S(2)}) async-start(bf16[32,8,8,1024]{3,2,1,0:T(8,128)(2,1)} %bitcast.24), calls=%async_computation | async-start | bytes 8388608 | tf_op jit(solution)/shard_map/all_to_all | solution.py:528
  42.5 6.6 %copy.32 = bf16[256,8,1024]{2,0,1:T(8,128)(2,1)} copy(bf16[256,8,1024]{2,1,0:T(8,128)(2,1)} %param.15) | data formatting | bytes 8388608 | tf_op args[0]
  49.2 0.9 copy.28.half_bias
  50.1 0.7 multiply_bitcast_fusion.w_in_t
  50.9 0.7 broadcast_multiply_fusion.w_out
  51.6 21.5 %frac_sums.1 = f32[2,64,8,128]{3,2,1,0:T(8,128)} custom-call(s32[2,4,16]{2,1,0:T(4,128)} %bitcast.29, s32[4,16]{1,0:T(4,128)} %bitcast.32, s32[4,16]{1,0:T(4,128)} %bitcast.35, f32[16,4,16]{2,1,0:T(4,128)} %fusion.5.wgt, bf16[17,16,1024]{2,1,0:T(8,128)(2,1)} %copy-done.1, bf16[8,256,1024]{2,1,0:T(8,128)(2,1)} %next_ref.1, bf16[8,256,1024]{2,1,0:T(8,128)(2,1)} %next_ref.1, ...), custom_call_target="tpu_custom_call" | custom-call | tf_op jit(solution)/shard_map/frac_sums/pallas_call | solution.py:386
  73.1 1.6 %reduce_sum.18 = f32[2,64]{1,0:T(2,128)S(1)} reduce(f32[2,64,8,128]{3,2,1,0:T(8,128)} %frac_sums.1, f32[]{:T(128)} %constant.9.clone.1), dimensions={2,3}, to_apply=%region_0.1 | reduce | flops 130944 | bytes 524804 | tf_op jit(solution)/shard_map/reduce_sum | solution.py:531
  75.0 0.9 pad.4.tail_ref
  75.9 19.6 %all-to-all-done.dy_ref = bf16[32,8,8,1024]{3,2,1,0:T(8,128)(2,1)} async-done(((bf16[32,8,8,1024]{3,2,1,0:T(8,128)(2,1)}), bf16[32,8,8,1024]{3,2,1,0:T(8,128)(2,1)}, u32[]{:S(2)}, u32[]{:S(2)}) %all-to-all-start) | async-done | bytes 4194336 | tf_op jit(solution)/shard_map/all_to_all | solution.py:528
  95.5 17.9 %mlp.1 = (bf16[8,256,1024]{2,1,0:T(8,128)(2,1)}, bf16[128,4,640]{2,1,0:T(4,128)(2,1)}) custom-call(bf16[8,256,1024]{2,1,0:T(8,128)(2,1)} %bitcast.23, bf16[32,8,8,1024]{3,2,1,0:T(8,128)(2,1)} %all-to-all-done.dy_ref, bf16[512,256]{1,0:T(8,128)(2,1)} %multiply_bitcast_fusion.w_in_t, bf16[256,512]{1,0:T(8,128)(2,1)} %w_in.1, ...), custom_call_target="tpu_custom_call" | custom-call | tf_op jit(solution)/shard_map/mlp/pallas_call | solution.py:477
  113.4 7.4 %all-to-all-start.1 = ((bf16[128,4,640]{2,1,0:T(4,128)(2,1)}), bf16[128,4,640]{2,1,0:T(4,128)(2,1)S(1)}, u32[]{:S(2)}, u32[]{:S(2)}) async-start(bf16[128,4,640]{2,1,0:T(4,128)(2,1)} %get-tuple-element.16), calls=%async_computation.1 | async-start | bytes 1310720 | tf_op jit(solution)/shard_map/all_to_all | solution.py:546
  120.8 6.5 %copy.29 = bf16[256,8,1024]{2,1,0:T(8,128)(2,1)} copy(bf16[256,8,1024]{2,0,1:T(8,128)(2,1)} %bitcast.25) | data formatting | bytes 8388608
  127.3 8.7 %all-to-all-done.1 = bf16[128,4,640]{2,1,0:T(4,128)(2,1)S(1)} async-done(((bf16[128,4,640]{2,1,0:T(4,128)(2,1)}), bf16[128,4,640]{2,1,0:T(4,128)(2,1)S(1)}, u32[]{:S(2)}, u32[]{:S(2)}) %all-to-all-start.1) | async-done | bytes 655392 | tf_op jit(solution)/shard_map/all_to_all | solution.py:546
  136.4 0.6 slice_multiply_fusion
  137.0 0.7 fusion.10
  137.8 0.7 copy.30
  (27 shorter events, 1.4 us)
Async XLA Ops:
  6.4 22.0 %collective-permute-start.1 = (bf16[17,16,1024]{2,1,0:T(8,128)(2,1)}, bf16[17,16,1024]{2,1,0:T(8,128)(2,1)S(1)}, u32[]{:S(2)}, u32[]{:S(2)}) collective-permute-start(bf16[17,16,1024]{2,1,0:T(8,128)(2,1)} %get-tuple-element.12), channel_id=1, source_target_pairs={{32,0},{64,32},{96,64},{33,1},{65,33},{97,65},{34,2},{66,34},{98,6... | collective-permute-start | bytes 1671176 | tf_op jit(solution)/shard_map/ppermute | solution.py:48
  9.7 18.7 %collective-permute-start = (bf16[17,16,1024]{2,1,0:T(8,128)(2,1)}, bf16[17,16,1024]{2,1,0:T(8,128)(2,1)S(1)}, u32[]{:S(2)}, u32[]{:S(2)}) collective-permute-start(bf16[17,16,1024]{2,1,0:T(8,128)(2,1)} %get-tuple-element.11), channel_id=1, source_target_pairs={{0,32},{32,64},{64,96},{1,33},{33,65},{65,97},{2,34},{34,66},{66,9... | collective-permute-start | bytes 1671176 | tf_op jit(solution)/shard_map/ppermute | solution.py:47
  28.4 0.8 copy-start
  28.4 1.1 copy-start.1
  33.7 61.8 %all-to-all-start = ((bf16[32,8,8,1024]{3,2,1,0:T(8,128)(2,1)}), bf16[32,8,8,1024]{3,2,1,0:T(8,128)(2,1)}, u32[]{:S(2)}, u32[]{:S(2)}) async-start(bf16[32,8,8,1024]{3,2,1,0:T(8,128)(2,1)} %bitcast.24), calls=%async_computation | async-start | bytes 8388608 | tf_op jit(solution)/shard_map/all_to_all | solution.py:528
  42.5 6.6 %copy-start.2 = (bf16[256,512]{1,0:T(8,128)(2,1)S(1)}, bf16[256,512]{1,0:T(8,128)(2,1)}, u32[]{:S(2)}) copy-start(bf16[256,512]{1,0:T(8,128)(2,1)} %w_in.1) | copy-start | bytes 786436
  42.5 6.7 %copy-start.4 = (f32[512]{0:T(512)S(1)}, f32[512]{0:T(512)}, u32[]{:S(2)}) copy-start(f32[512]{0:T(512)} %param.17) | copy-start | bytes 6148
  42.5 8.4 %copy-start.3 = (bf16[512,256]{1,0:T(8,128)(2,1)S(1)}, bf16[512,256]{1,0:T(8,128)(2,1)}, u32[]{:S(2)}) copy-start(bf16[512,256]{1,0:T(8,128)(2,1)} %param.18) | copy-start | bytes 786436
  113.4 22.6 %all-to-all-start.1 = ((bf16[128,4,640]{2,1,0:T(4,128)(2,1)}), bf16[128,4,640]{2,1,0:T(4,128)(2,1)S(1)}, u32[]{:S(2)}, u32[]{:S(2)}) async-start(bf16[128,4,640]{2,1,0:T(4,128)(2,1)} %get-tuple-element.16), calls=%async_computation.1 | async-start | bytes 1310720 | tf_op jit(solution)/shard_map/all_to_all | solution.py:546

commit v3 on v2

--- a/solution.py
+++ b/solution.py
@@ -1,8 +1,8 @@
+import functools
 import math
 
 import jax
 import jax.numpy as jnp
-import numpy as np
 from jax import lax
 from jax.experimental import pallas as pl
 from jax.experimental.pallas import tpu as pltpu
@@ -17,29 +17,32 @@
 BF16 = jnp.bfloat16
 
 
-CUBIC = (
-    (-1.0, 2.0, -1.0, 0.0),
-    (3.0, -5.0, 0.0, 2.0),
-    (-3.0, 4.0, 1.0, 0.0),
-    (1.0, -1.0, 0.0, 0.0),
-    (0.0, -3.0, 4.0, -1.0),
-    (0.0, 9.0, -10.0, 0.0),
-    (0.0, -9.0, 8.0, 1.0),
-    (0.0, 3.0, -2.0, 0.0),
-)
-COL_W, ROW_W, COL_S, ROW_S = 0, 4, 8, 12
-EDGE = 11
-
-
-def catmull(row_frac, col_frac):
-    order = (0, 1, 2, 3, 0, 1, 2, 3, 4, 5, 6, 7, 4, 5, 6, 7)
-    table = np.asarray([CUBIC[k] for k in order], np.float32)[:, :, None, None]
-    on_col = np.asarray([1, 1, 1, 1, 0, 0, 0, 0] * 2, np.bool_)[:, None, None]
-    frac = jnp.where(on_col, col_frac[None], row_frac[None])
+EDGE = 5
+
+
+def weights(frac):
     square = frac * frac
     cube = square * frac
-    value = table[:, 0] * cube + table[:, 1] * square + table[:, 2] * frac + table[:, 3]
-    return lax.reduce_precision(0.5 * value, 8, 7)
+    return (
+        0.5 * (-cube + 2.0 * square - frac),
+        0.5 * (3.0 * cube - 5.0 * square + 2.0),
+        0.5 * (-3.0 * cube + 4.0 * square + frac),
+        0.5 * (cube - square),
+    )
+
+
+def slopes(frac):
+    square = frac * frac
+    return (
+        0.5 * (-3.0 * square + 4.0 * frac - 1.0),
+        0.5 * (9.0 * square - 10.0 * frac),
+        0.5 * (-9.0 * square + 8.0 * frac + 1.0),
+        0.5 * (3.0 * square - 2.0 * frac),
+    )
+
+
+def splat(value):
+    return jnp.full((8, LANES), value, F32)
 
 
 def exchange(head, tail):
@@ -60,11 +63,11 @@
     return lane, lax.broadcasted_iota(jnp.int32, (8, LANES), 0)
 
 
-def col_taps(weights, shift):
+def col_taps(values, shift):
     lane, row = lanes()
     base = jnp.zeros((8, LANES), F32)
     for tap in range(4):
-        base = jnp.where(lane - row == tap, weights[tap], base)
+        base = jnp.where(lane - row == tap, values[tap], base)
     left, right = [], []
     for group in range(0, LANES, 8):
         moved = pltpu.roll(base, (shift + group) & (LANES - 1), 1)
@@ -78,55 +81,85 @@
 REACH = BH + 4
 
 
-def row_taps(weights):
+def row_taps(values):
     lane, row = lanes()
     base = jnp.zeros((8, LANES), F32)
     for tap in range(4):
-        base = jnp.where((lane - BH * row + tap) & (LANES - 1) == 0, weights[tap], base)
+        base = jnp.where((lane - BH * row + tap) & (LANES - 1) == 0, values[tap], base)
     own = lane // BH == row
     moved = [base] + [pltpu.roll(base, step, 1) for step in range(1, REACH)]
     return jnp.concatenate([jnp.where(own, part, 0.0) for part in moved], axis=0).astype(BF16)
 
 
-def pack_body(offs, srow, scol, wgt, *refs):
-    sources, (head_ref, tail_ref) = refs[:4], refs[4:]
-    channels = sources[0].shape[0]
+def pack_body(offs, srow, scol, fracs, cot, adv, head_ref, tail_ref, rows, meta, arrived, left):
+    channels = cot.shape[0]
     last = offs.shape[2] - 1
+    inward, outward = [], []
+    for side, (out_ref, row) in enumerate(((head_ref, 0), (tail_ref, last))):
+        for which, source in enumerate((cot, adv)):
+            job = 2 * side + which
+            inward.append(
+                pltpu.make_async_copy(
+                    source.at[:, row * BH : (row + 1) * BH, :], rows.at[job], arrived.at[job]
+                )
+            )
+            place = slice(which * channels, (which + 1) * channels)
+            outward.append(
+                pltpu.make_async_copy(rows.at[job], out_ref.at[place], left.at[job])
+            )
+    for job in inward:
+        job.start()
     lane = lax.broadcasted_iota(jnp.int32, (BH, LANES), 1)
     for side, (out_ref, row) in enumerate(((head_ref, 0), (tail_ref, last))):
-        out_ref[0:channels] = sources[2 * side][...]
-        out_ref[channels : 2 * channels] = sources[2 * side + 1][...]
         value = jnp.zeros((BH, LANES), F32)
         for block in range(4):
             own = [
                 (BH // 2 * offs[0, block, row] + srow[block, row]).astype(F32),
                 offs[1, block, row].astype(F32),
                 scol[block, row].astype(F32),
+                fracs[0, block, row],
+                fracs[1, block, row],
             ]
-            own = own + [wgt[tap, block, row] for tap in range(8)]
             for slot, entry in enumerate(own):
                 value = jnp.where(lane == block * EDGE + slot, entry, value)
-        out_ref[2 * channels] = jnp.zeros(out_ref.shape[1:], BF16)
-        out_ref[2 * channels, :, 0:LANES] = value.astype(BF16)
+        meta[side] = jnp.zeros(meta.shape[1:], BF16)
+        for part in range(3):
+            high = value.astype(BF16)
+            meta[side, :, part * LANES : (part + 1) * LANES] = high
+            value = value - high.astype(F32)
+        outward.append(
+            pltpu.make_async_copy(meta.at[side], out_ref.at[2 * channels], left.at[4 + side])
+        )
+        outward[-1].start()
+    for job in range(4):
+        inward[job].wait()
+        outward[job].start()
+    for job in outward:
+        job.wait()
 
 
 def pack(places, cot, adv):
     channels, band_rows, columns = cot.shape
-    shape = (2 * channels + 1, BH, columns)
-    first = pl.BlockSpec((channels, BH, columns), lambda g, *a: (0, 0, 0))
-    last = pl.BlockSpec((channels, BH, columns), lambda g, *a: (0, band_rows // BH - 1, 0))
+    shape = jax.ShapeDtypeStruct((2 * channels + 1, BH, columns), BF16)
+    anywhere = pl.BlockSpec(memory_space=pl.ANY)
     return pl.pallas_call(
         pack_body,
         name="pack",
-        out_shape=(jax.ShapeDtypeStruct(shape, BF16),) * 2,
+        out_shape=(shape, shape),
         grid_spec=pltpu.PrefetchScalarGridSpec(
             num_scalar_prefetch=4,
             grid=(1,),
-            in_specs=[first, first, last, last],
-            out_specs=[pl.BlockSpec(shape, lambda g, *a: (0, 0, 0))] * 2,
+            in_specs=[anywhere, anywhere],
+            out_specs=[anywhere, anywhere],
+            scratch_shapes=[
+                pltpu.VMEM((4, channels, BH, columns), BF16),
+                pltpu.VMEM((2, BH, columns), BF16),
+                pltpu.SemaphoreType.DMA((4,)),
+                pltpu.SemaphoreType.DMA((6,)),
+            ],
         ),
         compiler_params=pltpu.CompilerParams(dimension_semantics=("arbitrary",)),
-    )(*places, cot, adv, cot, adv)
+    )(*places, cot, adv)
 
 
 def spread_blocks(jobs, tap_scr, row_scr, z_scr, acc):
@@ -174,7 +207,7 @@
         out_ref[:, tile_index * LANES : (tile_index + 1) * LANES] = done.astype(BF16)
 
 
-def spread_body(offs, srow, scol, wgt, cot_ref, out_ref, edge_ref, tap_scr, row_scr, z_scr, acc):
+def spread_body(offs, srow, scol, fracs, cot_ref, out_ref, edge_ref, tap_scr, row_scr, z_scr, acc):
     step = pl.program_id(0)
     last = pl.num_programs(0) - 1
 
@@ -198,8 +231,8 @@
                         BH // 2 * offs[0, block, row] + srow[block, row],
                         offs[1, block, row],
                         scol[block, row],
-                        [wgt[COL_W + tap, block, row] for tap in range(4)],
-                        [wgt[ROW_W + tap, block, row] for tap in range(4)],
+                        weights(splat(fracs[1, block, row])),
+                        weights(splat(fracs[0, block, row])),
                     )
                 )
         spread_blocks(jobs, tap_scr, row_scr, z_scr, acc)
@@ -264,11 +297,16 @@
         acc[lower + BH :] = jnp.zeros((2 * BH,) + acc.shape[1:], F32)
         jobs = []
         for side, ref in enumerate((top_ref, bot_ref)):
-            rows = ref[...].reshape(LANES, ref.shape[2])
+            rows = ref[0 : LANES // BH].reshape(LANES, ref.shape[2])
             for block in range(4):
-                own = [meta[side, block * EDGE + slot] for slot in range(EDGE)]
-                place = [entry.astype(jnp.int32) for entry in own[:3]]
-                jobs.append((rows, block, side * lower, *place, own[3:7], own[7:11]))
+                at = [block * EDGE + slot for slot in range(EDGE)]
+                place = [meta[side, k].astype(jnp.int32) for k in at[:3]]
+                fracs = [
+                    meta[side, k] + meta[side, LANES + k] + meta[side, 2 * LANES + k]
+                    for k in at[3:]
+                ]
+                wy, wx = [weights(splat(frac)) for frac in fracs]
+                jobs.append((rows, block, side * lower, *place, wx, wy))
         spread_blocks(jobs, tap_scr, row_scr, z_scr, acc)
 
     emit(acc, upper + step * BH, out_ref.at[0])
@@ -285,8 +323,8 @@
             num_scalar_prefetch=1,
             grid=(2,),
             in_specs=[
-                pl.BlockSpec((channels, BH, columns), lambda g, a: (0, 0, 0)),
-                pl.BlockSpec((channels, BH, columns), lambda g, a: (0, 0, 0)),
+                pl.BlockSpec(memory_space=pltpu.VMEM),
+                pl.BlockSpec(memory_space=pltpu.VMEM),
                 pl.BlockSpec(edges.shape, lambda g, a: (0, 0, 0, 0, 0)),
                 pl.BlockSpec(memory_space=pl.ANY),
             ],
@@ -299,7 +337,7 @@
 
 
 def frac_body(
-    offs, srow, scol, wgt, top_ref, mid_ref, next_ref, bot_ref, cot_ref, out_ref, cot_scr, z_scr, field
+    offs, srow, scol, fracs, top_ref, mid_ref, next_ref, bot_ref, cot_ref, out_ref, cot_scr, z_scr, field
 ):
     step = pl.program_id(0)
     last = pl.num_programs(0) - 1
@@ -333,10 +371,11 @@
         py = BH // 2 * offs[0, block, step] + srow[block, step]
         tile = offs[1, block, step]
         shift = scol[block, step]
+        row_frac, col_frac = splat(fracs[0, block, step]), splat(fracs[1, block, step])
         both = jnp.concatenate(
             [
-                col_taps([wgt[COL_W + tap, block, step] for tap in range(4)], shift),
-                col_taps([wgt[COL_S + tap, block, step] for tap in range(4)], shift),
+                col_taps(weights(col_frac), shift),
+                col_taps(slopes(col_frac), shift),
             ],
             axis=1,
         )
@@ -372,9 +411,10 @@
                         by_slope[tap] = by_slope[tap] + value * pair[1][j - tap]
         first = jnp.zeros((8, LANES), F32)
         second = jnp.zeros((8, LANES), F32)
+        wy, sy = weights(row_frac), slopes(row_frac)
         for tap in range(4):
-            first = first + wgt[ROW_S + tap, block, step] * by_value[tap]
-            second = second + wgt[ROW_W + tap, block, step] * by_slope[tap]
+            first = first + sy[tap].astype(BF16).astype(F32) * by_value[tap]
+            second = second + wy[tap].astype(BF16).astype(F32) * by_slope[tap]
         out_ref[0, block] = first
         out_ref[1, block] = second
 
@@ -503,6 +543,39 @@
     )(x, dy, w_in.T * half, w_in, w_out * half, 0.5 * bias[:, None], tail)
 
 
+def finish_body(scale, frac_scale, got_ref, first_ref, second_ref, shift_ref, frac_ref):
+    total = jnp.sum(got_ref[...].astype(F32), axis=0)
+    each = total.shape[0]
+    held = 2 * frac_ref.shape[2]
+    first_ref[...] = total[:, 0:C] * scale
+    second_ref[...] = total[:, C : 2 * C] * scale
+    tail = total[:, 2 * C :]
+    lane = lax.broadcasted_iota(jnp.int32, (each, LANES), 1)
+    row = lax.broadcasted_iota(jnp.int32, (each, LANES), 0)
+    shift = tail[:, 0:1] + tail[:, 1:2]
+    shift = jnp.sum(jnp.where(lane == row, shift, 0.0), axis=0, keepdims=True)
+    shift_ref[...] = shift[:, 0:each] * scale
+    frac = tail[:, held : 2 * held] + tail[:, 2 * held : 3 * held]
+    half = held // 2
+    frac_ref[0] = frac[:, 0:half] * frac_scale
+    frac_ref[1] = frac[:, half:] * frac_scale
+
+
+def finish(got, scale, frac_scale, row_blocks):
+    each = got.shape[1]
+    return pl.pallas_call(
+        functools.partial(finish_body, scale, frac_scale),
+        name="finish",
+        out_shape=(
+            jax.ShapeDtypeStruct((each, C), F32),
+            jax.ShapeDtypeStruct((each, C), F32),
+            jax.ShapeDtypeStruct((1, each), F32),
+            jax.ShapeDtypeStruct((2, each, row_blocks), F32),
+        ),
+        in_specs=[pl.BlockSpec(memory_space=pltpu.VMEM)],
+    )(got)
+
+
 def shards(
     inputs, w_in, bias_in, w_out, advected, cotangent, offsets, stencil_row, stencil_col, fracs
 ):
@@ -512,28 +585,27 @@
     lat = lax.axis_size("lat")
     grp = lax.axis_size("grp")
 
-    fracs = fracs.transpose(0, 2, 1)
     places = (
         offsets.transpose(0, 2, 1),
         stencil_row.T,
         stencil_col.T,
-        catmull(fracs[0], fracs[1]),
+        fracs.transpose(0, 2, 1),
     )
     head, tail = pack(places, cotangent, advected)
     top, bottom = exchange(head, tail)
     dy_band, edges = spread(places, cotangent)
-    meta = jnp.stack([top[2 * channels_dev, 0, :LANES], bottom[2 * channels_dev, 0, :LANES]])
+    meta = jnp.stack([halo[2 * channels_dev, 0, : 3 * LANES] for halo in (top, bottom)])
     dy_band = spread_edges(meta.astype(F32), top, bottom, edges, dy_band)
     dy_send = dy_band.reshape(grp, point_rows, channels_dev, columns)
     dy_points = lax.all_to_all(dy_send, "grp", split_axis=0, concat_axis=0, tiled=True)
 
     frac_parts = frac_sums(places, top, advected, bottom, cotangent)
-    frac_local = jnp.sum(frac_parts, axis=(2, 3)).reshape(-1)
     parts = lat * grp
     each = HID // parts
-    held = frac_local.shape[0] // each
+    held = 2 * row_blocks
+    frac_local = jnp.sum(frac_parts, axis=(2, 3)).reshape(held, columns // BW).T
     high = lax.reduce_precision(frac_local, 8, 7)
-    both = jnp.stack([high.reshape(each, held), (frac_local - high).reshape(each, held)], axis=1)
+    both = jnp.stack([high, frac_local - high], axis=1)
     mine = jnp.where(jnp.arange(lat) == lax.axis_index("lat"), 1.0, 0.0)
     slots = mine[:, None, None, None] * both.reshape(1, 1, each, 2 * held)
     slots = jnp.broadcast_to(slots, (lat, grp, each, 2 * held)).reshape(HID, 2 * held)
@@ -544,14 +616,9 @@
     grad_inputs = dx_rows.transpose(1, 0, 2)
 
     got = lax.all_to_all(send, ("lat", "grp"), split_axis=0, concat_axis=0, tiled=True)
-    total = jnp.sum(got.astype(F32), axis=0)
     scale = 1.0 / math.sqrt(point_rows * columns * parts)
-    grad_first = total[:, :C].T * scale
-    grad_second = total[:, C : 2 * C] * scale
-    grad_shift = (total[:, 2 * C] + total[:, 2 * C + 1]) * scale
-    total = total[:, 2 * C + held : 2 * C + 2 * held] + total[:, 2 * C + 2 * held : 2 * C + 3 * held]
-    grad_frac = total.reshape(2, row_blocks, columns // BW) / math.sqrt(C * BH * BW)
-    return (grad_inputs, grad_first, grad_shift, grad_second, grad_frac)
+    first, second, shift, frac = finish(got, scale, 1.0 / math.sqrt(C * BH * BW), row_blocks)
+    return (grad_inputs, first.T, shift.reshape(each), second, frac.transpose(0, 2, 1))
 
 
 def solution(mesh):

time: 139 us -> 137 us (0.986)
  other arithmetic: 6.98 us -> 3.82 us
    reduce_precision x2 -> x0, other arithmetic: 1.49 us -> none  [the longest x1 1.48 us: catmull(): return lax.reduce_precision(0.5 * value, 8, 7)]
    pallas_call x1 -> x2, Pallas kernels: 3.6 us -> 4.96 us  [the longest x1 2.92 us: pack(): pl.pallas_call(pack_body, name='pack', out_shape=(shape, shape), grid_spe...]
    unnamed x14 -> x15, local copies, waits for them, and re-layouts: 14.3 us -> 14.5 us
  transfers between devices with their start and end apart: 4 -> 4, of which waited for: 2 -> 2; matrix products, arithmetic and copies ran while one was open for 13% -> 14% of each run, Pallas kernels for 26% -> 25%
where the time goes in v3:
time: 137 us; the launch traced here: 136 us
  Pallas kernels  61.9 us (45%)
  waiting for transfers between devices  28.6 us (21%)
  starting transfers between devices  24.4 us (18%)
  local copies, waits for them, and re-layouts  16.5 us (12%)
  other arithmetic  3.82 us (3%)
    pallas_call x1, Pallas kernels, frac_sums(): pl.pallas_call(frac_body, name='frac_sums', out_shape=jax.ShapeDtypeStruc...  21.3 us
    all_to_all x1, waiting for transfers between devices, shards(): lax.all_to_all(dy_send, 'grp', split_axis=0, concat_axis=0, tiled=True)  19.8 us
    pallas_call x1, Pallas kernels, mlp(): pl.pallas_call(mlp_body, name='mlp', out_shape=(jax.ShapeDtypeStruct((row...  17.9 us
    unnamed x15, local copies, waits for them, and re-layouts  14.5 us
    pallas_call x1, Pallas kernels, spread(): pl.pallas_call(spread_body, name='spread', out_shape=(jax.ShapeDtypeStruc...  13.4 us
    all_to_all x1, starting transfers between devices, shards(): lax.all_to_all(dy_send, 'grp', split_axis=0, concat_axis=0, tiled=True)  8.77 us
    all_to_all x1, waiting for transfers between devices, shards(): lax.all_to_all(send, ('lat', 'grp'), split_axis=0, concat_axis=0, tiled=T...  8.71 us
    all_to_all x1, starting transfers between devices, shards(): lax.all_to_all(send, ('lat', 'grp'), split_axis=0, concat_axis=0, tiled=T...  7.55 us
  transfers between devices with their start and end apart: 4, of which 2 were waited for; matrix products, arithmetic and copies ran while one was open for 14% of the time, Pallas kernels for 25%

profile of v3, /device:TPU:1, one launch (start us, length us, event | category | flops | bytes accessed | tf_op | source)
XLA Modules:
  0.0 136.0 jit_solution(2312525249077020620)
XLA Ops:
  0.6 2.9 %pack.1 = (bf16[17,16,1024]{2,1,0:T(8,128)(2,1)}, bf16[17,16,1024]{2,1,0:T(8,128)(2,1)}) custom-call(s32[2,4,16]{2,1,0:T(4,128)} %bitcast.31, s32[4,16]{1,0:T(4,128)} %bitcast.37, s32[4,16]{1,0:T(4,128)} %bitcast.40, f32[2,4,16]{2,1,0:T(4,128)} %bitcast.34, bf16[8,256,1024]{2,1,0:T(8,128)(2,1)} %cot_ref.3, bf16[8,256,1024]{2,1,0:T(8,128)(2,1)} %next_ref.1), custom_call_target="tpu_custom_call" | custom-call | tf_op jit(solution)/shard_map/pack/pallas_call | solution.py:145
  3.6 3.3 %collective-permute-start.1 = (bf16[17,16,1024]{2,1,0:T(8,128)(2,1)}, bf16[17,16,1024]{2,1,0:T(8,128)(2,1)S(1)}, u32[]{:S(2)}, u32[]{:S(2)}) collective-permute-start(bf16[17,16,1024]{2,1,0:T(8,128)(2,1)} %get-tuple-element.16), channel_id=1, source_target_pairs={{32,0},{64,32},{96,64},{33,1},{65,33},{97,65},{34,2},{66,34},{98,6... | collective-permute-start | bytes 1671176 | tf_op jit(solution)/shard_map/ppermute | solution.py:51
  6.9 4.8 %collective-permute-start = (bf16[17,16,1024]{2,1,0:T(8,128)(2,1)}, bf16[17,16,1024]{2,1,0:T(8,128)(2,1)S(1)}, u32[]{:S(2)}, u32[]{:S(2)}) collective-permute-start(bf16[17,16,1024]{2,1,0:T(8,128)(2,1)} %get-tuple-element.15), channel_id=1, source_target_pairs={{0,32},{32,64},{64,96},{1,33},{33,65},{65,97},{2,34},{34,66},{66,9... | collective-permute-start | bytes 1671176 | tf_op jit(solution)/shard_map/ppermute | solution.py:50
  11.7 13.4 %spread.1 = (bf16[16,128,1024]{2,1,0:T(8,128)(2,1)}, f32[2,16,8,8,128]{4,3,2,1,0:T(8,128)}) custom-call(s32[2,4,16]{2,1,0:T(4,128)} %bitcast.32, s32[4,16]{1,0:T(4,128)} %bitcast.38, s32[4,16]{1,0:T(4,128)} %bitcast.41, f32[2,4,16]{2,1,0:T(4,128)} %bitcast.35, bf16[8,256,1024]{2,1,0:T(8,128)(2,1)} %cot_ref.3), custom_call_target="tpu_custom_call" | custom-call | tf_op jit(solution)/shard_map/spread/pallas_call | solution.py:257
  25.1 0.7 maximum_convert_fusion.meta
  25.8 0.1 copy-done.1
  25.9 0.2 copy-done.2
  26.2 4.4 %spread_edges.1 = bf16[16,128,1024]{2,1,0:T(8,128)(2,1)} custom-call(f32[2,384]{1,0:T(2,128)} %maximum_convert_fusion.meta, bf16[17,16,1024]{2,1,0:T(8,128)(2,1)} %copy-done.2, bf16[17,16,1024]{2,1,0:T(8,128)(2,1)} %copy-done.1, f32[2,16,8,8,128]{4,3,2,1,0:T(8,128)} %get-tuple-element.17.edge_ref, ...), custom_call_target="tpu_custom_call", output_to_operand_aliasing={{}: (4, {})} | custom-call | tf_op jit(solution)/shard_map/spread_edges/pallas_call | solution.py:318
  30.6 8.8 %all-to-all-start = ((bf16[32,8,8,1024]{3,2,1,0:T(8,128)(2,1)}), bf16[32,8,8,1024]{3,2,1,0:T(8,128)(2,1)}, u32[]{:S(2)}, u32[]{:S(2)}) async-start(bf16[32,8,8,1024]{3,2,1,0:T(8,128)(2,1)} %bitcast.28), calls=%async_computation | async-start | bytes 8388608 | tf_op jit(solution)/shard_map/all_to_all | solution.py:600
  39.4 6.6 %copy.35 = bf16[256,8,1024]{2,0,1:T(8,128)(2,1)} copy(bf16[256,8,1024]{2,1,0:T(8,128)(2,1)} %param.10) | data formatting | bytes 8388608 | tf_op args[0]
  46.0 0.1 copy.29
  46.1 0.9 copy.32.half_bias
  47.0 0.7 multiply_bitcast_fusion.w_in_t
  47.7 0.7 broadcast_multiply_fusion.w_out
  48.5 21.3 %frac_sums.1 = f32[2,64,8,128]{3,2,1,0:T(8,128)} custom-call(s32[2,4,16]{2,1,0:T(4,128)} %bitcast.33, s32[4,16]{1,0:T(4,128)} %bitcast.39, s32[4,16]{1,0:T(4,128)} %bitcast.42, f32[2,4,16]{2,1,0:T(4,128)} %bitcast.36, bf16[17,16,1024]{2,1,0:T(8,128)(2,1)} %copy-done.2, bf16[8,256,1024]{2,1,0:T(8,128)(2,1)} %next_ref.1, bf16[8,256,1024]{2,1,0:T(8,128)(2,1)} %next_ref.1, ...), custom_call_target="tpu_custom_call" | custom-call | tf_op jit(solution)/shard_map/frac_sums/pallas_call | solution.py:426
  69.7 1.6 %reduce_sum.9 = f32[2,64]{1,0:T(2,128)S(1)} reduce(f32[2,64,8,128]{3,2,1,0:T(8,128)} %frac_sums.1, f32[]{:T(128)} %constant.15.clone.1), dimensions={2,3}, to_apply=%region_0.0 | reduce | flops 130944 | bytes 524804 | tf_op jit(solution)/shard_map/reduce_sum | solution.py:606
  71.7 0.9 pad.4.tail_ref
  72.6 19.8 %all-to-all-done.dy_ref = bf16[32,8,8,1024]{3,2,1,0:T(8,128)(2,1)} async-done(((bf16[32,8,8,1024]{3,2,1,0:T(8,128)(2,1)}), bf16[32,8,8,1024]{3,2,1,0:T(8,128)(2,1)}, u32[]{:S(2)}, u32[]{:S(2)}) %all-to-all-start) | async-done | bytes 4194336 | tf_op jit(solution)/shard_map/all_to_all | solution.py:600
  92.4 17.9 %mlp.1 = (bf16[8,256,1024]{2,1,0:T(8,128)(2,1)}, bf16[128,4,640]{2,1,0:T(4,128)(2,1)}) custom-call(bf16[8,256,1024]{2,1,0:T(8,128)(2,1)} %bitcast.27, bf16[32,8,8,1024]{3,2,1,0:T(8,128)(2,1)} %all-to-all-done.dy_ref, bf16[512,256]{1,0:T(8,128)(2,1)} %multiply_bitcast_fusion.w_in_t, bf16[256,512]{1,0:T(8,128)(2,1)} %w_in.1, ...), custom_call_target="tpu_custom_call" | custom-call | tf_op jit(solution)/shard_map/mlp/pallas_call | solution.py:517
  110.3 7.6 %all-to-all-start.1 = ((bf16[128,4,640]{2,1,0:T(4,128)(2,1)}), bf16[128,4,640]{2,1,0:T(4,128)(2,1)S(1)}, u32[]{:S(2)}, u32[]{:S(2)}) async-start(bf16[128,4,640]{2,1,0:T(4,128)(2,1)} %get-tuple-element.20), calls=%async_computation.1 | async-start | bytes 1310720 | tf_op jit(solution)/shard_map/all_to_all | solution.py:618
  117.9 6.5 %copy.33 = bf16[256,8,1024]{2,1,0:T(8,128)(2,1)} copy(bf16[256,8,1024]{2,0,1:T(8,128)(2,1)} %bitcast.29) | data formatting | bytes 8388608
  124.4 8.7 %all-to-all-done.1.got_ref = bf16[128,4,640]{2,1,0:T(4,128)(2,1)S(1)} async-done(((bf16[128,4,640]{2,1,0:T(4,128)(2,1)}), bf16[128,4,640]{2,1,0:T(4,128)(2,1)S(1)}, u32[]{:S(2)}, u32[]{:S(2)}) %all-to-all-start.1) | async-done | bytes 655392 | tf_op jit(solution)/shard_map/all_to_all | solution.py:618
  133.1 0.8 copy-done
  134.0 2.0 %finish.1 = (f32[4,256]{1,0:T(4,128)}, f32[4,256]{1,0:T(4,128)}, f32[1,4]{1,0:T(1,128)}, f32[2,4,16]{2,1,0:T(4,128)}) custom-call(bf16[128,4,640]{2,1,0:T(4,128)(2,1)} %copy-done), custom_call_target="tpu_custom_call" | custom-call | tf_op jit(solution)/shard_map/finish/pallas_call | solution.py:566
  (23 shorter events, 0.4 us)
Async XLA Ops:
  3.6 21.5 %collective-permute-start.1 = (bf16[17,16,1024]{2,1,0:T(8,128)(2,1)}, bf16[17,16,1024]{2,1,0:T(8,128)(2,1)S(1)}, u32[]{:S(2)}, u32[]{:S(2)}) collective-permute-start(bf16[17,16,1024]{2,1,0:T(8,128)(2,1)} %get-tuple-element.16), channel_id=1, source_target_pairs={{32,0},{64,32},{96,64},{33,1},{65,33},{97,65},{34,2},{66,34},{98,6... | collective-permute-start | bytes 1671176 | tf_op jit(solution)/shard_map/ppermute | solution.py:51
  6.9 18.3 %collective-permute-start = (bf16[17,16,1024]{2,1,0:T(8,128)(2,1)}, bf16[17,16,1024]{2,1,0:T(8,128)(2,1)S(1)}, u32[]{:S(2)}, u32[]{:S(2)}) collective-permute-start(bf16[17,16,1024]{2,1,0:T(8,128)(2,1)} %get-tuple-element.15), channel_id=1, source_target_pairs={{0,32},{32,64},{64,96},{1,33},{33,65},{65,97},{2,34},{34,66},{66,9... | collective-permute-start | bytes 1671176 | tf_op jit(solution)/shard_map/ppermute | solution.py:50
  25.1 0.8 copy-start.1
  25.1 1.0 copy-start.2
  30.6 61.9 %all-to-all-start = ((bf16[32,8,8,1024]{3,2,1,0:T(8,128)(2,1)}), bf16[32,8,8,1024]{3,2,1,0:T(8,128)(2,1)}, u32[]{:S(2)}, u32[]{:S(2)}) async-start(bf16[32,8,8,1024]{3,2,1,0:T(8,128)(2,1)} %bitcast.28), calls=%async_computation | async-start | bytes 8388608 | tf_op jit(solution)/shard_map/all_to_all | solution.py:600
  39.4 6.6 %copy-start.3 = (bf16[256,512]{1,0:T(8,128)(2,1)S(1)}, bf16[256,512]{1,0:T(8,128)(2,1)}, u32[]{:S(2)}) copy-start(bf16[256,512]{1,0:T(8,128)(2,1)} %w_in.1) | copy-start | bytes 786436
  39.4 6.7 %copy-start.5 = (f32[512]{0:T(512)S(1)}, f32[512]{0:T(512)}, u32[]{:S(2)}) copy-start(f32[512]{0:T(512)} %param.12) | copy-start | bytes 6148
  39.4 8.3 %copy-start.4 = (bf16[512,256]{1,0:T(8,128)(2,1)S(1)}, bf16[512,256]{1,0:T(8,128)(2,1)}, u32[]{:S(2)}) copy-start(bf16[512,256]{1,0:T(8,128)(2,1)} %param.13) | copy-start | bytes 786436
  110.3 22.8 %all-to-all-start.1 = ((bf16[128,4,640]{2,1,0:T(4,128)(2,1)}), bf16[128,4,640]{2,1,0:T(4,128)(2,1)S(1)}, u32[]{:S(2)}, u32[]{:S(2)}) async-start(bf16[128,4,640]{2,1,0:T(4,128)(2,1)} %get-tuple-element.20), calls=%async_computation.1 | async-start | bytes 1310720 | tf_op jit(solution)/shard_map/all_to_all | solution.py:618
  133.1 0.8 copy-start

commit v4 on v3

--- a/solution.py
+++ b/solution.py
@@ -448,9 +448,36 @@
     )(*places, top, field, field, bottom, cot)
 
 
+def gate_body(x_ref, w_in_t, half_bias, act_ref, slope_ref):
+    part = 256
+    for at in range(0, x_ref.shape[2], part):
+        x = x_ref[0, :, at : at + part]
+        half = jnp.dot(w_in_t[...], x, preferred_element_type=F32) + half_bias[...]
+        twice = 1.0 + jnp.tanh(half)
+        act = half * twice
+        act_ref[0, :, at : at + part] = act.astype(BF16)
+        slope_ref[0, :, at : at + part] = (twice + act * (2.0 - twice)).astype(BF16)
+
+
+def gate(x, w_in, bias):
+    rows, channels, columns = x.shape
+    whole = lambda shape: pl.BlockSpec(shape, lambda r: (0,) * len(shape))
+    tile = lambda height: pl.BlockSpec((1, height, columns), lambda r: (r, 0, 0))
+    half = jnp.asarray(0.5, BF16)
+    return pl.pallas_call(
+        gate_body,
+        name="gate",
+        out_shape=(jax.ShapeDtypeStruct((rows, HID, columns), BF16),) * 2,
+        grid=(rows,),
+        in_specs=[tile(channels), whole((HID, channels)), whole((HID, 1))],
+        out_specs=[tile(HID), tile(HID)],
+        compiler_params=pltpu.CompilerParams(dimension_semantics=("arbitrary",)),
+    )(x, w_in.T * half, 0.5 * bias[:, None])
+
+
 def mlp_body(
-    x_ref, dy_ref, w_in_t, w_in, w_out, half_bias, tail_ref, dx_ref, send_ref, g_in, g_out, g_bias,
-    act_scr, dpre_scr
+    x_ref, dy_ref, act_ref, slope_ref, w_in, w_out, tail_ref, dx_ref, send_ref, g_in, g_out, g_bias,
+    dpre_scr
 ):
     row = pl.program_id(0)
 
@@ -464,14 +491,9 @@
     points = (((1,), (1,)), ((), ()))
 
     def gates(at):
-        x = x_ref[0, :, at : at + part]
         dy = dy_ref[:, :, at : at + part].reshape(C, part)
-        half = jnp.dot(w_in_t[...], x, preferred_element_type=F32) + half_bias[...]
-        twice = 1.0 + jnp.tanh(half)
-        act = half * twice
         dact = jnp.dot(w_out[...], dy, preferred_element_type=F32)
-        dpre = (dact * (twice + act * (2.0 - twice))).astype(BF16)
-        act_scr[:, at : at + part] = act.astype(BF16)
+        dpre = (dact * slope_ref[0, :, at : at + part].astype(F32)).astype(BF16)
         dpre_scr[:, at : at + part] = dpre
         total = g_bias[...]
         for lane in range(0, part, LANES):
@@ -486,7 +508,7 @@
         dx_ref[0, :, at : at + part] = dx.astype(BF16)
         g_in[...] += lax.dot_general(dpre, x, points, preferred_element_type=F32)
         g_out[...] += lax.dot_general(
-            act_scr[:, at : at + part], dy, points, preferred_element_type=F32
+            act_ref[0, :, at : at + part], dy, points, preferred_element_type=F32
         )
 
     width = x_ref.shape[2]
@@ -507,13 +529,12 @@
         send_ref[...] = send.reshape(parts, each, lanes).astype(BF16)
 
 
-def mlp(x, dy, w_in, bias, w_out, tail, parts):
+def mlp(x, dy, act, slope, w_in, w_out, tail, parts):
     rows, channels, columns = x.shape
     sources = dy.shape[0]
     whole = lambda shape: pl.BlockSpec(shape, lambda r: (0,) * len(shape))
-    tile = pl.BlockSpec((1, channels, columns), lambda r: (r, 0, 0))
+    tile = lambda height: pl.BlockSpec((1, height, columns), lambda r: (r, 0, 0))
     send = (parts, HID // parts, 2 * channels + LANES)
-    half = jnp.asarray(0.5, BF16)
     return pl.pallas_call(
         mlp_body,
         name="mlp",
@@ -523,28 +544,27 @@
         ),
         grid=(rows,),
         in_specs=[
-            tile,
+            tile(channels),
             pl.BlockSpec((sources, None, 8, columns), lambda r: (0, r, 0, 0)),
-            whole((HID, channels)),
+            tile(HID),
+            tile(HID),
             whole((channels, HID)),
             whole((HID, channels)),
-            whole((HID, 1)),
             whole((HID, LANES)),
         ],
-        out_specs=[tile, whole(send)],
+        out_specs=[tile(channels), whole(send)],
         scratch_shapes=[
             pltpu.VMEM((HID, channels), F32),
             pltpu.VMEM((HID, channels), F32),
             pltpu.VMEM((HID, LANES), F32),
             pltpu.VMEM((HID, columns), BF16),
-            pltpu.VMEM((HID, columns), BF16),
         ],
         compiler_params=pltpu.CompilerParams(dimension_semantics=("arbitrary",)),
-    )(x, dy, w_in.T * half, w_in, w_out * half, 0.5 * bias[:, None], tail)
+    )(x, dy, act, slope, w_in, w_out * jnp.asarray(0.5, BF16), tail)
 
 
 def finish_body(scale, frac_scale, got_ref, first_ref, second_ref, shift_ref, frac_ref):
-    total = jnp.sum(got_ref[...].astype(F32), axis=0)
+    total = got_ref[...]
     each = total.shape[0]
     held = 2 * frac_ref.shape[2]
     first_ref[...] = total[:, 0:C] * scale
@@ -562,7 +582,7 @@
 
 
 def finish(got, scale, frac_scale, row_blocks):
-    each = got.shape[1]
+    each = got.shape[0]
     return pl.pallas_call(
         functools.partial(finish_body, scale, frac_scale),
         name="finish",
@@ -612,12 +632,13 @@
     extra = jnp.pad(slots, ((0, 0), (held, LANES - 3 * held)))
 
     x_rows = inputs.transpose(1, 0, 2)
-    dx_rows, send = mlp(x_rows, dy_points, w_in, bias_in, w_out, extra, parts)
+    act, slope = gate(x_rows, w_in, bias_in)
+    dx_rows, send = mlp(x_rows, dy_points, act, slope, w_in, w_out, extra, parts)
     grad_inputs = dx_rows.transpose(1, 0, 2)
 
     got = lax.all_to_all(send, ("lat", "grp"), split_axis=0, concat_axis=0, tiled=True)
     scale = 1.0 / math.sqrt(point_rows * columns * parts)
-    first, second, shift, frac = finish(got, scale, 1.0 / math.sqrt(C * BH * BW), row_blocks)
+    first, second, shift, frac = finish(jnp.sum(got.astype(F32), axis=0), scale, 1.0 / math.sqrt(C * BH * BW), row_blocks)
     return (grad_inputs, first.T, shift.reshape(each), second, frac.transpose(0, 2, 1))
 
 

time: 137 us -> 137 us (level)
  waiting for transfers between devices: 28.6 us -> 16.9 us
  Pallas kernels: 61.9 us -> 71.8 us
  starting transfers between devices: 24.4 us -> 26.5 us
    all_to_all x1, waiting for transfers between devices: 19.8 us -> 8.14 us  [shards(): lax.all_to_all(dy_send, 'grp', split_axis=0, concat_axis=0, tiled=True)]
    pallas_call x0 -> x1, Pallas kernels: none -> 11.3 us  [gate(): pl.pallas_call(gate_body, name='gate', out_shape=(jax.ShapeDtypeStruct((r...]
    all_to_all x1, starting transfers between devices: 7.55 us -> 10.1 us  [shards(): lax.all_to_all(send, ('lat', 'grp'), split_axis=0, concat_axis=0, tiled=T...]
    unnamed x15 -> x13, local copies, waits for them, and re-layouts: 14.5 us -> 13.6 us
  transfers between devices with their start and end apart: 4 -> 4, of which waited for: 2 -> 2; matrix products, arithmetic and copies ran while one was open for 14% -> 13% of each run, Pallas kernels for 25% -> 34%
where the time goes in v4:
time: 137 us; the launch traced here: 136 us
  Pallas kernels  71.8 us (52%)
  starting transfers between devices  26.5 us (19%)
  waiting for transfers between devices  16.9 us (12%)
  local copies, waits for them, and re-layouts  15.6 us (11%)
  other arithmetic  4.74 us (3%)
    pallas_call x1, Pallas kernels, frac_sums(): pl.pallas_call(frac_body, name='frac_sums', out_shape=jax.ShapeDtypeStruc...  21.3 us
    pallas_call x1, Pallas kernels, mlp(): pl.pallas_call(mlp_body, name='mlp', out_shape=(jax.ShapeDtypeStruct((row...  17.1 us
    unnamed x13, local copies, waits for them, and re-layouts  13.6 us
    pallas_call x1, Pallas kernels, spread(): pl.pallas_call(spread_body, name='spread', out_shape=(jax.ShapeDtypeStruc...  13.4 us
    pallas_call x1, Pallas kernels, gate(): pl.pallas_call(gate_body, name='gate', out_shape=(jax.ShapeDtypeStruct((r...  11.3 us
    all_to_all x1, starting transfers between devices, shards(): lax.all_to_all(send, ('lat', 'grp'), split_axis=0, concat_axis=0, tiled=T...  10.1 us
    all_to_all x1, waiting for transfers between devices, shards(): lax.all_to_all(send, ('lat', 'grp'), split_axis=0, concat_axis=0, tiled=T...  8.71 us
    all_to_all x1, starting transfers between devices, shards(): lax.all_to_all(dy_send, 'grp', split_axis=0, concat_axis=0, tiled=True)  8.26 us
  transfers between devices with their start and end apart: 4, of which 2 were waited for; matrix products, arithmetic and copies ran while one was open for 13% of the time, Pallas kernels for 34%

profile of v4, /device:TPU:1, one launch (start us, length us, event | category | flops | bytes accessed | tf_op | source)
XLA Modules:
  0.0 136.3 jit_solution(489058989612027672)
XLA Ops:
  0.6 2.9 %pack.1 = (bf16[17,16,1024]{2,1,0:T(8,128)(2,1)}, bf16[17,16,1024]{2,1,0:T(8,128)(2,1)}) custom-call(s32[2,4,16]{2,1,0:T(4,128)} %bitcast.32, s32[4,16]{1,0:T(4,128)} %bitcast.38, s32[4,16]{1,0:T(4,128)} %bitcast.41, f32[2,4,16]{2,1,0:T(4,128)} %bitcast.35, bf16[8,256,1024]{2,1,0:T(8,128)(2,1)} %cot_ref.3, bf16[8,256,1024]{2,1,0:T(8,128)(2,1)} %next_ref.1), custom_call_target="tpu_custom_call" | custom-call | tf_op jit(solution)/shard_map/pack/pallas_call | solution.py:145
  3.5 6.2 %collective-permute-start = (bf16[17,16,1024]{2,1,0:T(8,128)(2,1)}, bf16[17,16,1024]{2,1,0:T(8,128)(2,1)S(1)}, u32[]{:S(2)}, u32[]{:S(2)}) collective-permute-start(bf16[17,16,1024]{2,1,0:T(8,128)(2,1)} %get-tuple-element.17), channel_id=1, source_target_pairs={{0,32},{32,64},{64,96},{1,33},{33,65},{65,97},{2,34},{34,66},{66,9... | collective-permute-start | bytes 1671176 | tf_op jit(solution)/shard_map/ppermute | solution.py:50
  9.7 1.9 %collective-permute-start.1 = (bf16[17,16,1024]{2,1,0:T(8,128)(2,1)}, bf16[17,16,1024]{2,1,0:T(8,128)(2,1)S(1)}, u32[]{:S(2)}, u32[]{:S(2)}) collective-permute-start(bf16[17,16,1024]{2,1,0:T(8,128)(2,1)} %get-tuple-element.18), channel_id=1, source_target_pairs={{32,0},{64,32},{96,64},{33,1},{65,33},{97,65},{34,2},{66,34},{98,6... | collective-permute-start | bytes 1671176 | tf_op jit(solution)/shard_map/ppermute | solution.py:51
  11.7 13.4 %spread.1 = (bf16[16,128,1024]{2,1,0:T(8,128)(2,1)}, f32[2,16,8,8,128]{4,3,2,1,0:T(8,128)}) custom-call(s32[2,4,16]{2,1,0:T(4,128)} %bitcast.33, s32[4,16]{1,0:T(4,128)} %bitcast.39, s32[4,16]{1,0:T(4,128)} %bitcast.42, f32[2,4,16]{2,1,0:T(4,128)} %bitcast.36, bf16[8,256,1024]{2,1,0:T(8,128)(2,1)} %cot_ref.3), custom_call_target="tpu_custom_call" | custom-call | tf_op jit(solution)/shard_map/spread/pallas_call | solution.py:257
  25.1 0.7 maximum_convert_fusion.meta
  25.8 0.1 copy-done
  25.9 0.2 copy-done.1
  26.2 4.4 %spread_edges.1 = bf16[16,128,1024]{2,1,0:T(8,128)(2,1)} custom-call(f32[2,384]{1,0:T(2,128)} %maximum_convert_fusion.meta, bf16[17,16,1024]{2,1,0:T(8,128)(2,1)} %copy-done, bf16[17,16,1024]{2,1,0:T(8,128)(2,1)} %copy-done.1, f32[2,16,8,8,128]{4,3,2,1,0:T(8,128)} %get-tuple-element.19.edge_ref, ...), custom_call_target="tpu_custom_call", output_to_operand_aliasing={{}: (4, {})} | custom-call | tf_op jit(solution)/shard_map/spread_edges/pallas_call | solution.py:318
  30.5 8.3 %all-to-all-start = ((bf16[32,8,8,1024]{3,2,1,0:T(8,128)(2,1)}), bf16[32,8,8,1024]{3,2,1,0:T(8,128)(2,1)}, u32[]{:S(2)}, u32[]{:S(2)}) async-start(bf16[32,8,8,1024]{3,2,1,0:T(8,128)(2,1)} %bitcast.29), calls=%async_computation | async-start | bytes 8388608 | tf_op jit(solution)/shard_map/all_to_all | solution.py:620
  38.8 0.9 copy.30.half_bias
  39.8 6.5 %copy.35 = bf16[256,8,1024]{2,0,1:T(8,128)(2,1)} copy(bf16[256,8,1024]{2,1,0:T(8,128)(2,1)} %param.10) | data formatting | bytes 8388608 | tf_op args[0]
  46.4 0.7 multiply_bitcast_fusion.w_in_t
  47.1 11.3 %gate.1 = (bf16[8,512,1024]{2,1,0:T(8,128)(2,1)}, bf16[8,512,1024]{2,1,0:T(8,128)(2,1)}) custom-call(bf16[8,256,1024]{2,1,0:T(8,128)(2,1)} %bitcast.27, bf16[512,256]{1,0:T(8,128)(2,1)} %multiply_bitcast_fusion.w_in_t, f32[512,1]{1,0:T(8,128)} %copy.30.half_bias), custom_call_target="tpu_custom_call" | custom-call | tf_op jit(solution)/shard_map/gate/pallas_call | solution.py:467
  58.5 0.7 broadcast_multiply_fusion.w_out
  59.2 21.3 %frac_sums.1 = f32[2,64,8,128]{3,2,1,0:T(8,128)} custom-call(s32[2,4,16]{2,1,0:T(4,128)} %bitcast.34, s32[4,16]{1,0:T(4,128)} %bitcast.40, s32[4,16]{1,0:T(4,128)} %bitcast.43, f32[2,4,16]{2,1,0:T(4,128)} %bitcast.37, bf16[17,16,1024]{2,1,0:T(8,128)(2,1)} %copy-done, bf16[8,256,1024]{2,1,0:T(8,128)(2,1)} %next_ref.1, bf16[8,256,1024]{2,1,0:T(8,128)(2,1)} %next_ref.1, ...), custom_call_target="tpu_custom_call" | custom-call | tf_op jit(solution)/shard_map/frac_sums/pallas_call | solution.py:426
  80.5 1.6 %reduce_sum.18 = f32[2,64]{1,0:T(2,128)S(1)} reduce(f32[2,64,8,128]{3,2,1,0:T(8,128)} %frac_sums.1, f32[]{:T(128)} %constant.15.clone.1), dimensions={2,3}, to_apply=%region_0.0 | reduce | flops 130944 | bytes 524804 | tf_op jit(solution)/shard_map/reduce_sum | solution.py:626
  82.5 0.9 pad.4.tail_ref
  83.3 8.1 %all-to-all-done.dy_ref = bf16[32,8,8,1024]{3,2,1,0:T(8,128)(2,1)} async-done(((bf16[32,8,8,1024]{3,2,1,0:T(8,128)(2,1)}), bf16[32,8,8,1024]{3,2,1,0:T(8,128)(2,1)}, u32[]{:S(2)}, u32[]{:S(2)}) %all-to-all-start) | async-done | bytes 4194336 | tf_op jit(solution)/shard_map/all_to_all | solution.py:620
  91.5 17.1 %mlp.1 = (bf16[8,256,1024]{2,1,0:T(8,128)(2,1)}, bf16[128,4,640]{2,1,0:T(4,128)(2,1)}) custom-call(bf16[8,256,1024]{2,1,0:T(8,128)(2,1)} %bitcast.28, bf16[32,8,8,1024]{3,2,1,0:T(8,128)(2,1)} %all-to-all-done.dy_ref, bf16[8,512,1024]{2,1,0:T(8,128)(2,1)} %get-tuple-element.21.act_ref, bf16[8,512,1024]{2,1,0:T(8,128)(2,1)} %get-tuple-element.22.slope_ref, ...), custom_call_target="tpu_custom_call" | custom-call | tf_op jit(solution)/shard_map/mlp/pallas_call | solution.py:538
  108.6 10.1 %all-to-all-start.1 = ((bf16[128,4,640]{2,1,0:T(4,128)(2,1)}), bf16[128,4,640]{2,1,0:T(4,128)(2,1)S(1)}, u32[]{:S(2)}, u32[]{:S(2)}) async-start(bf16[128,4,640]{2,1,0:T(4,128)(2,1)} %get-tuple-element.24), calls=%async_computation.1 | async-start | bytes 1310720 | tf_op jit(solution)/shard_map/all_to_all | solution.py:639
  118.7 6.5 %copy.33 = bf16[256,8,1024]{2,1,0:T(8,128)(2,1)} copy(bf16[256,8,1024]{2,0,1:T(8,128)(2,1)} %bitcast.30) | data formatting | bytes 8388608
  125.2 8.7 %all-to-all-done.1 = bf16[128,4,640]{2,1,0:T(4,128)(2,1)S(1)} async-done(((bf16[128,4,640]{2,1,0:T(4,128)(2,1)}), bf16[128,4,640]{2,1,0:T(4,128)(2,1)S(1)}, u32[]{:S(2)}, u32[]{:S(2)}) %all-to-all-start.1) | async-done | bytes 655392 | tf_op jit(solution)/shard_map/all_to_all | solution.py:639
  133.9 0.9 convert_reduce_fusion.got_ref
  134.8 1.4 %finish.1 = (f32[4,256]{1,0:T(4,128)}, f32[4,256]{1,0:T(4,128)}, f32[1,4]{1,0:T(1,128)}, f32[2,4,16]{2,1,0:T(4,128)}) custom-call(f32[4,640]{1,0:T(4,128)} %convert_reduce_fusion.got_ref), custom_call_target="tpu_custom_call" | custom-call | tf_op jit(solution)/shard_map/finish/pallas_call | solution.py:586
  (23 shorter events, 0.5 us)
Async XLA Ops:
  3.5 21.5 %collective-permute-start = (bf16[17,16,1024]{2,1,0:T(8,128)(2,1)}, bf16[17,16,1024]{2,1,0:T(8,128)(2,1)S(1)}, u32[]{:S(2)}, u32[]{:S(2)}) collective-permute-start(bf16[17,16,1024]{2,1,0:T(8,128)(2,1)} %get-tuple-element.17), channel_id=1, source_target_pairs={{0,32},{32,64},{64,96},{1,33},{33,65},{65,97},{2,34},{34,66},{66,9... | collective-permute-start | bytes 1671176 | tf_op jit(solution)/shard_map/ppermute | solution.py:50
  9.7 15.3 %collective-permute-start.1 = (bf16[17,16,1024]{2,1,0:T(8,128)(2,1)}, bf16[17,16,1024]{2,1,0:T(8,128)(2,1)S(1)}, u32[]{:S(2)}, u32[]{:S(2)}) collective-permute-start(bf16[17,16,1024]{2,1,0:T(8,128)(2,1)} %get-tuple-element.18), channel_id=1, source_target_pairs={{32,0},{64,32},{96,64},{33,1},{65,33},{97,65},{34,2},{66,34},{98,6... | collective-permute-start | bytes 1671176 | tf_op jit(solution)/shard_map/ppermute | solution.py:51
  25.1 0.8 copy-start
  25.1 1.1 copy-start.1
  30.5 8.3 %copy-start.4 = (f32[512]{0:T(512)S(1)}, f32[512]{0:T(512)}, u32[]{:S(2)}) copy-start(f32[512]{0:T(512)} %param.12) | copy-start | bytes 6148
  30.5 9.2 %copy-start.2 = (bf16[256,512]{1,0:T(8,128)(2,1)S(1)}, bf16[256,512]{1,0:T(8,128)(2,1)}, u32[]{:S(2)}) copy-start(bf16[256,512]{1,0:T(8,128)(2,1)} %w_in.1) | copy-start | bytes 786436
  30.5 60.9 %all-to-all-start = ((bf16[32,8,8,1024]{3,2,1,0:T(8,128)(2,1)}), bf16[32,8,8,1024]{3,2,1,0:T(8,128)(2,1)}, u32[]{:S(2)}, u32[]{:S(2)}) async-start(bf16[32,8,8,1024]{3,2,1,0:T(8,128)(2,1)} %bitcast.29), calls=%async_computation | async-start | bytes 8388608 | tf_op jit(solution)/shard_map/all_to_all | solution.py:620
  46.4 12.1 %copy-start.3 = (bf16[512,256]{1,0:T(8,128)(2,1)S(1)}, bf16[512,256]{1,0:T(8,128)(2,1)}, u32[]{:S(2)}) copy-start(bf16[512,256]{1,0:T(8,128)(2,1)} %param.13) | copy-start | bytes 786436
  108.6 25.4 %all-to-all-start.1 = ((bf16[128,4,640]{2,1,0:T(4,128)(2,1)}), bf16[128,4,640]{2,1,0:T(4,128)(2,1)S(1)}, u32[]{:S(2)}, u32[]{:S(2)}) async-start(bf16[128,4,640]{2,1,0:T(4,128)(2,1)} %get-tuple-element.24), calls=%async_computation.1 | async-start | bytes 1310720 | tf_op jit(solution)/shard_map/all_to_all | solution.py:639

commit v5 on v4

--- a/solution.py
+++ b/solution.py
@@ -323,8 +323,8 @@
             num_scalar_prefetch=1,
             grid=(2,),
             in_specs=[
-                pl.BlockSpec(memory_space=pltpu.VMEM),
-                pl.BlockSpec(memory_space=pltpu.VMEM),
+                pl.BlockSpec((channels, BH, columns), lambda g, a: (0, 0, 0)),
+                pl.BlockSpec((channels, BH, columns), lambda g, a: (0, 0, 0)),
                 pl.BlockSpec(edges.shape, lambda g, a: (0, 0, 0, 0, 0)),
                 pl.BlockSpec(memory_space=pl.ANY),
             ],
@@ -459,29 +459,33 @@
         slope_ref[0, :, at : at + part] = (twice + act * (2.0 - twice)).astype(BF16)
 
 
-def gate(x, w_in, bias):
+def gate(x, half_w_in_t, half_bias):
     rows, channels, columns = x.shape
+    rows = rows // 2
     whole = lambda shape: pl.BlockSpec(shape, lambda r: (0,) * len(shape))
     tile = lambda height: pl.BlockSpec((1, height, columns), lambda r: (r, 0, 0))
-    half = jnp.asarray(0.5, BF16)
     return pl.pallas_call(
         gate_body,
         name="gate",
         out_shape=(jax.ShapeDtypeStruct((rows, HID, columns), BF16),) * 2,
         grid=(rows,),
-        in_specs=[tile(channels), whole((HID, channels)), whole((HID, 1))],
+        in_specs=[
+            pl.BlockSpec((1, channels, columns), lambda r: (2 * r + 1, 0, 0)),
+            whole((HID, channels)),
+            whole((HID, 1)),
+        ],
         out_specs=[tile(HID), tile(HID)],
         compiler_params=pltpu.CompilerParams(dimension_semantics=("arbitrary",)),
-    )(x, w_in.T * half, 0.5 * bias[:, None])
+    )(x, half_w_in_t, half_bias)
 
 
 def mlp_body(
-    x_ref, dy_ref, act_ref, slope_ref, w_in, w_out, tail_ref, dx_ref, send_ref, g_in, g_out, g_bias,
-    dpre_scr
+    x_ref, dy_ref, act_ref, slope_ref, w_in_t, half_bias, w_in, w_out, tail_ref, dx_ref, send_ref,
+    g_in, g_out, g_bias, act_scr, dpre_scr
 ):
-    row = pl.program_id(0)
-
-    @pl.when(row == 0)
+    step = pl.program_id(0)
+
+    @pl.when(step == 0)
     def _():
         g_in[...] = jnp.zeros_like(g_in)
         g_out[...] = jnp.zeros_like(g_out)
@@ -490,35 +494,49 @@
     part = 256
     points = (((1,), (1,)), ((), ()))
 
-    def gates(at):
-        dy = dy_ref[:, :, at : at + part].reshape(C, part)
-        dact = jnp.dot(w_out[...], dy, preferred_element_type=F32)
-        dpre = (dact * slope_ref[0, :, at : at + part].astype(F32)).astype(BF16)
-        dpre_scr[:, at : at + part] = dpre
+    def field(item):
+        row, cut = item
+        return dy_ref[:, row, :, cut].reshape(C, part)
+
+    def gates(item, slot):
+        row, cut = item
+        if row == 0:
+            half = jnp.dot(w_in_t[...], x_ref[0, :, cut], preferred_element_type=F32)
+            half = half + half_bias[...]
+            twice = 1.0 + jnp.tanh(half)
+            act = half * twice
+            act_scr[slot] = act.astype(BF16)
+            slope = twice + act * (2.0 - twice)
+        else:
+            slope = slope_ref[0, :, cut].astype(F32)
+        dact = jnp.dot(w_out[...], field(item), preferred_element_type=F32)
+        dpre = (dact * slope).astype(BF16)
+        dpre_scr[slot] = dpre
         total = g_bias[...]
         for lane in range(0, part, LANES):
             total = total + dpre[:, lane : lane + LANES].astype(F32)
         g_bias[...] = total
 
-    def products(at):
-        x = x_ref[0, :, at : at + part]
-        dy = dy_ref[:, :, at : at + part].reshape(C, part)
-        dpre = dpre_scr[:, at : at + part]
+    def products(item, slot):
+        row, cut = item
+        dy = field(item)
+        dpre = dpre_scr[slot]
         dx = dy.astype(F32) + jnp.dot(w_in[...], dpre, preferred_element_type=F32)
-        dx_ref[0, :, at : at + part] = dx.astype(BF16)
-        g_in[...] += lax.dot_general(dpre, x, points, preferred_element_type=F32)
-        g_out[...] += lax.dot_general(
-            act_ref[0, :, at : at + part], dy, points, preferred_element_type=F32
-        )
-
-    width = x_ref.shape[2]
-    gates(0)
-    for at in range(part, width, part):
-        gates(at)
-        products(at - part)
-    products(width - part)
-
-    @pl.when(row == pl.num_programs(0) - 1)
+        dx_ref[row, :, cut] = dx.astype(BF16)
+        g_in[...] += lax.dot_general(dpre, x_ref[row, :, cut], points, preferred_element_type=F32)
+        act = act_scr[slot] if row == 0 else act_ref[0, :, cut]
+        g_out[...] += lax.dot_general(act, dy, points, preferred_element_type=F32)
+
+    items = []
+    for at in range(0, x_ref.shape[2], part):
+        items.extend([(0, slice(at, at + part)), (1, slice(at, at + part))])
+    gates(items[0], 0)
+    for index in range(1, len(items)):
+        gates(items[index], index % 3)
+        products(items[index - 1], (index - 1) % 3)
+    products(items[-1], (len(items) - 1) % 3)
+
+    @pl.when(step == pl.num_programs(0) - 1)
     def _():
         parts, each, lanes = send_ref.shape
         shift = jnp.sum(g_bias[...], axis=1, keepdims=True)
@@ -529,11 +547,12 @@
         send_ref[...] = send.reshape(parts, each, lanes).astype(BF16)
 
 
-def mlp(x, dy, act, slope, w_in, w_out, tail, parts):
+def mlp(x, dy, act, slope, half_w_in_t, half_bias, w_in, w_out, tail, parts):
     rows, channels, columns = x.shape
     sources = dy.shape[0]
     whole = lambda shape: pl.BlockSpec(shape, lambda r: (0,) * len(shape))
-    tile = lambda height: pl.BlockSpec((1, height, columns), lambda r: (r, 0, 0))
+    pair = pl.BlockSpec((2, channels, columns), lambda r: (r, 0, 0))
+    ready = pl.BlockSpec((1, HID, columns), lambda r: (r, 0, 0))
     send = (parts, HID // parts, 2 * channels + LANES)
     return pl.pallas_call(
         mlp_body,
@@ -542,25 +561,28 @@
             jax.ShapeDtypeStruct((rows, channels, columns), BF16),
             jax.ShapeDtypeStruct(send, BF16),
         ),
-        grid=(rows,),
+        grid=(rows // 2,),
         in_specs=[
-            tile(channels),
-            pl.BlockSpec((sources, None, 8, columns), lambda r: (0, r, 0, 0)),
-            tile(HID),
-            tile(HID),
+            pair,
+            pl.BlockSpec((sources, 2, 8, columns), lambda r: (0, r, 0, 0)),
+            ready,
+            ready,
+            whole((HID, channels)),
+            whole((HID, 1)),
             whole((channels, HID)),
             whole((HID, channels)),
             whole((HID, LANES)),
         ],
-        out_specs=[tile(channels), whole(send)],
+        out_specs=[pair, whole(send)],
         scratch_shapes=[
             pltpu.VMEM((HID, channels), F32),
             pltpu.VMEM((HID, channels), F32),
             pltpu.VMEM((HID, LANES), F32),
-            pltpu.VMEM((HID, columns), BF16),
+            pltpu.VMEM((3, HID, 256), BF16),
+            pltpu.VMEM((3, HID, 256), BF16),
         ],
         compiler_params=pltpu.CompilerParams(dimension_semantics=("arbitrary",)),
-    )(x, dy, act, slope, w_in, w_out * jnp.asarray(0.5, BF16), tail)
+    )(x, dy, act, slope, half_w_in_t, half_bias, w_in, w_out * jnp.asarray(0.5, BF16), tail)
 
 
 def finish_body(scale, frac_scale, got_ref, first_ref, second_ref, shift_ref, frac_ref):
@@ -632,8 +654,12 @@
     extra = jnp.pad(slots, ((0, 0), (held, LANES - 3 * held)))
 
     x_rows = inputs.transpose(1, 0, 2)
-    act, slope = gate(x_rows, w_in, bias_in)
-    dx_rows, send = mlp(x_rows, dy_points, act, slope, w_in, w_out, extra, parts)
+    half_w_in_t = w_in.T * jnp.asarray(0.5, BF16)
+    half_bias = 0.5 * bias_in[:, None]
+    act, slope = gate(x_rows, half_w_in_t, half_bias)
+    dx_rows, send = mlp(
+        x_rows, dy_points, act, slope, half_w_in_t, half_bias, w_in, w_out, extra, parts
+    )
     grad_inputs = dx_rows.transpose(1, 0, 2)
 
     got = lax.all_to_all(send, ("lat", "grp"), split_axis=0, concat_axis=0, tiled=True)

time: 137 us -> 136 us (level)
  Pallas kernels: 71.8 us -> 65.8 us
  waiting for transfers between devices: 16.9 us -> 21.5 us
    all_to_all x1, waiting for transfers between devices: 8.14 us -> 12.8 us  [shards(): lax.all_to_all(dy_send, 'grp', split_axis=0, concat_axis=0, tiled=True)]
    pallas_call x1, Pallas kernels: 11.3 us -> 6.74 us  [gate(): pl.pallas_call(gate_body, name='gate', out_shape=(jax.ShapeDtypeStruct((r...]
  transfers between devices with their start and end apart: 4 -> 4, of which waited for: 2 -> 2; matrix products, arithmetic and copies ran while one was open for 13% -> 14% of each run, Pallas kernels for 34% -> 31%
where the time goes in v5:
time: 136 us; the launch traced here: 135 us
  Pallas kernels  65.8 us (48%)
  starting transfers between devices  26.5 us (19%)
  waiting for transfers between devices  21.5 us (16%)
  local copies, waits for them, and re-layouts  15.5 us (11%)
  other arithmetic  4.73 us (3%)
    pallas_call x1, Pallas kernels, frac_sums(): pl.pallas_call(frac_body, name='frac_sums', out_shape=jax.ShapeDtypeStruc...  21.3 us
    pallas_call x1, Pallas kernels, mlp(): pl.pallas_call(mlp_body, name='mlp', out_shape=(jax.ShapeDtypeStruct((row...  15.9 us
    unnamed x13, local copies, waits for them, and re-layouts  13.5 us
    pallas_call x1, Pallas kernels, spread(): pl.pallas_call(spread_body, name='spread', out_shape=(jax.ShapeDtypeStruc...  13.4 us
    all_to_all x1, waiting for transfers between devices, shards(): lax.all_to_all(dy_send, 'grp', split_axis=0, concat_axis=0, tiled=True)  12.8 us
    all_to_all x1, starting transfers between devices, shards(): lax.all_to_all(send, ('lat', 'grp'), split_axis=0, concat_axis=0, tiled=T...  10.1 us
    all_to_all x1, waiting for transfers between devices, shards(): lax.all_to_all(send, ('lat', 'grp'), split_axis=0, concat_axis=0, tiled=T...  8.72 us
    all_to_all x1, starting transfers between devices, shards(): lax.all_to_all(dy_send, 'grp', split_axis=0, concat_axis=0, tiled=True)  8.26 us
  transfers between devices with their start and end apart: 4, of which 2 were waited for; matrix products, arithmetic and copies ran while one was open for 14% of the time, Pallas kernels for 31%

profile of v5, /device:TPU:1, one launch (start us, length us, event | category | flops | bytes accessed | tf_op | source)
XLA Modules:
  0.0 134.8 jit_solution(3222032172686814194)
XLA Ops:
  0.6 2.9 %pack.1 = (bf16[17,16,1024]{2,1,0:T(8,128)(2,1)}, bf16[17,16,1024]{2,1,0:T(8,128)(2,1)}) custom-call(s32[2,4,16]{2,1,0:T(4,128)} %bitcast.32, s32[4,16]{1,0:T(4,128)} %bitcast.38, s32[4,16]{1,0:T(4,128)} %bitcast.41, f32[2,4,16]{2,1,0:T(4,128)} %bitcast.35, bf16[8,256,1024]{2,1,0:T(8,128)(2,1)} %cot_ref.3, bf16[8,256,1024]{2,1,0:T(8,128)(2,1)} %next_ref.1), custom_call_target="tpu_custom_call" | custom-call | tf_op jit(solution)/shard_map/pack/pallas_call | solution.py:145
  3.5 6.2 %collective-permute-start = (bf16[17,16,1024]{2,1,0:T(8,128)(2,1)}, bf16[17,16,1024]{2,1,0:T(8,128)(2,1)S(1)}, u32[]{:S(2)}, u32[]{:S(2)}) collective-permute-start(bf16[17,16,1024]{2,1,0:T(8,128)(2,1)} %get-tuple-element.17), channel_id=1, source_target_pairs={{0,32},{32,64},{64,96},{1,33},{33,65},{65,97},{2,34},{34,66},{66,9... | collective-permute-start | bytes 1671176 | tf_op jit(solution)/shard_map/ppermute | solution.py:50
  9.7 1.9 %collective-permute-start.1 = (bf16[17,16,1024]{2,1,0:T(8,128)(2,1)}, bf16[17,16,1024]{2,1,0:T(8,128)(2,1)S(1)}, u32[]{:S(2)}, u32[]{:S(2)}) collective-permute-start(bf16[17,16,1024]{2,1,0:T(8,128)(2,1)} %get-tuple-element.18), channel_id=1, source_target_pairs={{32,0},{64,32},{96,64},{33,1},{65,33},{97,65},{34,2},{66,34},{98,6... | collective-permute-start | bytes 1671176 | tf_op jit(solution)/shard_map/ppermute | solution.py:51
  11.7 13.4 %spread.1 = (bf16[16,128,1024]{2,1,0:T(8,128)(2,1)}, f32[2,16,8,8,128]{4,3,2,1,0:T(8,128)}) custom-call(s32[2,4,16]{2,1,0:T(4,128)} %bitcast.33, s32[4,16]{1,0:T(4,128)} %bitcast.39, s32[4,16]{1,0:T(4,128)} %bitcast.42, f32[2,4,16]{2,1,0:T(4,128)} %bitcast.36, bf16[8,256,1024]{2,1,0:T(8,128)(2,1)} %cot_ref.3), custom_call_target="tpu_custom_call" | custom-call | tf_op jit(solution)/shard_map/spread/pallas_call | solution.py:257
  25.1 0.7 maximum_convert_fusion.meta
  25.9 0.2 copy-done.1
  26.1 4.2 %spread_edges.1 = bf16[16,128,1024]{2,1,0:T(8,128)(2,1)} custom-call(f32[2,384]{1,0:T(2,128)} %maximum_convert_fusion.meta, bf16[17,16,1024]{2,1,0:T(8,128)(2,1)} %copy-done, bf16[17,16,1024]{2,1,0:T(8,128)(2,1)} %copy-done.1, f32[2,16,8,8,128]{4,3,2,1,0:T(8,128)} %get-tuple-element.19.edge_ref, ...), custom_call_target="tpu_custom_call", output_to_operand_aliasing={{}: (4, {})} | custom-call | tf_op jit(solution)/shard_map/spread_edges/pallas_call | solution.py:318
  30.3 8.3 %all-to-all-start = ((bf16[32,8,8,1024]{3,2,1,0:T(8,128)(2,1)}), bf16[32,8,8,1024]{3,2,1,0:T(8,128)(2,1)}, u32[]{:S(2)}, u32[]{:S(2)}) async-start(bf16[32,8,8,1024]{3,2,1,0:T(8,128)(2,1)} %bitcast.29), calls=%async_computation | async-start | bytes 8388608 | tf_op jit(solution)/shard_map/all_to_all | solution.py:642
  38.6 0.9 copy.31.half_bias
  39.4 0.1 copy.30
  39.6 6.5 %copy.37 = bf16[256,8,1024]{2,0,1:T(8,128)(2,1)} copy(bf16[256,8,1024]{2,1,0:T(8,128)(2,1)} %param.10) | data formatting | bytes 8388608 | tf_op args[0]
  46.1 0.7 multiply_bitcast_fusion.w_in_t
  46.8 6.7 %gate.1 = (bf16[4,512,1024]{2,1,0:T(8,128)(2,1)}, bf16[4,512,1024]{2,1,0:T(8,128)(2,1)}) custom-call(bf16[8,256,1024]{2,1,0:T(8,128)(2,1)} %bitcast.27, bf16[512,256]{1,0:T(8,128)(2,1)} %multiply_bitcast_fusion.w_in_t, f32[512,1]{1,0:T(8,128)} %copy.31.half_bias), custom_call_target="tpu_custom_call" | custom-call | tf_op jit(solution)/shard_map/gate/pallas_call | solution.py:467
  53.6 0.7 broadcast_multiply_fusion.w_out
  54.3 21.3 %frac_sums.1 = f32[2,64,8,128]{3,2,1,0:T(8,128)} custom-call(s32[2,4,16]{2,1,0:T(4,128)} %bitcast.34, s32[4,16]{1,0:T(4,128)} %bitcast.40, s32[4,16]{1,0:T(4,128)} %bitcast.43, f32[2,4,16]{2,1,0:T(4,128)} %bitcast.37, bf16[17,16,1024]{2,1,0:T(8,128)(2,1)} %copy-done, bf16[8,256,1024]{2,1,0:T(8,128)(2,1)} %next_ref.1, bf16[8,256,1024]{2,1,0:T(8,128)(2,1)} %next_ref.1, ...), custom_call_target="tpu_custom_call" | custom-call | tf_op jit(solution)/shard_map/frac_sums/pallas_call | solution.py:426
  75.6 1.6 %reduce_sum.18 = f32[2,64]{1,0:T(2,128)S(1)} reduce(f32[2,64,8,128]{3,2,1,0:T(8,128)} %frac_sums.1, f32[]{:T(128)} %constant.15.clone.1), dimensions={2,3}, to_apply=%region_0.0 | reduce | flops 130944 | bytes 524804 | tf_op jit(solution)/shard_map/reduce_sum | solution.py:648
  77.6 0.8 pad.4.tail_ref
  78.4 12.8 %all-to-all-done.dy_ref = bf16[32,8,8,1024]{3,2,1,0:T(8,128)(2,1)} async-done(((bf16[32,8,8,1024]{3,2,1,0:T(8,128)(2,1)}), bf16[32,8,8,1024]{3,2,1,0:T(8,128)(2,1)}, u32[]{:S(2)}, u32[]{:S(2)}) %all-to-all-start) | async-done | bytes 4194336 | tf_op jit(solution)/shard_map/all_to_all | solution.py:642
  91.2 15.9 %mlp.1 = (bf16[8,256,1024]{2,1,0:T(8,128)(2,1)}, bf16[128,4,640]{2,1,0:T(4,128)(2,1)}) custom-call(bf16[8,256,1024]{2,1,0:T(8,128)(2,1)} %bitcast.28, bf16[32,8,8,1024]{3,2,1,0:T(8,128)(2,1)} %all-to-all-done.dy_ref, bf16[4,512,1024]{2,1,0:T(8,128)(2,1)} %get-tuple-element.21.act_ref, bf16[4,512,1024]{2,1,0:T(8,128)(2,1)} %get-tuple-element.22.slope_ref, ...), custom_call_target="tpu_custom_call" | custom-call | tf_op jit(solution)/shard_map/mlp/pallas_call | solution.py:557
  107.1 10.1 %all-to-all-start.1 = ((bf16[128,4,640]{2,1,0:T(4,128)(2,1)}), bf16[128,4,640]{2,1,0:T(4,128)(2,1)S(1)}, u32[]{:S(2)}, u32[]{:S(2)}) async-start(bf16[128,4,640]{2,1,0:T(4,128)(2,1)} %get-tuple-element.24), calls=%async_computation.1 | async-start | bytes 1310720 | tf_op jit(solution)/shard_map/all_to_all | solution.py:665
  117.2 6.5 %copy.35 = bf16[256,8,1024]{2,1,0:T(8,128)(2,1)} copy(bf16[256,8,1024]{2,0,1:T(8,128)(2,1)} %bitcast.30) | data formatting | bytes 8388608
  123.8 8.7 %all-to-all-done.1 = bf16[128,4,640]{2,1,0:T(4,128)(2,1)S(1)} async-done(((bf16[128,4,640]{2,1,0:T(4,128)(2,1)}), bf16[128,4,640]{2,1,0:T(4,128)(2,1)S(1)}, u32[]{:S(2)}, u32[]{:S(2)}) %all-to-all-start.1) | async-done | bytes 655392 | tf_op jit(solution)/shard_map/all_to_all | solution.py:665
  132.5 0.9 convert_reduce_fusion.got_ref
  133.4 1.4 %finish.1 = (f32[4,256]{1,0:T(4,128)}, f32[4,256]{1,0:T(4,128)}, f32[1,4]{1,0:T(1,128)}, f32[2,4,16]{2,1,0:T(4,128)}) custom-call(f32[4,640]{1,0:T(4,128)} %convert_reduce_fusion.got_ref), custom_call_target="tpu_custom_call" | custom-call | tf_op jit(solution)/shard_map/finish/pallas_call | solution.py:608
  (23 shorter events, 0.5 us)
Async XLA Ops:
  3.5 21.5 %collective-permute-start = (bf16[17,16,1024]{2,1,0:T(8,128)(2,1)}, bf16[17,16,1024]{2,1,0:T(8,128)(2,1)S(1)}, u32[]{:S(2)}, u32[]{:S(2)}) collective-permute-start(bf16[17,16,1024]{2,1,0:T(8,128)(2,1)} %get-tuple-element.17), channel_id=1, source_target_pairs={{0,32},{32,64},{64,96},{1,33},{33,65},{65,97},{2,34},{34,66},{66,9... | collective-permute-start | bytes 1671176 | tf_op jit(solution)/shard_map/ppermute | solution.py:50
  9.7 15.3 %collective-permute-start.1 = (bf16[17,16,1024]{2,1,0:T(8,128)(2,1)}, bf16[17,16,1024]{2,1,0:T(8,128)(2,1)S(1)}, u32[]{:S(2)}, u32[]{:S(2)}) collective-permute-start(bf16[17,16,1024]{2,1,0:T(8,128)(2,1)} %get-tuple-element.18), channel_id=1, source_target_pairs={{32,0},{64,32},{96,64},{33,1},{65,33},{97,65},{34,2},{66,34},{98,6... | collective-permute-start | bytes 1671176 | tf_op jit(solution)/shard_map/ppermute | solution.py:51
  25.0 0.8 copy-start
  25.1 1.0 copy-start.1
  30.3 8.3 %copy-start.4 = (f32[512]{0:T(512)S(1)}, f32[512]{0:T(512)}, u32[]{:S(2)}) copy-start(f32[512]{0:T(512)} %param.12) | copy-start | bytes 6148
  30.3 9.2 %copy-start.2 = (bf16[256,512]{1,0:T(8,128)(2,1)S(1)}, bf16[256,512]{1,0:T(8,128)(2,1)}, u32[]{:S(2)}) copy-start(bf16[256,512]{1,0:T(8,128)(2,1)} %w_in.1) | copy-start | bytes 786436
  30.3 60.9 %all-to-all-start = ((bf16[32,8,8,1024]{3,2,1,0:T(8,128)(2,1)}), bf16[32,8,8,1024]{3,2,1,0:T(8,128)(2,1)}, u32[]{:S(2)}, u32[]{:S(2)}) async-start(bf16[32,8,8,1024]{3,2,1,0:T(8,128)(2,1)} %bitcast.29), calls=%async_computation | async-start | bytes 8388608 | tf_op jit(solution)/shard_map/all_to_all | solution.py:642
  46.1 7.5 %copy-start.3 = (bf16[512,256]{1,0:T(8,128)(2,1)S(1)}, bf16[512,256]{1,0:T(8,128)(2,1)}, u32[]{:S(2)}) copy-start(bf16[512,256]{1,0:T(8,128)(2,1)} %param.13) | copy-start | bytes 786436
  107.1 25.4 %all-to-all-start.1 = ((bf16[128,4,640]{2,1,0:T(4,128)(2,1)}), bf16[128,4,640]{2,1,0:T(4,128)(2,1)S(1)}, u32[]{:S(2)}, u32[]{:S(2)}) async-start(bf16[128,4,640]{2,1,0:T(4,128)(2,1)} %get-tuple-element.24), calls=%async_computation.1 | async-start | bytes 1310720 | tf_op jit(solution)/shard_map/all_to_all | solution.py:665

commit v6 on v5

--- a/solution.py
+++ b/solution.py
@@ -7,6 +7,7 @@
 from jax.experimental import pallas as pl
 from jax.experimental.pallas import tpu as pltpu
 from jax.sharding import PartitionSpec as P
+
 
 C = 256
 BH = 16
@@ -47,8 +48,8 @@
 
 def exchange(head, tail):
     count = lax.axis_size("lat")
+    below = lax.ppermute(head, "lat", [(i + 1, i) for i in range(count - 1)])
     above = lax.ppermute(tail, "lat", [(i, i + 1) for i in range(count - 1)])
-    below = lax.ppermute(head, "lat", [(i + 1, i) for i in range(count - 1)])
     return above, below
 
 
@@ -139,7 +140,7 @@
 
 
 def pack(places, cot, adv):
-    channels, band_rows, columns = cot.shape
+    channels, _, columns = cot.shape
     shape = jax.ShapeDtypeStruct((2 * channels + 1, BH, columns), BF16)
     anywhere = pl.BlockSpec(memory_space=pl.ANY)
     return pl.pallas_call(
@@ -387,8 +388,8 @@
             axis=0,
         )
         z_scr[block] = jnp.dot(halves, both, preferred_element_type=F32)
-        by_value = [jnp.zeros((8, LANES), F32) for tap in range(4)]
-        by_slope = [jnp.zeros((8, LANES), F32) for tap in range(4)]
+        by_value = [jnp.zeros((8, LANES), F32) for _ in range(4)]
+        by_slope = [jnp.zeros((8, LANES), F32) for _ in range(4)]
         for part in range(3):
             pair = []
             for lane in (0, 2 * LANES):

time: 136 us -> 136 us (level)
  no operation moved by 1% of the time
where the time goes in v6:
time: 136 us; the launch traced here: 135 us
  Pallas kernels  65.9 us (48%)
  starting transfers between devices  26.4 us (19%)
  waiting for transfers between devices  21.5 us (16%)
  local copies, waits for them, and re-layouts  15.5 us (11%)
  other arithmetic  4.73 us (3%)
    pallas_call x1, Pallas kernels, frac_sums(): pl.pallas_call(frac_body, name='frac_sums', out_shape=jax.ShapeDtypeStruc...  21.3 us
    pallas_call x1, Pallas kernels, mlp(): pl.pallas_call(mlp_body, name='mlp', out_shape=(jax.ShapeDtypeStruct((row...  15.9 us
    unnamed x13, local copies, waits for them, and re-layouts  13.5 us
    pallas_call x1, Pallas kernels, spread(): pl.pallas_call(spread_body, name='spread', out_shape=(jax.ShapeDtypeStruc...  13.4 us
    all_to_all x1, waiting for transfers between devices, shards(): lax.all_to_all(dy_send, 'grp', split_axis=0, concat_axis=0, tiled=True)  12.8 us
    all_to_all x1, starting transfers between devices, shards(): lax.all_to_all(send, ('lat', 'grp'), split_axis=0, concat_axis=0, tiled=T...  10.1 us
    all_to_all x1, waiting for transfers between devices, shards(): lax.all_to_all(send, ('lat', 'grp'), split_axis=0, concat_axis=0, tiled=T...  8.72 us
    all_to_all x1, starting transfers between devices, shards(): lax.all_to_all(dy_send, 'grp', split_axis=0, concat_axis=0, tiled=True)  8.26 us
  transfers between devices with their start and end apart: 4, of which 2 were waited for; matrix products, arithmetic and copies ran while one was open for 14% of the time, Pallas kernels for 31%

profile of v6, /device:TPU:1, one launch (start us, length us, event | category | flops | bytes accessed | tf_op | source)
XLA Modules:
  0.0 134.9 jit_solution(3222032172686814194)
XLA Ops:
  0.6 2.9 %pack.1 = (bf16[17,16,1024]{2,1,0:T(8,128)(2,1)}, bf16[17,16,1024]{2,1,0:T(8,128)(2,1)}) custom-call(s32[2,4,16]{2,1,0:T(4,128)} %bitcast.32, s32[4,16]{1,0:T(4,128)} %bitcast.38, s32[4,16]{1,0:T(4,128)} %bitcast.41, f32[2,4,16]{2,1,0:T(4,128)} %bitcast.35, bf16[8,256,1024]{2,1,0:T(8,128)(2,1)} %cot_ref.3, bf16[8,256,1024]{2,1,0:T(8,128)(2,1)} %next_ref.1), custom_call_target="tpu_custom_call" | custom-call | tf_op jit(solution)/shard_map/pack/pallas_call | solution.py:146
  3.5 6.2 %collective-permute-start = (bf16[17,16,1024]{2,1,0:T(8,128)(2,1)}, bf16[17,16,1024]{2,1,0:T(8,128)(2,1)S(1)}, u32[]{:S(2)}, u32[]{:S(2)}) collective-permute-start(bf16[17,16,1024]{2,1,0:T(8,128)(2,1)} %get-tuple-element.17), channel_id=1, source_target_pairs={{0,32},{32,64},{64,96},{1,33},{33,65},{65,97},{2,34},{34,66},{66,9... | collective-permute-start | bytes 1671176 | tf_op jit(solution)/shard_map/ppermute | solution.py:52
  9.7 1.9 %collective-permute-start.1 = (bf16[17,16,1024]{2,1,0:T(8,128)(2,1)}, bf16[17,16,1024]{2,1,0:T(8,128)(2,1)S(1)}, u32[]{:S(2)}, u32[]{:S(2)}) collective-permute-start(bf16[17,16,1024]{2,1,0:T(8,128)(2,1)} %get-tuple-element.18), channel_id=1, source_target_pairs={{32,0},{64,32},{96,64},{33,1},{65,33},{97,65},{34,2},{66,34},{98,6... | collective-permute-start | bytes 1671176 | tf_op jit(solution)/shard_map/ppermute | solution.py:51
  11.7 13.4 %spread.1 = (bf16[16,128,1024]{2,1,0:T(8,128)(2,1)}, f32[2,16,8,8,128]{4,3,2,1,0:T(8,128)}) custom-call(s32[2,4,16]{2,1,0:T(4,128)} %bitcast.33, s32[4,16]{1,0:T(4,128)} %bitcast.39, s32[4,16]{1,0:T(4,128)} %bitcast.42, f32[2,4,16]{2,1,0:T(4,128)} %bitcast.36, bf16[8,256,1024]{2,1,0:T(8,128)(2,1)} %cot_ref.3), custom_call_target="tpu_custom_call" | custom-call | tf_op jit(solution)/shard_map/spread/pallas_call | solution.py:258
  25.1 0.7 maximum_convert_fusion.meta
  25.9 0.2 copy-done.1
  26.1 4.2 %spread_edges.1 = bf16[16,128,1024]{2,1,0:T(8,128)(2,1)} custom-call(f32[2,384]{1,0:T(2,128)} %maximum_convert_fusion.meta, bf16[17,16,1024]{2,1,0:T(8,128)(2,1)} %copy-done, bf16[17,16,1024]{2,1,0:T(8,128)(2,1)} %copy-done.1, f32[2,16,8,8,128]{4,3,2,1,0:T(8,128)} %get-tuple-element.19.edge_ref, ...), custom_call_target="tpu_custom_call", output_to_operand_aliasing={{}: (4, {})} | custom-call | tf_op jit(solution)/shard_map/spread_edges/pallas_call | solution.py:319
  30.3 8.3 %all-to-all-start = ((bf16[32,8,8,1024]{3,2,1,0:T(8,128)(2,1)}), bf16[32,8,8,1024]{3,2,1,0:T(8,128)(2,1)}, u32[]{:S(2)}, u32[]{:S(2)}) async-start(bf16[32,8,8,1024]{3,2,1,0:T(8,128)(2,1)} %bitcast.29), calls=%async_computation | async-start | bytes 8388608 | tf_op jit(solution)/shard_map/all_to_all | solution.py:643
  38.6 0.9 copy.31.half_bias
  39.5 0.1 copy.30
  39.6 6.5 %copy.37 = bf16[256,8,1024]{2,0,1:T(8,128)(2,1)} copy(bf16[256,8,1024]{2,1,0:T(8,128)(2,1)} %param.10) | data formatting | bytes 8388608 | tf_op args[0]
  46.2 0.7 multiply_bitcast_fusion.w_in_t
  46.9 6.7 %gate.1 = (bf16[4,512,1024]{2,1,0:T(8,128)(2,1)}, bf16[4,512,1024]{2,1,0:T(8,128)(2,1)}) custom-call(bf16[8,256,1024]{2,1,0:T(8,128)(2,1)} %bitcast.27, bf16[512,256]{1,0:T(8,128)(2,1)} %multiply_bitcast_fusion.w_in_t, f32[512,1]{1,0:T(8,128)} %copy.31.half_bias), custom_call_target="tpu_custom_call" | custom-call | tf_op jit(solution)/shard_map/gate/pallas_call | solution.py:468
  53.6 0.7 broadcast_multiply_fusion.w_out
  54.4 21.3 %frac_sums.1 = f32[2,64,8,128]{3,2,1,0:T(8,128)} custom-call(s32[2,4,16]{2,1,0:T(4,128)} %bitcast.34, s32[4,16]{1,0:T(4,128)} %bitcast.40, s32[4,16]{1,0:T(4,128)} %bitcast.43, f32[2,4,16]{2,1,0:T(4,128)} %bitcast.37, bf16[17,16,1024]{2,1,0:T(8,128)(2,1)} %copy-done, bf16[8,256,1024]{2,1,0:T(8,128)(2,1)} %next_ref.1, bf16[8,256,1024]{2,1,0:T(8,128)(2,1)} %next_ref.1, ...), custom_call_target="tpu_custom_call" | custom-call | tf_op jit(solution)/shard_map/frac_sums/pallas_call | solution.py:427
  75.6 1.6 %reduce_sum.18 = f32[2,64]{1,0:T(2,128)S(1)} reduce(f32[2,64,8,128]{3,2,1,0:T(8,128)} %frac_sums.1, f32[]{:T(128)} %constant.15.clone.1), dimensions={2,3}, to_apply=%region_0.0 | reduce | flops 130944 | bytes 524804 | tf_op jit(solution)/shard_map/reduce_sum | solution.py:649
  77.7 0.8 pad.4.tail_ref
  78.5 12.8 %all-to-all-done.dy_ref = bf16[32,8,8,1024]{3,2,1,0:T(8,128)(2,1)} async-done(((bf16[32,8,8,1024]{3,2,1,0:T(8,128)(2,1)}), bf16[32,8,8,1024]{3,2,1,0:T(8,128)(2,1)}, u32[]{:S(2)}, u32[]{:S(2)}) %all-to-all-start) | async-done | bytes 4194336 | tf_op jit(solution)/shard_map/all_to_all | solution.py:643
  91.3 15.9 %mlp.1 = (bf16[8,256,1024]{2,1,0:T(8,128)(2,1)}, bf16[128,4,640]{2,1,0:T(4,128)(2,1)}) custom-call(bf16[8,256,1024]{2,1,0:T(8,128)(2,1)} %bitcast.28, bf16[32,8,8,1024]{3,2,1,0:T(8,128)(2,1)} %all-to-all-done.dy_ref, bf16[4,512,1024]{2,1,0:T(8,128)(2,1)} %get-tuple-element.21.act_ref, bf16[4,512,1024]{2,1,0:T(8,128)(2,1)} %get-tuple-element.22.slope_ref, ...), custom_call_target="tpu_custom_call" | custom-call | tf_op jit(solution)/shard_map/mlp/pallas_call | solution.py:558
  107.2 10.1 %all-to-all-start.1 = ((bf16[128,4,640]{2,1,0:T(4,128)(2,1)}), bf16[128,4,640]{2,1,0:T(4,128)(2,1)S(1)}, u32[]{:S(2)}, u32[]{:S(2)}) async-start(bf16[128,4,640]{2,1,0:T(4,128)(2,1)} %get-tuple-element.24), calls=%async_computation.1 | async-start | bytes 1310720 | tf_op jit(solution)/shard_map/all_to_all | solution.py:666
  117.3 6.5 %copy.35 = bf16[256,8,1024]{2,1,0:T(8,128)(2,1)} copy(bf16[256,8,1024]{2,0,1:T(8,128)(2,1)} %bitcast.30) | data formatting | bytes 8388608
  123.8 8.7 %all-to-all-done.1 = bf16[128,4,640]{2,1,0:T(4,128)(2,1)S(1)} async-done(((bf16[128,4,640]{2,1,0:T(4,128)(2,1)}), bf16[128,4,640]{2,1,0:T(4,128)(2,1)S(1)}, u32[]{:S(2)}, u32[]{:S(2)}) %all-to-all-start.1) | async-done | bytes 655392 | tf_op jit(solution)/shard_map/all_to_all | solution.py:666
  132.5 0.9 convert_reduce_fusion.got_ref
  133.4 1.4 %finish.1 = (f32[4,256]{1,0:T(4,128)}, f32[4,256]{1,0:T(4,128)}, f32[1,4]{1,0:T(1,128)}, f32[2,4,16]{2,1,0:T(4,128)}) custom-call(f32[4,640]{1,0:T(4,128)} %convert_reduce_fusion.got_ref), custom_call_target="tpu_custom_call" | custom-call | tf_op jit(solution)/shard_map/finish/pallas_call | solution.py:609
  (23 shorter events, 0.5 us)
Async XLA Ops:
  3.5 21.6 %collective-permute-start = (bf16[17,16,1024]{2,1,0:T(8,128)(2,1)}, bf16[17,16,1024]{2,1,0:T(8,128)(2,1)S(1)}, u32[]{:S(2)}, u32[]{:S(2)}) collective-permute-start(bf16[17,16,1024]{2,1,0:T(8,128)(2,1)} %get-tuple-element.17), channel_id=1, source_target_pairs={{0,32},{32,64},{64,96},{1,33},{33,65},{65,97},{2,34},{34,66},{66,9... | collective-permute-start | bytes 1671176 | tf_op jit(solution)/shard_map/ppermute | solution.py:52
  9.7 15.4 %collective-permute-start.1 = (bf16[17,16,1024]{2,1,0:T(8,128)(2,1)}, bf16[17,16,1024]{2,1,0:T(8,128)(2,1)S(1)}, u32[]{:S(2)}, u32[]{:S(2)}) collective-permute-start(bf16[17,16,1024]{2,1,0:T(8,128)(2,1)} %get-tuple-element.18), channel_id=1, source_target_pairs={{32,0},{64,32},{96,64},{33,1},{65,33},{97,65},{34,2},{66,34},{98,6... | collective-permute-start | bytes 1671176 | tf_op jit(solution)/shard_map/ppermute | solution.py:51
  25.1 0.8 copy-start
  25.1 1.0 copy-start.1
  30.3 8.3 %copy-start.4 = (f32[512]{0:T(512)S(1)}, f32[512]{0:T(512)}, u32[]{:S(2)}) copy-start(f32[512]{0:T(512)} %param.12) | copy-start | bytes 6148
  30.3 9.2 %copy-start.2 = (bf16[256,512]{1,0:T(8,128)(2,1)S(1)}, bf16[256,512]{1,0:T(8,128)(2,1)}, u32[]{:S(2)}) copy-start(bf16[256,512]{1,0:T(8,128)(2,1)} %w_in.1) | copy-start | bytes 786436
  30.3 61.0 %all-to-all-start = ((bf16[32,8,8,1024]{3,2,1,0:T(8,128)(2,1)}), bf16[32,8,8,1024]{3,2,1,0:T(8,128)(2,1)}, u32[]{:S(2)}, u32[]{:S(2)}) async-start(bf16[32,8,8,1024]{3,2,1,0:T(8,128)(2,1)} %bitcast.29), calls=%async_computation | async-start | bytes 8388608 | tf_op jit(solution)/shard_map/all_to_all | solution.py:643
  46.1 7.5 %copy-start.3 = (bf16[512,256]{1,0:T(8,128)(2,1)S(1)}, bf16[512,256]{1,0:T(8,128)(2,1)}, u32[]{:S(2)}) copy-start(bf16[512,256]{1,0:T(8,128)(2,1)} %param.13) | copy-start | bytes 786436
  107.2 25.3 %all-to-all-start.1 = ((bf16[128,4,640]{2,1,0:T(4,128)(2,1)}), bf16[128,4,640]{2,1,0:T(4,128)(2,1)S(1)}, u32[]{:S(2)}, u32[]{:S(2)}) async-start(bf16[128,4,640]{2,1,0:T(4,128)(2,1)} %get-tuple-element.24), calls=%async_computation.1 | async-start | bytes 1310720 | tf_op jit(solution)/shard_map/all_to_all | solution.py:666

commit v7 on v6

--- a/solution.py
+++ b/solution.py
@@ -186,9 +186,9 @@
 
 def spread_scratch():
     return [
-        pltpu.VMEM((8, LANES, 2 * LANES), BF16),
-        pltpu.VMEM((8, REACH * 8, LANES), BF16),
-        pltpu.VMEM((8, LANES, 3 * LANES), BF16),
+        pltpu.VMEM((16, LANES, 2 * LANES), BF16),
+        pltpu.VMEM((16, REACH * 8, LANES), BF16),
+        pltpu.VMEM((16, LANES, 3 * LANES), BF16),
     ]
 
 
@@ -218,10 +218,10 @@
 
     @pl.when(step < last)
     def _():
-        acc[pl.ds((2 * step + 2) * BH, 2 * BH)] = jnp.zeros((2 * BH,) + acc.shape[1:], F32)
+        acc[pl.ds((4 * step + 2) * BH, 4 * BH)] = jnp.zeros((4 * BH,) + acc.shape[1:], F32)
         jobs = []
-        for half in range(2):
-            row = 2 * step + half
+        for half in range(4):
+            row = 4 * step + half
             rows = cot_ref[:, half * BH : (half + 1) * BH].reshape(LANES, cot_ref.shape[2])
             for block in range(4):
                 jobs.append(
@@ -238,8 +238,8 @@
                 )
         spread_blocks(jobs, tap_scr, row_scr, z_scr, acc)
 
-    emit(acc, jnp.maximum(2 * step - 1, 0) * BH, out_ref.at[0])
-    emit(acc, 2 * step * BH, out_ref.at[1])
+    for slot in range(4):
+        emit(acc, jnp.maximum(4 * step - 3 + slot, 0) * BH, out_ref.at[slot])
 
     @pl.when(step == 0)
     def _():
@@ -247,13 +247,13 @@
 
     @pl.when(step == last)
     def _():
-        edge_ref[0] = acc[pl.ds(2 * last * BH, BH)]
+        edge_ref[0] = acc[pl.ds(4 * last * BH, BH)]
 
 
 def spread(places, cot):
     channels, band_rows, columns = cot.shape
     blocks = band_rows // BH
-    pairs = blocks // 2
+    quads = blocks // 4
     tiles = columns // LANES
     return pl.pallas_call(
         spread_body,
@@ -264,19 +264,19 @@
         ),
         grid_spec=pltpu.PrefetchScalarGridSpec(
             num_scalar_prefetch=4,
-            grid=(pairs + 1,),
+            grid=(quads + 1,),
             in_specs=[
                 pl.BlockSpec(
-                    (channels, 2 * BH, columns), lambda g, *a: (0, jnp.minimum(g, pairs - 1), 0)
+                    (channels, 4 * BH, columns), lambda g, *a: (0, jnp.minimum(g, quads - 1), 0)
                 )
             ],
             out_specs=[
                 pl.BlockSpec(
-                    (2, BH * channels, columns), lambda g, *a: (jnp.maximum(g - 1, 0), 0, 0)
+                    (4, BH * channels, columns), lambda g, *a: (jnp.maximum(g - 1, 0), 0, 0)
                 ),
                 pl.BlockSpec(
                     (1, BH, tiles, channels, LANES),
-                    lambda g, *a: (jnp.where(g == pairs, 1, 0), 0, 0, 0, 0),
+                    lambda g, *a: (jnp.where(g == quads, 1, 0), 0, 0, 0, 0),
                 ),
             ],
             scratch_shapes=spread_scratch()

time: 136 us -> 135 us (level)
  transfers between devices with their start and end apart: 4 -> 4, of which waited for: 2 -> 2; matrix products, arithmetic and copies ran while one was open for 14% -> 14% of each run, Pallas kernels for 31% -> 30%
where the time goes in v7:
time: 135 us; the launch traced here: 134 us
  Pallas kernels  65.3 us (48%)
  starting transfers between devices  26.7 us (20%)
  waiting for transfers between devices  21.3 us (16%)
  local copies, waits for them, and re-layouts  15.5 us (11%)
  other arithmetic  4.73 us (4%)
    pallas_call x1, Pallas kernels, frac_sums(): pl.pallas_call(frac_body, name='frac_sums', out_shape=jax.ShapeDtypeStruc...  21.3 us
    pallas_call x1, Pallas kernels, mlp(): pl.pallas_call(mlp_body, name='mlp', out_shape=(jax.ShapeDtypeStruct((row...  15.9 us
    unnamed x13, local copies, waits for them, and re-layouts  13.5 us
    pallas_call x1, Pallas kernels, spread(): pl.pallas_call(spread_body, name='spread', out_shape=(jax.ShapeDtypeStruc...  12.8 us
    all_to_all x1, waiting for transfers between devices, shards(): lax.all_to_all(dy_send, 'grp', split_axis=0, concat_axis=0, tiled=True)  12.6 us
    all_to_all x1, starting transfers between devices, shards(): lax.all_to_all(send, ('lat', 'grp'), split_axis=0, concat_axis=0, tiled=T...  10.1 us
    all_to_all x1, waiting for transfers between devices, shards(): lax.all_to_all(send, ('lat', 'grp'), split_axis=0, concat_axis=0, tiled=T...  8.72 us
    all_to_all x1, starting transfers between devices, shards(): lax.all_to_all(dy_send, 'grp', split_axis=0, concat_axis=0, tiled=True)  8.43 us
  transfers between devices with their start and end apart: 4, of which 2 were waited for; matrix products, arithmetic and copies ran while one was open for 14% of the time, Pallas kernels for 30%

profile of v7, /device:TPU:1, one launch (start us, length us, event | category | flops | bytes accessed | tf_op | source)
XLA Modules:
  0.0 134.3 jit_solution(9918785571412407761)
XLA Ops:
  0.6 2.9 %pack.1 = (bf16[17,16,1024]{2,1,0:T(8,128)(2,1)}, bf16[17,16,1024]{2,1,0:T(8,128)(2,1)}) custom-call(s32[2,4,16]{2,1,0:T(4,128)} %bitcast.32, s32[4,16]{1,0:T(4,128)} %bitcast.38, s32[4,16]{1,0:T(4,128)} %bitcast.41, f32[2,4,16]{2,1,0:T(4,128)} %bitcast.35, bf16[8,256,1024]{2,1,0:T(8,128)(2,1)} %cot_ref.3, bf16[8,256,1024]{2,1,0:T(8,128)(2,1)} %next_ref.1), custom_call_target="tpu_custom_call" | custom-call | tf_op jit(solution)/shard_map/pack/pallas_call | solution.py:146
  3.5 6.2 %collective-permute-start = (bf16[17,16,1024]{2,1,0:T(8,128)(2,1)}, bf16[17,16,1024]{2,1,0:T(8,128)(2,1)S(1)}, u32[]{:S(2)}, u32[]{:S(2)}) collective-permute-start(bf16[17,16,1024]{2,1,0:T(8,128)(2,1)} %get-tuple-element.17), channel_id=1, source_target_pairs={{0,32},{32,64},{64,96},{1,33},{33,65},{65,97},{2,34},{34,66},{66,9... | collective-permute-start | bytes 1671176 | tf_op jit(solution)/shard_map/ppermute | solution.py:52
  9.7 1.9 %collective-permute-start.1 = (bf16[17,16,1024]{2,1,0:T(8,128)(2,1)}, bf16[17,16,1024]{2,1,0:T(8,128)(2,1)S(1)}, u32[]{:S(2)}, u32[]{:S(2)}) collective-permute-start(bf16[17,16,1024]{2,1,0:T(8,128)(2,1)} %get-tuple-element.18), channel_id=1, source_target_pairs={{32,0},{64,32},{96,64},{33,1},{65,33},{97,65},{34,2},{66,34},{98,6... | collective-permute-start | bytes 1671176 | tf_op jit(solution)/shard_map/ppermute | solution.py:51
  11.7 12.8 %spread.1 = (bf16[16,128,1024]{2,1,0:T(8,128)(2,1)}, f32[2,16,8,8,128]{4,3,2,1,0:T(8,128)}) custom-call(s32[2,4,16]{2,1,0:T(4,128)} %bitcast.33, s32[4,16]{1,0:T(4,128)} %bitcast.39, s32[4,16]{1,0:T(4,128)} %bitcast.42, f32[2,4,16]{2,1,0:T(4,128)} %bitcast.36, bf16[8,256,1024]{2,1,0:T(8,128)(2,1)} %cot_ref.3), custom_call_target="tpu_custom_call" | custom-call | tf_op jit(solution)/shard_map/spread/pallas_call | solution.py:258
  24.5 0.7 maximum_convert_fusion.meta
  25.3 0.2 copy-done.1
  25.5 4.2 %spread_edges.1 = bf16[16,128,1024]{2,1,0:T(8,128)(2,1)} custom-call(f32[2,384]{1,0:T(2,128)} %maximum_convert_fusion.meta, bf16[17,16,1024]{2,1,0:T(8,128)(2,1)} %copy-done, bf16[17,16,1024]{2,1,0:T(8,128)(2,1)} %copy-done.1, f32[2,16,8,8,128]{4,3,2,1,0:T(8,128)} %get-tuple-element.19.edge_ref, ...), custom_call_target="tpu_custom_call", output_to_operand_aliasing={{}: (4, {})} | custom-call | tf_op jit(solution)/shard_map/spread_edges/pallas_call | solution.py:319
  29.7 8.4 %all-to-all-start = ((bf16[32,8,8,1024]{3,2,1,0:T(8,128)(2,1)}), bf16[32,8,8,1024]{3,2,1,0:T(8,128)(2,1)}, u32[]{:S(2)}, u32[]{:S(2)}) async-start(bf16[32,8,8,1024]{3,2,1,0:T(8,128)(2,1)} %bitcast.29), calls=%async_computation | async-start | bytes 8388608 | tf_op jit(solution)/shard_map/all_to_all | solution.py:643
  38.2 0.9 copy.31.half_bias
  39.0 0.1 copy.30
  39.2 6.5 %copy.37 = bf16[256,8,1024]{2,0,1:T(8,128)(2,1)} copy(bf16[256,8,1024]{2,1,0:T(8,128)(2,1)} %param.10) | data formatting | bytes 8388608 | tf_op args[0]
  45.7 0.7 multiply_bitcast_fusion.w_in_t
  46.4 6.7 %gate.1 = (bf16[4,512,1024]{2,1,0:T(8,128)(2,1)}, bf16[4,512,1024]{2,1,0:T(8,128)(2,1)}) custom-call(bf16[8,256,1024]{2,1,0:T(8,128)(2,1)} %bitcast.27, bf16[512,256]{1,0:T(8,128)(2,1)} %multiply_bitcast_fusion.w_in_t, f32[512,1]{1,0:T(8,128)} %copy.31.half_bias), custom_call_target="tpu_custom_call" | custom-call | tf_op jit(solution)/shard_map/gate/pallas_call | solution.py:468
  53.2 0.7 broadcast_multiply_fusion.w_out
  53.9 21.3 %frac_sums.1 = f32[2,64,8,128]{3,2,1,0:T(8,128)} custom-call(s32[2,4,16]{2,1,0:T(4,128)} %bitcast.34, s32[4,16]{1,0:T(4,128)} %bitcast.40, s32[4,16]{1,0:T(4,128)} %bitcast.43, f32[2,4,16]{2,1,0:T(4,128)} %bitcast.37, bf16[17,16,1024]{2,1,0:T(8,128)(2,1)} %copy-done, bf16[8,256,1024]{2,1,0:T(8,128)(2,1)} %next_ref.1, bf16[8,256,1024]{2,1,0:T(8,128)(2,1)} %next_ref.1, ...), custom_call_target="tpu_custom_call" | custom-call | tf_op jit(solution)/shard_map/frac_sums/pallas_call | solution.py:427
  75.2 1.6 %reduce_sum.18 = f32[2,64]{1,0:T(2,128)S(1)} reduce(f32[2,64,8,128]{3,2,1,0:T(8,128)} %frac_sums.1, f32[]{:T(128)} %constant.15.clone.1), dimensions={2,3}, to_apply=%region_0.0 | reduce | flops 130944 | bytes 524804 | tf_op jit(solution)/shard_map/reduce_sum | solution.py:649
  77.2 0.8 pad.4.tail_ref
  78.0 12.6 %all-to-all-done.dy_ref = bf16[32,8,8,1024]{3,2,1,0:T(8,128)(2,1)} async-done(((bf16[32,8,8,1024]{3,2,1,0:T(8,128)(2,1)}), bf16[32,8,8,1024]{3,2,1,0:T(8,128)(2,1)}, u32[]{:S(2)}, u32[]{:S(2)}) %all-to-all-start) | async-done | bytes 4194336 | tf_op jit(solution)/shard_map/all_to_all | solution.py:643
  90.6 15.9 %mlp.1 = (bf16[8,256,1024]{2,1,0:T(8,128)(2,1)}, bf16[128,4,640]{2,1,0:T(4,128)(2,1)}) custom-call(bf16[8,256,1024]{2,1,0:T(8,128)(2,1)} %bitcast.28, bf16[32,8,8,1024]{3,2,1,0:T(8,128)(2,1)} %all-to-all-done.dy_ref, bf16[4,512,1024]{2,1,0:T(8,128)(2,1)} %get-tuple-element.21.act_ref, bf16[4,512,1024]{2,1,0:T(8,128)(2,1)} %get-tuple-element.22.slope_ref, ...), custom_call_target="tpu_custom_call" | custom-call | tf_op jit(solution)/shard_map/mlp/pallas_call | solution.py:558
  106.6 10.1 %all-to-all-start.1 = ((bf16[128,4,640]{2,1,0:T(4,128)(2,1)}), bf16[128,4,640]{2,1,0:T(4,128)(2,1)S(1)}, u32[]{:S(2)}, u32[]{:S(2)}) async-start(bf16[128,4,640]{2,1,0:T(4,128)(2,1)} %get-tuple-element.24), calls=%async_computation.1 | async-start | bytes 1310720 | tf_op jit(solution)/shard_map/all_to_all | solution.py:666
  116.7 6.5 %copy.35 = bf16[256,8,1024]{2,1,0:T(8,128)(2,1)} copy(bf16[256,8,1024]{2,0,1:T(8,128)(2,1)} %bitcast.30) | data formatting | bytes 8388608
  123.2 8.7 %all-to-all-done.1 = bf16[128,4,640]{2,1,0:T(4,128)(2,1)S(1)} async-done(((bf16[128,4,640]{2,1,0:T(4,128)(2,1)}), bf16[128,4,640]{2,1,0:T(4,128)(2,1)S(1)}, u32[]{:S(2)}, u32[]{:S(2)}) %all-to-all-start.1) | async-done | bytes 655392 | tf_op jit(solution)/shard_map/all_to_all | solution.py:666
  131.9 0.9 convert_reduce_fusion.got_ref
  132.8 1.4 %finish.1 = (f32[4,256]{1,0:T(4,128)}, f32[4,256]{1,0:T(4,128)}, f32[1,4]{1,0:T(1,128)}, f32[2,4,16]{2,1,0:T(4,128)}) custom-call(f32[4,640]{1,0:T(4,128)} %convert_reduce_fusion.got_ref), custom_call_target="tpu_custom_call" | custom-call | tf_op jit(solution)/shard_map/finish/pallas_call | solution.py:609
  (23 shorter events, 0.5 us)
Async XLA Ops:
  3.5 20.9 %collective-permute-start = (bf16[17,16,1024]{2,1,0:T(8,128)(2,1)}, bf16[17,16,1024]{2,1,0:T(8,128)(2,1)S(1)}, u32[]{:S(2)}, u32[]{:S(2)}) collective-permute-start(bf16[17,16,1024]{2,1,0:T(8,128)(2,1)} %get-tuple-element.17), channel_id=1, source_target_pairs={{0,32},{32,64},{64,96},{1,33},{33,65},{65,97},{2,34},{34,66},{66,9... | collective-permute-start | bytes 1671176 | tf_op jit(solution)/shard_map/ppermute | solution.py:52
  9.7 14.7 %collective-permute-start.1 = (bf16[17,16,1024]{2,1,0:T(8,128)(2,1)}, bf16[17,16,1024]{2,1,0:T(8,128)(2,1)S(1)}, u32[]{:S(2)}, u32[]{:S(2)}) collective-permute-start(bf16[17,16,1024]{2,1,0:T(8,128)(2,1)} %get-tuple-element.18), channel_id=1, source_target_pairs={{32,0},{64,32},{96,64},{33,1},{65,33},{97,65},{34,2},{66,34},{98,6... | collective-permute-start | bytes 1671176 | tf_op jit(solution)/shard_map/ppermute | solution.py:51
  24.5 0.8 copy-start
  24.5 1.0 copy-start.1
  29.7 8.4 %copy-start.4 = (f32[512]{0:T(512)S(1)}, f32[512]{0:T(512)}, u32[]{:S(2)}) copy-start(f32[512]{0:T(512)} %param.12) | copy-start | bytes 6148
  29.7 9.3 %copy-start.2 = (bf16[256,512]{1,0:T(8,128)(2,1)S(1)}, bf16[256,512]{1,0:T(8,128)(2,1)}, u32[]{:S(2)}) copy-start(bf16[256,512]{1,0:T(8,128)(2,1)} %w_in.1) | copy-start | bytes 786436
  29.7 60.9 %all-to-all-start = ((bf16[32,8,8,1024]{3,2,1,0:T(8,128)(2,1)}), bf16[32,8,8,1024]{3,2,1,0:T(8,128)(2,1)}, u32[]{:S(2)}, u32[]{:S(2)}) async-start(bf16[32,8,8,1024]{3,2,1,0:T(8,128)(2,1)} %bitcast.29), calls=%async_computation | async-start | bytes 8388608 | tf_op jit(solution)/shard_map/all_to_all | solution.py:643
  45.7 7.5 %copy-start.3 = (bf16[512,256]{1,0:T(8,128)(2,1)S(1)}, bf16[512,256]{1,0:T(8,128)(2,1)}, u32[]{:S(2)}) copy-start(bf16[512,256]{1,0:T(8,128)(2,1)} %param.13) | copy-start | bytes 786436
  106.6 25.3 %all-to-all-start.1 = ((bf16[128,4,640]{2,1,0:T(4,128)(2,1)}), bf16[128,4,640]{2,1,0:T(4,128)(2,1)S(1)}, u32[]{:S(2)}, u32[]{:S(2)}) async-start(bf16[128,4,640]{2,1,0:T(4,128)(2,1)} %get-tuple-element.24), calls=%async_computation.1 | async-start | bytes 1310720 | tf_op jit(solution)/shard_map/all_to_all | solution.py:666
